TPU v7x, 32 devices: a whole 2x2x4 slice. The times are simulated.
32 devices in a mesh: row: 4 (over y, core), col: 8 (over z, x).
Axes of the slice: x: 2, y: 2, z: 4, core: 2. Of those that a mesh axis runs over, the one named last changes fastest.
Arguments:
- embeddings: float32 [32768, 1024], P(('row', 'col')), may hold values from -6 to 6
- neighbour_ids: int32 [64, 12], P(('row', 'col')), may hold values from 0 to 63, as said below
- start_vectors: float32 [32768, 64], P(('row', 'col')), may hold values from -15 to 15
Outputs:
- spectral_vectors: float32 [32768, 64], P(('row', 'col'))
Inputs may be any that keep to these rules, and one draw needn't show every extreme that they name: `neighbour_ids`: slot 0 of block b is b itself. The other slots of block b name distinct blocks other than b held by devices of the same row index whose col index differs from that of b's device by at most 2 cyclically, followed by padding slots that repeat b. Block b sits on device b // 2, with device index row * 8 + col.
All inputs are finite; a program needn't handle non-finite values.
Results may differ from a plain program's by a relative error of at most 0.005.
Values may be sent and summed in bfloat16 or wider, within the bound.
No kernel may reach another device: no remote copies, remote signals or barrier semaphores. Data moves between devices by JAX's collectives and lax.ppermute only.
A program may use at most 128 MiB of HBM per device.

v0:
```python
import math

import jax
import jax.numpy as jnp
from jax import lax
from jax.sharding import PartitionSpec as P

D = 1024
BS = 512
SLOTS = 12
REACH = 2
ITERS = 3
BLK_DEV = 2


SHARP = 8.0
EPSILON = 1e-06


def passed_along(shard, axis, by):
    count = lax.axis_size(axis)
    return lax.ppermute(shard, axis, [(i, (i + by) % count) for i in range(count)])


def unit_rows(points):
    rms_inverse = lax.rsqrt(jnp.mean(points * points, axis=-1, keepdims=True) + EPSILON)
    return (points * rms_inverse).astype(jnp.bfloat16)


def band_index(neighbour_ids, col_count, col_index):
    holder = neighbour_ids // BLK_DEV
    offset = (holder % col_count - col_index + col_count + REACH) % col_count
    return offset * BLK_DEV + neighbour_ids % BLK_DEV


def assemble(pieces):
    return jnp.concatenate([pieces[offset] for offset in range(-REACH, REACH + 1)], axis=0)


def point_band(normed):
    pieces = {0: normed}
    for offset in [shifted for shifted in range(-REACH, REACH + 1) if shifted != 0]:
        pieces[offset] = passed_along(normed, "col", -offset)
    return assemble(pieces)


def vector_band(scaled):
    pieces = {0: scaled}
    for offset in [shifted for shifted in range(-REACH, REACH + 1) if shifted != 0]:
        pieces[offset] = passed_along(scaled, "col", -offset)
    return assemble(pieces)


def orthonormal(image_rows, total_rows):
    gram_sum = lax.dot_general(
        image_rows,
        image_rows,
        (((0,), (0,)), ((), ())),
        precision=lax.Precision.HIGHEST,
        preferred_element_type=jnp.float32,
    )
    gram_sum = lax.psum(gram_sum, ("row", "col"))
    factor = jnp.linalg.cholesky(gram_sum)
    solved = lax.linalg.triangular_solve(
        factor, image_rows, left_side=False, lower=True, transpose_a=True
    )
    return solved * math.sqrt(total_rows)


def on_device(embeddings, neighbour_ids, start_vectors):
    col_count = lax.axis_size("col")
    col_index = lax.axis_index("col")
    device = lax.axis_index("row") * col_count + col_index
    total_rows = embeddings.shape[0] * lax.axis_size("row") * col_count
    normed = unit_rows(embeddings)
    point_rows = point_band(normed)
    own_ids = device * BLK_DEV + jnp.arange(BLK_DEV, dtype=jnp.int32)
    slot_ids = jnp.arange(SLOTS, dtype=jnp.int32)
    live_mask = ((slot_ids[None, :] == 0) | (neighbour_ids != own_ids[:, None])).astype(jnp.float32)
    position = band_index(neighbour_ids, col_count, col_index)
    candidates = (2 * REACH + 1) * BLK_DEV
    own_blocks = normed.reshape(BLK_DEV, BS, D)
    tile_list = []
    degree_list = []
    chosen = jnp.sum(
        (position[:, :, None] == jnp.arange(candidates, dtype=jnp.int32)[None, None, :]).astype(
            jnp.float32
        )
        * live_mask[:, :, None],
        axis=1,
    )
    for member in range(BLK_DEV):
        cosine = (
            lax.dot_general(
                own_blocks[member],
                point_rows,
                (((1,), (1,)), ((), ())),
                preferred_element_type=jnp.float32,
            )
            / D
        )
        affinity = (
            jnp.exp(SHARP * (cosine - 1.0)).reshape(BS, candidates, BS)
            * chosen[member][None, :, None]
        )
        degree_list.append(jnp.sum(affinity, axis=(1, 2)))
        tile_list.append(affinity.reshape(BS, candidates * BS).astype(jnp.bfloat16))
    inv_root = lax.rsqrt(jnp.stack(degree_list))
    vectors = start_vectors
    for iteration in range(ITERS):
        scaled = (vectors * inv_root.reshape(-1, 1)).astype(jnp.bfloat16)
        spread = vector_band(scaled)
        image_list = []
        for member in range(BLK_DEV):
            partial_rows = jnp.dot(tile_list[member], spread, preferred_element_type=jnp.float32)
            image_list.append(partial_rows * inv_root[member][:, None])
        image_rows = jnp.concatenate(image_list, axis=0)
        vectors = orthonormal(image_rows, total_rows)
    return vectors


def solution(mesh):
    in_specs = (P(("row", "col"), None), P(("row", "col"), None), P(("row", "col"), None))
    out_specs = P(("row", "col"), None)
    return jax.shard_map(
        on_device, mesh=mesh, in_specs=in_specs, out_specs=out_specs, check_vma=False
    )
```

profile of v0, /device:TPU:0, one launch (start us, length us, event | category | flops | bytes accessed | tf_op | source)
XLA Modules:
  0.0 388.7 jit_solution(13238385011617048183)
XLA Ops:
  0.0 2.7 multiply_reduce_fusion
  2.7 0.7 copy-done.3
  3.5 1.6 multiply_convert_fusion
  5.1 3.1 collective-permute-start
  8.1 1.5 collective-permute-start.1
  9.6 3.2 collective-permute-start.2
  13.7 43.3 %collective-permute-done = bf16[1024,1024]{1,0:T(8,128)(2,1)} collective-permute-done((bf16[1024,1024]{1,0:T(8,128)(2,1)}, bf16[1024,1024]{1,0:T(8,128)(2,1)}, u32[]{:S(2)}, u32[]{:S(2)}) %collective-permute-start) | collective-permute-done | bytes 2097184 | tf_op jit(solution)/shard_map/ppermute | solution.py:22
  57.0 3.1 constant_dynamic-update-slice_fusion.4
  60.1 43.0 %collective-permute-done.1 = bf16[1024,1024]{1,0:T(8,128)(2,1)} collective-permute-done((bf16[1024,1024]{1,0:T(8,128)(2,1)}, bf16[1024,1024]{1,0:T(8,128)(2,1)}, u32[]{:S(2)}, u32[]{:S(2)}) %collective-permute-start.1) | collective-permute-done | bytes 2097184 | tf_op jit(solution)/shard_map/ppermute | solution.py:22
  103.1 3.1 constant_dynamic-update-slice_fusion.3
  106.2 1.6 constant_dynamic-update-slice_fusion.2
  107.8 3.2 constant_dynamic-update-slice_fusion.1
  111.0 34.9 %collective-permute-done.3 = bf16[1024,1024]{1,0:T(8,128)(2,1)S(1)} collective-permute-done((bf16[1024,1024]{1,0:T(8,128)(2,1)}, bf16[1024,1024]{1,0:T(8,128)(2,1)S(1)}, u32[]{:S(2)}, u32[]{:S(2)}) %collective-permute-start.3) | collective-permute-done | bytes 2097184 | tf_op jit(solution)/shard_map/ppermute | solution.py:22
  145.9 1.5 constant_dynamic-update-slice_fusion
  147.4 10.0 %fusion.45 = (f32[512]{0:T(512)S(1)}, bf16[512,5120]{1,0:T(8,128)(2,1)S(1)}) fusion(f32[5120]{0:T(1024)S(1)} %mul.152, bf16[5120,1024]{1,0:T(8,128)(2,1)} %constant_dynamic-update-slice_fusion, bf16[1024,1024]{1,0:T(8,128)(2,1)} %multiply_convert_fusion), kind=kOutput, calls=%fused_computation.114 | convolution fusion | flops 5384437248 | bytes 16799744 | tf_op jit(solution)/shard_map/dot_general | solution.py:94
  157.4 11.9 %fusion.44 = (f32[512]{0:T(512)S(1)}, bf16[512,5120]{1,0:T(8,128)(2,1)S(1)}) fusion(f32[5120]{0:T(1024)S(1)} %mul.158, bf16[5120,1024]{1,0:T(8,128)(2,1)} %constant_dynamic-update-slice_fusion, bf16[1024,1024]{1,0:T(8,128)(2,1)} %multiply_convert_fusion), kind=kOutput, calls=%fused_computation.113 | convolution fusion | flops 5384437248 | bytes 16799744 | tf_op jit(solution)/shard_map/dot_general | solution.py:94
  170.1 1.5 collective-permute-start.5
  171.6 3.3 collective-permute-start.6
  174.8 10.5 %collective-permute-start.7 = (bf16[1024,64]{0,1:T(8,128)(2,1)S(1)}, bf16[1024,64]{0,1:T(8,128)(2,1)S(1)}, u32[]{:S(2)}, u32[]{:S(2)}) collective-permute-start(bf16[1024,64]{0,1:T(8,128)(2,1)S(1)} %multiply_convert_fusion.1), channel_id=1, source_target_pairs={{0,6},{1,7},{2,0},{3,1},{4,2},{5,3},{6,4},{7,5},{8,14},{9,15},{10,... | collective-permute-start | bytes 393224 | tf_op jit(solution)/shard_map/ppermute | solution.py:22
  185.4 0.9 collective-permute-done.6
  186.3 2.9 collective-permute-done.7
  189.1 1.7 convolution_multiply_fusion.5
  190.8 1.7 convolution_multiply_fusion.4
  192.9 39.6 %psum.21 = f32[64,64]{0,1:T(8,128)S(1)} all-reduce(f32[64,64]{0,1:T(8,128)S(1)} %fusion.9), channel_id=1, replica_groups=mesh['row'=4,'col'=8] {'row','col'}, use_global_device_ids=true, to_apply=%region_4.5 | all-reduce | flops 4096 | bytes 32768 | tf_op jit(solution)/shard_map/psum | solution.py:62
  232.6 5.8 %cholesky.59 = f32[64,64]{1,0:T(8,128)S(1)} custom-call(f32[64,64]{1,0:T(8,128)S(1)} %fusion.18), custom_call_target="Cholesky" | custom-call | tf_op jit(solution)/shard_map/jit(cholesky)/cholesky | solution.py:63
  239.8 4.9 %custom-call.7 = f32[1,64,64]{1,2,0:T(8,128)S(1)} custom-call(f32[1,64,64]{2,1,0:T(8,128)S(1)} %fusion.10), custom_call_target="InvertDiagBlocksLowerTriangular" | custom-call | tf_op jit(solution)/shard_map/triangular_solve/custom-call.0 | solution.py:64
  245.1 1.2 collective-permute-start.8
  246.3 2.3 collective-permute-start.9
  248.5 2.5 collective-permute-start.10
  251.0 0.9 collective-permute-start.11
  251.9 0.9 collective-permute-done.8
  252.9 4.5 %collective-permute-done.9 = bf16[1024,64]{0,1:T(8,128)(2,1)S(1)} collective-permute-done((bf16[1024,64]{0,1:T(8,128)(2,1)S(1)}, bf16[1024,64]{0,1:T(8,128)(2,1)S(1)}, u32[]{:S(2)}, u32[]{:S(2)}) %collective-permute-start.9) | collective-permute-done | bytes 131104 | tf_op jit(solution)/shard_map/ppermute | solution.py:22
  257.5 4.2 %convolution_multiply_fusion.3 = f32[512,64]{0,1:T(8,128)S(1)} fusion(bf16[5120,64]{0,1:T(8,128)(2,1)S(1)} %constant_dynamic-update-slice_fusion.10, f32[512]{0:T(512)S(1)} %bitcast.68, bf16[512,5120]{1,0:T(8,128)(2,1)} %copy-done), kind=kOutput, calls=%fused_computation.15 | convolution fusion | flops 335577088 | bytes 6031360 | tf_op jit(solution)/shard_map/dot_general | solution.py:115
  261.7 1.7 convolution_multiply_fusion.2
  263.8 38.8 %psum.22 = f32[64,64]{0,1:T(8,128)S(1)} all-reduce(f32[64,64]{0,1:T(8,128)S(1)} %fusion.8), channel_id=1, replica_groups=mesh['row'=4,'col'=8] {'row','col'}, use_global_device_ids=true, to_apply=%region_7.10 | all-reduce | flops 4096 | bytes 32768 | tf_op jit(solution)/shard_map/psum | solution.py:62
  302.7 5.8 %cholesky.70 = f32[64,64]{1,0:T(8,128)S(1)} custom-call(f32[64,64]{1,0:T(8,128)S(1)} %fusion.16), custom_call_target="Cholesky" | custom-call | tf_op jit(solution)/shard_map/jit(cholesky)/cholesky | solution.py:63
  309.9 4.9 %custom-call.8 = f32[1,64,64]{1,2,0:T(8,128)S(1)} custom-call(f32[1,64,64]{2,1,0:T(8,128)S(1)} %fusion.11), custom_call_target="InvertDiagBlocksLowerTriangular" | custom-call | tf_op jit(solution)/shard_map/triangular_solve/custom-call.0 | solution.py:64
  315.2 1.6 collective-permute-start.12
  316.8 2.3 collective-permute-start.13
  319.1 2.5 collective-permute-start.14
  322.0 0.9 collective-permute-done.12
  323.0 4.5 %collective-permute-done.13 = bf16[1024,64]{0,1:T(8,128)(2,1)S(1)} collective-permute-done((bf16[1024,64]{0,1:T(8,128)(2,1)S(1)}, bf16[1024,64]{0,1:T(8,128)(2,1)S(1)}, u32[]{:S(2)}, u32[]{:S(2)}) %collective-permute-start.13) | collective-permute-done | bytes 131104 | tf_op jit(solution)/shard_map/ppermute | solution.py:22
  327.6 4.2 %convolution_multiply_fusion.1 = f32[512,64]{0,1:T(8,128)S(1)} fusion(bf16[5120,64]{0,1:T(8,128)(2,1)S(1)} %constant_dynamic-update-slice_fusion.15, f32[512]{0:T(512)S(1)} %bitcast.69, bf16[512,5120]{1,0:T(8,128)(2,1)} %copy-done), kind=kOutput, calls=%fused_computation.13 | convolution fusion | flops 335577088 | bytes 6031360 | tf_op jit(solution)/shard_map/dot_general | solution.py:115
  331.8 4.2 %convolution_multiply_fusion = f32[512,64]{0,1:T(8,128)S(1)} fusion(bf16[5120,64]{0,1:T(8,128)(2,1)S(1)} %constant_dynamic-update-slice_fusion.15, f32[512]{0:T(512)S(1)} %bitcast.66, bf16[512,5120]{1,0:T(8,128)(2,1)} %copy-done.1), kind=kOutput, calls=%fused_computation.12 | convolution fusion | flops 335577088 | bytes 6031360 | tf_op jit(solution)/shard_map/dot_general | solution.py:115
  336.3 39.1 %psum.23 = f32[64,64]{0,1:T(8,128)S(1)} all-reduce(f32[64,64]{0,1:T(8,128)S(1)} %fusion.7), channel_id=1, replica_groups=mesh['row'=4,'col'=8] {'row','col'}, use_global_device_ids=true, to_apply=%region_8.11 | all-reduce | flops 4096 | bytes 32768 | tf_op jit(solution)/shard_map/psum | solution.py:62
  375.5 5.8 %cholesky.81 = f32[64,64]{1,0:T(8,128)S(1)} custom-call(f32[64,64]{1,0:T(8,128)S(1)} %fusion.14), custom_call_target="Cholesky" | custom-call | tf_op jit(solution)/shard_map/jit(cholesky)/cholesky | solution.py:63
  382.7 4.9 %custom-call.9 = f32[1,64,64]{1,2,0:T(8,128)S(1)} custom-call(f32[1,64,64]{2,1,0:T(8,128)S(1)} %fusion.12), custom_call_target="InvertDiagBlocksLowerTriangular" | custom-call | tf_op jit(solution)/shard_map/triangular_solve/custom-call.0 | solution.py:64
  387.6 1.1 fusion
  (74 shorter events, 8.4 us)
Async XLA Ops:
  0.0 3.4 copy-start.3
  0.0 13.1 %copy-start.6 = (s32[2,12]{1,0:T(2,128)S(1)}, s32[2,12]{1,0:T(2,128)}, u32[]{:S(2)}) copy-start(s32[2,12]{1,0:T(2,128)} %param.7) | copy-start | bytes 292
  5.1 51.9 %collective-permute-start = (bf16[1024,1024]{1,0:T(8,128)(2,1)}, bf16[1024,1024]{1,0:T(8,128)(2,1)}, u32[]{:S(2)}, u32[]{:S(2)}) collective-permute-start(bf16[1024,1024]{1,0:T(8,128)(2,1)} %multiply_convert_fusion), channel_id=1, source_target_pairs={{0,2},{1,3},{2,4},{3,5},{4,6},{5,7},{6,0},{7,1},{8,10},{9,11},{10,... | collective-permute-start | bytes 6291464 | tf_op jit(solution)/shard_map/ppermute | solution.py:22
  8.1 94.9 %collective-permute-start.1 = (bf16[1024,1024]{1,0:T(8,128)(2,1)}, bf16[1024,1024]{1,0:T(8,128)(2,1)}, u32[]{:S(2)}, u32[]{:S(2)}) collective-permute-start(bf16[1024,1024]{1,0:T(8,128)(2,1)} %multiply_convert_fusion), channel_id=1, source_target_pairs={{0,1},{1,2},{2,3},{3,4},{4,5},{5,6},{6,7},{7,0},{8,9},{9,10},{10,1... | collective-permute-start | bytes 6291464 | tf_op jit(solution)/shard_map/ppermute | solution.py:22
  9.6 98.2 %collective-permute-start.2 = (bf16[1024,1024]{1,0:T(8,128)(2,1)}, bf16[1024,1024]{1,0:T(8,128)(2,1)}, u32[]{:S(2)}, u32[]{:S(2)}) collective-permute-start(bf16[1024,1024]{1,0:T(8,128)(2,1)} %multiply_convert_fusion), channel_id=1, source_target_pairs={{0,7},{1,0},{2,1},{3,2},{4,3},{5,4},{6,5},{7,6},{8,15},{9,8},{10,9... | collective-permute-start | bytes 6291464 | tf_op jit(solution)/shard_map/ppermute | solution.py:22
  12.9 133.0 %collective-permute-start.3 = (bf16[1024,1024]{1,0:T(8,128)(2,1)}, bf16[1024,1024]{1,0:T(8,128)(2,1)S(1)}, u32[]{:S(2)}, u32[]{:S(2)}) collective-permute-start(bf16[1024,1024]{1,0:T(8,128)(2,1)} %multiply_convert_fusion), channel_id=1, source_target_pairs={{0,6},{1,7},{2,0},{3,1},{4,2},{5,3},{6,4},{7,5},{8,14},{9,15},{10,... | collective-permute-start | bytes 6291464 | tf_op jit(solution)/shard_map/ppermute | solution.py:22
  13.7 92.5 %copy-start.4 = (f32[1024,1024]{1,0:T(8,128)S(1)}, f32[1024,1024]{1,0:T(8,128)}, u32[]{:S(2)}) copy-start(f32[1024,1024]{1,0:T(8,128)} %param.6) | copy-start | bytes 12582916
  157.4 31.7 %copy-start = (bf16[512,5120]{1,0:T(8,128)(2,1)}, bf16[512,5120]{1,0:T(8,128)(2,1)S(1)}, u32[]{:S(2)}) copy-start(bf16[512,5120]{1,0:T(8,128)(2,1)S(1)} %get-tuple-element.16) | copy-start | bytes 15728644
  157.4 12.0 %copy-start.5 = (f32[1024,64]{0,1:T(8,128)S(1)}, f32[1024,64]{0,1:T(8,128)}, u32[]{:S(2)}) copy-start(f32[1024,64]{0,1:T(8,128)} %param.8) | copy-start | bytes 786436
  169.4 23.2 %copy-start.1 = (bf16[512,5120]{1,0:T(8,128)(2,1)}, bf16[512,5120]{1,0:T(8,128)(2,1)S(1)}, u32[]{:S(2)}) copy-start(bf16[512,5120]{1,0:T(8,128)(2,1)S(1)} %get-tuple-element.14) | copy-start | bytes 15728644
  169.4 15.8 %collective-permute-start.4 = (bf16[1024,64]{0,1:T(8,128)(2,1)S(1)}, bf16[1024,64]{0,1:T(8,128)(2,1)S(1)}, u32[]{:S(2)}, u32[]{:S(2)}) collective-permute-start(bf16[1024,64]{0,1:T(8,128)(2,1)S(1)} %multiply_convert_fusion.1), channel_id=1, source_target_pairs={{0,2},{1,3},{2,4},{3,5},{4,6},{5,7},{6,0},{7,1},{8,10},{9,11},{10,... | collective-permute-start | bytes 393224 | tf_op jit(solution)/shard_map/ppermute | solution.py:22
  170.1 15.2 %collective-permute-start.5 = (bf16[1024,64]{0,1:T(8,128)(2,1)S(1)}, bf16[1024,64]{0,1:T(8,128)(2,1)S(1)}, u32[]{:S(2)}, u32[]{:S(2)}) collective-permute-start(bf16[1024,64]{0,1:T(8,128)(2,1)S(1)} %multiply_convert_fusion.1), channel_id=1, source_target_pairs={{0,1},{1,2},{2,3},{3,4},{4,5},{5,6},{6,7},{7,0},{8,9},{9,10},{10,1... | collective-permute-start | bytes 393224 | tf_op jit(solution)/shard_map/ppermute | solution.py:22
  171.6 14.7 %collective-permute-start.6 = (bf16[1024,64]{0,1:T(8,128)(2,1)S(1)}, bf16[1024,64]{0,1:T(8,128)(2,1)S(1)}, u32[]{:S(2)}, u32[]{:S(2)}) collective-permute-start(bf16[1024,64]{0,1:T(8,128)(2,1)S(1)} %multiply_convert_fusion.1), channel_id=1, source_target_pairs={{0,7},{1,0},{2,1},{3,2},{4,3},{5,4},{6,5},{7,6},{8,15},{9,8},{10,9... | collective-permute-start | bytes 393224 | tf_op jit(solution)/shard_map/ppermute | solution.py:22
  174.8 14.3 %collective-permute-start.7 = (bf16[1024,64]{0,1:T(8,128)(2,1)S(1)}, bf16[1024,64]{0,1:T(8,128)(2,1)S(1)}, u32[]{:S(2)}, u32[]{:S(2)}) collective-permute-start(bf16[1024,64]{0,1:T(8,128)(2,1)S(1)} %multiply_convert_fusion.1), channel_id=1, source_target_pairs={{0,6},{1,7},{2,0},{3,1},{4,2},{5,3},{6,4},{7,5},{8,14},{9,15},{10,... | collective-permute-start | bytes 393224 | tf_op jit(solution)/shard_map/ppermute | solution.py:22
  244.7 17.0 %copy-start.2 = (bf16[512,5120]{1,0:T(8,128)(2,1)S(1)}, bf16[512,5120]{1,0:T(8,128)(2,1)}, u32[]{:S(2)}) copy-start(bf16[512,5120]{1,0:T(8,128)(2,1)} %copy-done.1) | copy-start | bytes 15728644
  245.1 7.7 %collective-permute-start.8 = (bf16[1024,64]{0,1:T(8,128)(2,1)S(1)}, bf16[1024,64]{0,1:T(8,128)(2,1)S(1)}, u32[]{:S(2)}, u32[]{:S(2)}) collective-permute-start(bf16[1024,64]{0,1:T(8,128)(2,1)S(1)} %fusion.3), channel_id=1, source_target_pairs={{0,2},{1,3},{2,4},{3,5},{4,6},{5,7},{6,0},{7,1},{8,10},{9,11},{10,... | collective-permute-start | bytes 393224 | tf_op jit(solution)/shard_map/ppermute | solution.py:22
  246.3 11.1 %collective-permute-start.9 = (bf16[1024,64]{0,1:T(8,128)(2,1)S(1)}, bf16[1024,64]{0,1:T(8,128)(2,1)S(1)}, u32[]{:S(2)}, u32[]{:S(2)}) collective-permute-start(bf16[1024,64]{0,1:T(8,128)(2,1)S(1)} %fusion.3), channel_id=1, source_target_pairs={{0,1},{1,2},{2,3},{3,4},{4,5},{5,6},{6,7},{7,0},{8,9},{9,10},{10,1... | collective-permute-start | bytes 393224 | tf_op jit(solution)/shard_map/ppermute | solution.py:22
  248.5 8.9 %collective-permute-start.10 = (bf16[1024,64]{0,1:T(8,128)(2,1)S(1)}, bf16[1024,64]{0,1:T(8,128)(2,1)S(1)}, u32[]{:S(2)}, u32[]{:S(2)}) collective-permute-start(bf16[1024,64]{0,1:T(8,128)(2,1)S(1)} %fusion.3), channel_id=1, source_target_pairs={{0,7},{1,0},{2,1},{3,2},{4,3},{5,4},{6,5},{7,6},{8,15},{9,8},{10,9... | collective-permute-start | bytes 393224 | tf_op jit(solution)/shard_map/ppermute | solution.py:22
  251.0 6.5 %collective-permute-start.11 = (bf16[1024,64]{0,1:T(8,128)(2,1)S(1)}, bf16[1024,64]{0,1:T(8,128)(2,1)S(1)}, u32[]{:S(2)}, u32[]{:S(2)}) collective-permute-start(bf16[1024,64]{0,1:T(8,128)(2,1)S(1)} %fusion.3), channel_id=1, source_target_pairs={{0,6},{1,7},{2,0},{3,1},{4,2},{5,3},{6,4},{7,5},{8,14},{9,15},{10,... | collective-permute-start | bytes 393224 | tf_op jit(solution)/shard_map/ppermute | solution.py:22
  315.2 7.7 %collective-permute-start.12 = (bf16[1024,64]{0,1:T(8,128)(2,1)S(1)}, bf16[1024,64]{0,1:T(8,128)(2,1)S(1)}, u32[]{:S(2)}, u32[]{:S(2)}) collective-permute-start(bf16[1024,64]{0,1:T(8,128)(2,1)S(1)} %fusion.4), channel_id=1, source_target_pairs={{0,2},{1,3},{2,4},{3,5},{4,6},{5,7},{6,0},{7,1},{8,10},{9,11},{10,... | collective-permute-start | bytes 393224 | tf_op jit(solution)/shard_map/ppermute | solution.py:22
  316.8 10.7 %collective-permute-start.13 = (bf16[1024,64]{0,1:T(8,128)(2,1)S(1)}, bf16[1024,64]{0,1:T(8,128)(2,1)S(1)}, u32[]{:S(2)}, u32[]{:S(2)}) collective-permute-start(bf16[1024,64]{0,1:T(8,128)(2,1)S(1)} %fusion.4), channel_id=1, source_target_pairs={{0,1},{1,2},{2,3},{3,4},{4,5},{5,6},{6,7},{7,0},{8,9},{9,10},{10,1... | collective-permute-start | bytes 393224 | tf_op jit(solution)/shard_map/ppermute | solution.py:22
  319.1 8.5 %collective-permute-start.14 = (bf16[1024,64]{0,1:T(8,128)(2,1)S(1)}, bf16[1024,64]{0,1:T(8,128)(2,1)S(1)}, u32[]{:S(2)}, u32[]{:S(2)}) collective-permute-start(bf16[1024,64]{0,1:T(8,128)(2,1)S(1)} %fusion.4), channel_id=1, source_target_pairs={{0,7},{1,0},{2,1},{3,2},{4,3},{5,4},{6,5},{7,6},{8,15},{9,8},{10,9... | collective-permute-start | bytes 393224 | tf_op jit(solution)/shard_map/ppermute | solution.py:22
  321.5 6.0 %collective-permute-start.15 = (bf16[1024,64]{0,1:T(8,128)(2,1)S(1)}, bf16[1024,64]{0,1:T(8,128)(2,1)S(1)}, u32[]{:S(2)}, u32[]{:S(2)}) collective-permute-start(bf16[1024,64]{0,1:T(8,128)(2,1)S(1)} %fusion.4), channel_id=1, source_target_pairs={{0,6},{1,7},{2,0},{3,1},{4,2},{5,3},{6,4},{7,5},{8,14},{9,15},{10,... | collective-permute-start | bytes 393224 | tf_op jit(solution)/shard_map/ppermute | solution.py:22
where the time goes:
time: 389 us
  waiting for transfers between devices  136 us (35%)
  blocking collectives  117 us (30%)
  matrix products  42.8 us (11%)
  other arithmetic  42.4 us (11%)
  starting transfers between devices  37.5 us (10%)
  local copies, waits for them, and re-layouts  12.3 us (3%)
    ppermute x16, waiting for transfers between devices, passed_along(): lax.ppermute(shard, axis, [(i, (i + by) % count) for i in range(count)])  136 us
    psum x3, blocking collectives, orthonormal(): gram_sum = lax.psum(gram_sum, ('row', 'col'))  117 us
    ppermute x16, starting transfers between devices, passed_along(): lax.ppermute(shard, axis, [(i, (i + by) % count) for i in range(count)])  37.5 us
    dot_general x2, matrix products, on_device(): lax.dot_general(own_blocks[member], point_rows, (((1,), (1,)), ((), ())),...  22 us
    another operation x9, other arithmetic, orthonormal(): factor = jnp.linalg.cholesky(gram_sum)  19.6 us
    dot_general x6, matrix products, on_device(): jnp.dot(tile_list[member], spread, preferred_element_type=jnp.float32)  17.7 us
    another operation x6, other arithmetic, orthonormal(): lax.linalg.triangular_solve(factor, image_rows, left_side=False, lower=Tr...  16.6 us
    unnamed x29, local copies, waits for them, and re-layouts  10.2 us
  transfers between devices with their start and end apart: 16, of which 9 were waited for; matrix products, arithmetic and copies ran while one was open for 3% of the time, Pallas kernels for 0%

commit v1 on v0

--- a/solution.py
+++ b/solution.py
@@ -51,6 +51,35 @@
     return assemble(pieces)
 
 
+def exchange_masks(row_count, col_count):
+    low = [1 << bit for bit in range(col_count.bit_length() - 1)]
+    high = [col_count << bit for bit in range(row_count.bit_length() - 1)]
+    stages = [(high[0],), (high[1], low[0]), (low[1], low[2])]
+    rest = high[2:] + low[3:]
+    return stages + [tuple(rest[at : at + 2]) for at in range(0, len(rest), 2)]
+
+
+def total_sum(value):
+    row_count = lax.axis_size("row")
+    col_count = lax.axis_size("col")
+    devices = row_count * col_count
+    if devices & (devices - 1) or row_count < 4 or col_count < 8:
+        return lax.psum(value, ("row", "col"))
+
+    def fetched(mask):
+        pairs = [(source, source ^ mask) for source in range(devices)]
+        return lax.ppermute(value, ("row", "col"), pairs)
+
+    for masks in exchange_masks(row_count, col_count):
+        if len(masks) == 1:
+            value = value + fetched(masks[0])
+        else:
+            first, second = masks
+            near, far, both = fetched(first), fetched(second), fetched(first ^ second)
+            value = (value + near) + (far + both)
+    return value
+
+
 def orthonormal(image_rows, total_rows):
     gram_sum = lax.dot_general(
         image_rows,
@@ -59,7 +88,7 @@
         precision=lax.Precision.HIGHEST,
         preferred_element_type=jnp.float32,
     )
-    gram_sum = lax.psum(gram_sum, ("row", "col"))
+    gram_sum = total_sum(gram_sum)
     factor = jnp.linalg.cholesky(gram_sum)
     solved = lax.linalg.triangular_solve(
         factor, image_rows, left_side=False, lower=True, transpose_a=True

time: 389 us -> 317 us (0.81)
  blocking collectives: 117 us -> 0 us
  starting transfers between devices: 37.5 us -> 61.5 us
  waiting for transfers between devices: 136 us -> 160 us
    psum x3 -> x0, blocking collectives: 117 us -> none  [orthonormal(): gram_sum = lax.psum(gram_sum, ('row', 'col'))]
    ppermute x0 -> x21, waiting for transfers between devices: none -> 28.8 us  [fetched(): return lax.ppermute(value, ('row', 'col'), pairs)]
    ppermute x0 -> x21, starting transfers between devices: none -> 24 us  [fetched(): return lax.ppermute(value, ('row', 'col'), pairs)]
    ppermute x16, waiting for transfers between devices: 136 us -> 131 us  [passed_along(): lax.ppermute(shard, axis, [(i, (i + by) % count) for i in range(count)])]
    unnamed x29 -> x33, local copies, waits for them, and re-layouts: 10.2 us -> 10.3 us
  transfers between devices with their start and end apart: 16 -> 37, of which waited for: 9 -> 29; matrix products, arithmetic and copies ran while one was open for 3% -> 4% of each run, Pallas kernels for 0% -> 0%
where the time goes in v1:
time: 317 us
  waiting for transfers between devices  160 us (50%)
  starting transfers between devices  61.5 us (19%)
  other arithmetic  42.5 us (13%)
  matrix products  40.2 us (13%)
  local copies, waits for them, and re-layouts  12.4 us (4%)
    ppermute x16, waiting for transfers between devices, passed_along(): lax.ppermute(shard, axis, [(i, (i + by) % count) for i in range(count)])  131 us
    ppermute x16, starting transfers between devices, passed_along(): lax.ppermute(shard, axis, [(i, (i + by) % count) for i in range(count)])  37.5 us
    ppermute x21, waiting for transfers between devices, fetched(): return lax.ppermute(value, ('row', 'col'), pairs)  28.8 us
    ppermute x21, starting transfers between devices, fetched(): return lax.ppermute(value, ('row', 'col'), pairs)  24 us
    dot_general x2, matrix products, on_device(): lax.dot_general(own_blocks[member], point_rows, (((1,), (1,)), ((), ())),...  22 us
    another operation x9, other arithmetic, orthonormal(): factor = jnp.linalg.cholesky(gram_sum)  19.6 us
    another operation x6, other arithmetic, orthonormal(): lax.linalg.triangular_solve(factor, image_rows, left_side=False, lower=Tr...  16.6 us
    dot_general x6, matrix products, on_device(): jnp.dot(tile_list[member], spread, preferred_element_type=jnp.float32)  15.2 us
  transfers between devices with their start and end apart: 37, of which 29 were waited for; matrix products, arithmetic and copies ran while one was open for 4% of the time, Pallas kernels for 0%

profile of v1, /device:TPU:0, one launch (start us, length us, event | category | flops | bytes accessed | tf_op | source)
XLA Modules:
  0.0 316.9 jit_solution(13005026280911991942)
XLA Ops:
  0.0 2.7 multiply_reduce_fusion
  3.5 1.6 multiply_convert_fusion
  5.1 3.1 collective-permute-start
  9.6 3.2 %collective-permute-start.2 = (bf16[1024,1024]{1,0:T(8,128)(2,1)}, bf16[1024,1024]{1,0:T(8,128)(2,1)}, u32[]{:S(2)}, u32[]{:S(2)}) collective-permute-start(bf16[1024,1024]{1,0:T(8,128)(2,1)} %multiply_convert_fusion), channel_id=1, source_target_pairs={{0,7},{1,0},{2,1},{3,2},{4,3},{5,4},{6,5},{7,6},{8,15},{9,8},{10,9... | collective-permute-start | bytes 6291464 | tf_op jit(solution)/shard_map/ppermute | solution.py:22
  13.7 43.3 %collective-permute-done = bf16[1024,1024]{1,0:T(8,128)(2,1)} collective-permute-done((bf16[1024,1024]{1,0:T(8,128)(2,1)}, bf16[1024,1024]{1,0:T(8,128)(2,1)}, u32[]{:S(2)}, u32[]{:S(2)}) %collective-permute-start) | collective-permute-done | bytes 2097184 | tf_op jit(solution)/shard_map/ppermute | solution.py:22
  57.0 3.1 constant_dynamic-update-slice_fusion.4
  60.1 43.0 %collective-permute-done.1 = bf16[1024,1024]{1,0:T(8,128)(2,1)} collective-permute-done((bf16[1024,1024]{1,0:T(8,128)(2,1)}, bf16[1024,1024]{1,0:T(8,128)(2,1)}, u32[]{:S(2)}, u32[]{:S(2)}) %collective-permute-start.1) | collective-permute-done | bytes 2097184 | tf_op jit(solution)/shard_map/ppermute | solution.py:22
  103.1 3.1 constant_dynamic-update-slice_fusion.3
  106.2 1.6 constant_dynamic-update-slice_fusion.2
  107.8 3.1 constant_dynamic-update-slice_fusion.1
  111.0 34.9 %collective-permute-done.3 = bf16[1024,1024]{1,0:T(8,128)(2,1)S(1)} collective-permute-done((bf16[1024,1024]{1,0:T(8,128)(2,1)}, bf16[1024,1024]{1,0:T(8,128)(2,1)S(1)}, u32[]{:S(2)}, u32[]{:S(2)}) %collective-permute-start.3) | collective-permute-done | bytes 2097184 | tf_op jit(solution)/shard_map/ppermute | solution.py:22
  147.4 10.0 %fusion.45 = (f32[512]{0:T(512)S(1)}, bf16[512,5120]{1,0:T(8,128)(2,1)S(1)}) fusion(f32[5120]{0:T(1024)S(1)} %mul.152, bf16[5120,1024]{1,0:T(8,128)(2,1)} %constant_dynamic-update-slice_fusion, bf16[1024,1024]{1,0:T(8,128)(2,1)} %multiply_convert_fusion), kind=kOutput, calls=%fused_computation.120 | convolution fusion | flops 5384437248 | bytes 16799744 | tf_op jit(solution)/shard_map/dot_general | solution.py:123
  157.4 11.9 %fusion.44 = (f32[512]{0:T(512)S(1)}, bf16[512,5120]{1,0:T(8,128)(2,1)S(1)}) fusion(f32[5120]{0:T(1024)S(1)} %mul.158, bf16[5120,1024]{1,0:T(8,128)(2,1)} %constant_dynamic-update-slice_fusion, bf16[1024,1024]{1,0:T(8,128)(2,1)} %multiply_convert_fusion), kind=kOutput, calls=%fused_computation.119 | convolution fusion | flops 5384437248 | bytes 16799744 | tf_op jit(solution)/shard_map/dot_general | solution.py:123
  171.6 3.3 %collective-permute-start.6 = (bf16[1024,64]{0,1:T(8,128)(2,1)S(1)}, bf16[1024,64]{0,1:T(8,128)(2,1)S(1)}, u32[]{:S(2)}, u32[]{:S(2)}) collective-permute-start(bf16[1024,64]{0,1:T(8,128)(2,1)S(1)} %multiply_convert_fusion.1), channel_id=1, source_target_pairs={{0,7},{1,0},{2,1},{3,2},{4,3},{5,4},{6,5},{7,6},{8,15},{9,8},{10,9... | collective-permute-start | bytes 393224 | tf_op jit(solution)/shard_map/ppermute | solution.py:22
  174.9 10.5 %collective-permute-start.7 = (bf16[1024,64]{0,1:T(8,128)(2,1)S(1)}, bf16[1024,64]{0,1:T(8,128)(2,1)S(1)}, u32[]{:S(2)}, u32[]{:S(2)}) collective-permute-start(bf16[1024,64]{0,1:T(8,128)(2,1)S(1)} %multiply_convert_fusion.1), channel_id=1, source_target_pairs={{0,6},{1,7},{2,0},{3,1},{4,2},{5,3},{6,4},{7,5},{8,14},{9,15},{10,... | collective-permute-start | bytes 393224 | tf_op jit(solution)/shard_map/ppermute | solution.py:22
  186.3 2.9 collective-permute-done.7
  189.2 1.7 convolution_multiply_fusion.5
  190.9 1.7 convolution_multiply_fusion.4
  194.4 2.9 collective-permute-start.11
  199.5 1.7 collective-permute-done.9
  201.2 1.6 collective-permute-start.12
  202.8 1.9 collective-permute-start.13
  205.7 2.5 collective-permute-done.13
  208.1 2.3 collective-permute-done.14
  210.6 5.8 %cholesky.59 = f32[64,64]{1,0:T(8,128)S(1)} custom-call(f32[64,64]{1,0:T(8,128)S(1)} %fusion.18), custom_call_target="Cholesky" | custom-call | tf_op jit(solution)/shard_map/jit(cholesky)/cholesky | solution.py:92
  217.8 4.9 %custom-call.7 = f32[1,64,64]{1,2,0:T(8,128)S(1)} custom-call(f32[1,64,64]{2,1,0:T(8,128)S(1)} %fusion.10), custom_call_target="InvertDiagBlocksLowerTriangular" | custom-call | tf_op jit(solution)/shard_map/triangular_solve/custom-call.0 | solution.py:93
  223.5 4.4 %collective-permute-start.17 = (bf16[1024,64]{0,1:T(8,128)(2,1)S(1)}, bf16[1024,64]{0,1:T(8,128)(2,1)S(1)}, u32[]{:S(2)}, u32[]{:S(2)}) collective-permute-start(bf16[1024,64]{0,1:T(8,128)(2,1)S(1)} %fusion.3), channel_id=1, source_target_pairs={{0,7},{1,0},{2,1},{3,2},{4,3},{5,4},{6,5},{7,6},{8,15},{9,8},{10,9... | collective-permute-start | bytes 393224 | tf_op jit(solution)/shard_map/ppermute | solution.py:22
  228.0 2.0 collective-permute-start.18
  232.9 4.2 %convolution_multiply_fusion.3 = f32[512,64]{0,1:T(8,128)S(1)} fusion(bf16[5120,64]{0,1:T(8,128)(2,1)S(1)} %constant_dynamic-update-slice_fusion.10, f32[512]{0:T(512)S(1)} %bitcast.70, bf16[512,5120]{1,0:T(8,128)(2,1)} %copy-done), kind=kOutput, calls=%fused_computation.15 | convolution fusion | flops 335577088 | bytes 6031360 | tf_op jit(solution)/shard_map/dot_general | solution.py:144
  237.1 1.7 convolution_multiply_fusion.2
  242.1 1.9 collective-permute-start.22
  245.3 1.6 collective-permute-done.22
  247.8 2.8 collective-permute-start.24
  252.6 3.7 %collective-permute-done.25 = f32[64,64]{0,1:T(8,128)S(1)} collective-permute-done((f32[64,64]{0,1:T(8,128)S(1)}, f32[64,64]{0,1:T(8,128)S(1)}, u32[]{:S(2)}, u32[]{:S(2)}) %collective-permute-start.25) | collective-permute-done | bytes 16416 | tf_op jit(solution)/shard_map/ppermute | solution.py:71
  256.5 5.8 %cholesky.70 = f32[64,64]{1,0:T(8,128)S(1)} custom-call(f32[64,64]{1,0:T(8,128)S(1)} %fusion.16), custom_call_target="Cholesky" | custom-call | tf_op jit(solution)/shard_map/jit(cholesky)/cholesky | solution.py:92
  263.6 4.9 %custom-call.8 = f32[1,64,64]{1,2,0:T(8,128)S(1)} custom-call(f32[1,64,64]{2,1,0:T(8,128)S(1)} %fusion.11), custom_call_target="InvertDiagBlocksLowerTriangular" | custom-call | tf_op jit(solution)/shard_map/triangular_solve/custom-call.0 | solution.py:93
  269.1 1.7 collective-permute-start.27
  270.7 3.2 %collective-permute-start.28 = (bf16[1024,64]{0,1:T(8,128)(2,1)S(1)}, bf16[1024,64]{0,1:T(8,128)(2,1)S(1)}, u32[]{:S(2)}, u32[]{:S(2)}) collective-permute-start(bf16[1024,64]{0,1:T(8,128)(2,1)S(1)} %fusion.4), channel_id=1, source_target_pairs={{0,7},{1,0},{2,1},{3,2},{4,3},{5,4},{6,5},{7,6},{8,15},{9,8},{10,9... | collective-permute-start | bytes 393224 | tf_op jit(solution)/shard_map/ppermute | solution.py:22
  273.9 1.9 collective-permute-start.29
  278.9 4.2 %convolution_multiply_fusion.1 = f32[512,64]{0,1:T(8,128)S(1)} fusion(bf16[5120,64]{0,1:T(8,128)(2,1)S(1)} %constant_dynamic-update-slice_fusion.15, f32[512]{0:T(512)S(1)} %bitcast.71, bf16[512,5120]{1,0:T(8,128)(2,1)} %copy-done), kind=kOutput, calls=%fused_computation.13 | convolution fusion | flops 335577088 | bytes 6031360 | tf_op jit(solution)/shard_map/dot_general | solution.py:144
  283.1 1.7 convolution_multiply_fusion
  286.5 1.5 collective-permute-start.31
  290.4 1.8 collective-permute-done.32
  292.2 2.1 collective-permute-done.33
  294.8 3.0 collective-permute-start.35
  299.7 3.8 %collective-permute-done.36 = f32[64,64]{0,1:T(8,128)S(1)} collective-permute-done((f32[64,64]{0,1:T(8,128)S(1)}, f32[64,64]{0,1:T(8,128)S(1)}, u32[]{:S(2)}, u32[]{:S(2)}) %collective-permute-start.36) | collective-permute-done | bytes 16416 | tf_op jit(solution)/shard_map/ppermute | solution.py:71
  303.7 5.8 %cholesky.81 = f32[64,64]{1,0:T(8,128)S(1)} custom-call(f32[64,64]{1,0:T(8,128)S(1)} %fusion.14), custom_call_target="Cholesky" | custom-call | tf_op jit(solution)/shard_map/jit(cholesky)/cholesky | solution.py:92
  310.9 4.9 %custom-call.9 = f32[1,64,64]{1,2,0:T(8,128)S(1)} custom-call(f32[1,64,64]{2,1,0:T(8,128)S(1)} %fusion.12), custom_call_target="InvertDiagBlocksLowerTriangular" | custom-call | tf_op jit(solution)/shard_map/triangular_solve/custom-call.0 | solution.py:93
  (127 shorter events, 39.1 us)
Async XLA Ops:
  0.0 3.4 %copy-start.3 = (f32[1024,1024]{1,0:T(8,128)S(1)}, f32[1024,1024]{1,0:T(8,128)}, u32[]{:S(2)}) copy-start(f32[1024,1024]{1,0:T(8,128)} %param.6) | copy-start | bytes 12582916
  0.0 13.1 %copy-start.6 = (s32[2,12]{1,0:T(2,128)S(1)}, s32[2,12]{1,0:T(2,128)}, u32[]{:S(2)}) copy-start(s32[2,12]{1,0:T(2,128)} %param.7) | copy-start | bytes 292
  5.1 51.9 %collective-permute-start = (bf16[1024,1024]{1,0:T(8,128)(2,1)}, bf16[1024,1024]{1,0:T(8,128)(2,1)}, u32[]{:S(2)}, u32[]{:S(2)}) collective-permute-start(bf16[1024,1024]{1,0:T(8,128)(2,1)} %multiply_convert_fusion), channel_id=1, source_target_pairs={{0,2},{1,3},{2,4},{3,5},{4,6},{5,7},{6,0},{7,1},{8,10},{9,11},{10,... | collective-permute-start | bytes 6291464 | tf_op jit(solution)/shard_map/ppermute | solution.py:22
  8.1 94.9 %collective-permute-start.1 = (bf16[1024,1024]{1,0:T(8,128)(2,1)}, bf16[1024,1024]{1,0:T(8,128)(2,1)}, u32[]{:S(2)}, u32[]{:S(2)}) collective-permute-start(bf16[1024,1024]{1,0:T(8,128)(2,1)} %multiply_convert_fusion), channel_id=1, source_target_pairs={{0,1},{1,2},{2,3},{3,4},{4,5},{5,6},{6,7},{7,0},{8,9},{9,10},{10,1... | collective-permute-start | bytes 6291464 | tf_op jit(solution)/shard_map/ppermute | solution.py:22
  9.6 98.2 %collective-permute-start.2 = (bf16[1024,1024]{1,0:T(8,128)(2,1)}, bf16[1024,1024]{1,0:T(8,128)(2,1)}, u32[]{:S(2)}, u32[]{:S(2)}) collective-permute-start(bf16[1024,1024]{1,0:T(8,128)(2,1)} %multiply_convert_fusion), channel_id=1, source_target_pairs={{0,7},{1,0},{2,1},{3,2},{4,3},{5,4},{6,5},{7,6},{8,15},{9,8},{10,9... | collective-permute-start | bytes 6291464 | tf_op jit(solution)/shard_map/ppermute | solution.py:22
  12.9 133.0 %collective-permute-start.3 = (bf16[1024,1024]{1,0:T(8,128)(2,1)}, bf16[1024,1024]{1,0:T(8,128)(2,1)S(1)}, u32[]{:S(2)}, u32[]{:S(2)}) collective-permute-start(bf16[1024,1024]{1,0:T(8,128)(2,1)} %multiply_convert_fusion), channel_id=1, source_target_pairs={{0,6},{1,7},{2,0},{3,1},{4,2},{5,3},{6,4},{7,5},{8,14},{9,15},{10,... | collective-permute-start | bytes 6291464 | tf_op jit(solution)/shard_map/ppermute | solution.py:22
  13.7 92.5 %copy-start.4 = (f32[1024,1024]{1,0:T(8,128)S(1)}, f32[1024,1024]{1,0:T(8,128)}, u32[]{:S(2)}) copy-start(f32[1024,1024]{1,0:T(8,128)} %param.6) | copy-start | bytes 12582916
  157.4 31.8 %copy-start = (bf16[512,5120]{1,0:T(8,128)(2,1)}, bf16[512,5120]{1,0:T(8,128)(2,1)S(1)}, u32[]{:S(2)}) copy-start(bf16[512,5120]{1,0:T(8,128)(2,1)S(1)} %get-tuple-element.16) | copy-start | bytes 15728644
  157.4 12.0 %copy-start.5 = (f32[1024,64]{0,1:T(8,128)S(1)}, f32[1024,64]{0,1:T(8,128)}, u32[]{:S(2)}) copy-start(f32[1024,64]{0,1:T(8,128)} %param.8) | copy-start | bytes 786436
  169.4 23.3 %copy-start.1 = (bf16[512,5120]{1,0:T(8,128)(2,1)}, bf16[512,5120]{1,0:T(8,128)(2,1)S(1)}, u32[]{:S(2)}) copy-start(bf16[512,5120]{1,0:T(8,128)(2,1)S(1)} %get-tuple-element.14) | copy-start | bytes 15728644
  169.5 15.9 %collective-permute-start.4 = (bf16[1024,64]{0,1:T(8,128)(2,1)S(1)}, bf16[1024,64]{0,1:T(8,128)(2,1)S(1)}, u32[]{:S(2)}, u32[]{:S(2)}) collective-permute-start(bf16[1024,64]{0,1:T(8,128)(2,1)S(1)} %multiply_convert_fusion.1), channel_id=1, source_target_pairs={{0,2},{1,3},{2,4},{3,5},{4,6},{5,7},{6,0},{7,1},{8,10},{9,11},{10,... | collective-permute-start | bytes 393224 | tf_op jit(solution)/shard_map/ppermute | solution.py:22
  170.1 15.2 %collective-permute-start.5 = (bf16[1024,64]{0,1:T(8,128)(2,1)S(1)}, bf16[1024,64]{0,1:T(8,128)(2,1)S(1)}, u32[]{:S(2)}, u32[]{:S(2)}) collective-permute-start(bf16[1024,64]{0,1:T(8,128)(2,1)S(1)} %multiply_convert_fusion.1), channel_id=1, source_target_pairs={{0,1},{1,2},{2,3},{3,4},{4,5},{5,6},{6,7},{7,0},{8,9},{9,10},{10,1... | collective-permute-start | bytes 393224 | tf_op jit(solution)/shard_map/ppermute | solution.py:22
  171.6 14.8 %collective-permute-start.6 = (bf16[1024,64]{0,1:T(8,128)(2,1)S(1)}, bf16[1024,64]{0,1:T(8,128)(2,1)S(1)}, u32[]{:S(2)}, u32[]{:S(2)}) collective-permute-start(bf16[1024,64]{0,1:T(8,128)(2,1)S(1)} %multiply_convert_fusion.1), channel_id=1, source_target_pairs={{0,7},{1,0},{2,1},{3,2},{4,3},{5,4},{6,5},{7,6},{8,15},{9,8},{10,9... | collective-permute-start | bytes 393224 | tf_op jit(solution)/shard_map/ppermute | solution.py:22
  174.9 14.3 %collective-permute-start.7 = (bf16[1024,64]{0,1:T(8,128)(2,1)S(1)}, bf16[1024,64]{0,1:T(8,128)(2,1)S(1)}, u32[]{:S(2)}, u32[]{:S(2)}) collective-permute-start(bf16[1024,64]{0,1:T(8,128)(2,1)S(1)} %multiply_convert_fusion.1), channel_id=1, source_target_pairs={{0,6},{1,7},{2,0},{3,1},{4,2},{5,3},{6,4},{7,5},{8,14},{9,15},{10,... | collective-permute-start | bytes 393224 | tf_op jit(solution)/shard_map/ppermute | solution.py:22
  193.0 1.3 collective-permute-start.8
  194.3 4.0 %collective-permute-start.10 = (f32[64,64]{0,1:T(8,128)S(1)}, f32[64,64]{0,1:T(8,128)S(1)}, u32[]{:S(2)}, u32[]{:S(2)}) collective-permute-start(f32[64,64]{0,1:T(8,128)S(1)} %add.134), channel_id=1, source_target_pairs={{0,1},{1,0},{2,3},{3,2},{4,5},{5,4},{6,7},{7,6},{8,9},{9,8},{10,11... | collective-permute-start | bytes 49160 | tf_op jit(solution)/shard_map/ppermute | solution.py:71
  194.4 5.1 %collective-permute-start.11 = (f32[64,64]{0,1:T(8,128)S(1)}, f32[64,64]{0,1:T(8,128)S(1)}, u32[]{:S(2)}, u32[]{:S(2)}) collective-permute-start(f32[64,64]{0,1:T(8,128)S(1)} %add.134), channel_id=1, source_target_pairs={{0,17},{1,16},{2,19},{3,18},{4,21},{5,20},{6,23},{7,22},{8,25},{9,... | collective-permute-start | bytes 49160 | tf_op jit(solution)/shard_map/ppermute | solution.py:71
  197.3 3.9 %collective-permute-start.9 = (f32[64,64]{0,1:T(8,128)S(1)}, f32[64,64]{0,1:T(8,128)S(1)}, u32[]{:S(2)}, u32[]{:S(2)}) collective-permute-start(f32[64,64]{0,1:T(8,128)S(1)} %add.134), channel_id=1, source_target_pairs={{0,16},{1,17},{2,18},{3,19},{4,20},{5,21},{6,22},{7,23},{8,24},{9,... | collective-permute-start | bytes 49160 | tf_op jit(solution)/shard_map/ppermute | solution.py:71
  201.2 4.5 %collective-permute-start.12 = (f32[64,64]{0,1:T(8,128)S(1)}, f32[64,64]{0,1:T(8,128)S(1)}, u32[]{:S(2)}, u32[]{:S(2)}) collective-permute-start(f32[64,64]{0,1:T(8,128)S(1)} %add_add_fusion.5), channel_id=1, source_target_pairs={{0,2},{1,3},{2,0},{3,1},{4,6},{5,7},{6,4},{7,5},{8,10},{9,11},{10,... | collective-permute-start | bytes 49160 | tf_op jit(solution)/shard_map/ppermute | solution.py:71
  202.8 5.3 %collective-permute-start.13 = (f32[64,64]{0,1:T(8,128)S(1)}, f32[64,64]{0,1:T(8,128)S(1)}, u32[]{:S(2)}, u32[]{:S(2)}) collective-permute-start(f32[64,64]{0,1:T(8,128)S(1)} %add_add_fusion.5), channel_id=1, source_target_pairs={{0,4},{1,5},{2,6},{3,7},{4,0},{5,1},{6,2},{7,3},{8,12},{9,13},{10,... | collective-permute-start | bytes 49160 | tf_op jit(solution)/shard_map/ppermute | solution.py:71
  204.8 5.7 %collective-permute-start.14 = (f32[64,64]{0,1:T(8,128)S(1)}, f32[64,64]{0,1:T(8,128)S(1)}, u32[]{:S(2)}, u32[]{:S(2)}) collective-permute-start(f32[64,64]{0,1:T(8,128)S(1)} %add_add_fusion.5), channel_id=1, source_target_pairs={{0,6},{1,7},{2,4},{3,5},{4,2},{5,3},{6,0},{7,1},{8,14},{9,15},{10,... | collective-permute-start | bytes 49160 | tf_op jit(solution)/shard_map/ppermute | solution.py:71
  222.7 14.5 %copy-start.2 = (bf16[512,5120]{1,0:T(8,128)(2,1)S(1)}, bf16[512,5120]{1,0:T(8,128)(2,1)}, u32[]{:S(2)}) copy-start(bf16[512,5120]{1,0:T(8,128)(2,1)} %copy-done.1) | copy-start | bytes 15728644
  223.1 8.2 %collective-permute-start.15 = (bf16[1024,64]{0,1:T(8,128)(2,1)S(1)}, bf16[1024,64]{0,1:T(8,128)(2,1)S(1)}, u32[]{:S(2)}, u32[]{:S(2)}) collective-permute-start(bf16[1024,64]{0,1:T(8,128)(2,1)S(1)} %fusion.3), channel_id=1, source_target_pairs={{0,2},{1,3},{2,4},{3,5},{4,6},{5,7},{6,0},{7,1},{8,10},{9,11},{10,... | collective-permute-start | bytes 393224 | tf_op jit(solution)/shard_map/ppermute | solution.py:22
  223.2 8.6 %collective-permute-start.16 = (bf16[1024,64]{0,1:T(8,128)(2,1)S(1)}, bf16[1024,64]{0,1:T(8,128)(2,1)S(1)}, u32[]{:S(2)}, u32[]{:S(2)}) collective-permute-start(bf16[1024,64]{0,1:T(8,128)(2,1)S(1)} %fusion.3), channel_id=1, source_target_pairs={{0,1},{1,2},{2,3},{3,4},{4,5},{5,6},{6,7},{7,0},{8,9},{9,10},{10,1... | collective-permute-start | bytes 393224 | tf_op jit(solution)/shard_map/ppermute | solution.py:22
  223.5 8.3 %collective-permute-start.17 = (bf16[1024,64]{0,1:T(8,128)(2,1)S(1)}, bf16[1024,64]{0,1:T(8,128)(2,1)S(1)}, u32[]{:S(2)}, u32[]{:S(2)}) collective-permute-start(bf16[1024,64]{0,1:T(8,128)(2,1)S(1)} %fusion.3), channel_id=1, source_target_pairs={{0,7},{1,0},{2,1},{3,2},{4,3},{5,4},{6,5},{7,6},{8,15},{9,8},{10,9... | collective-permute-start | bytes 393224 | tf_op jit(solution)/shard_map/ppermute | solution.py:22
  228.0 5.0 %collective-permute-start.18 = (bf16[1024,64]{0,1:T(8,128)(2,1)S(1)}, bf16[1024,64]{0,1:T(8,128)(2,1)S(1)}, u32[]{:S(2)}, u32[]{:S(2)}) collective-permute-start(bf16[1024,64]{0,1:T(8,128)(2,1)S(1)} %fusion.3), channel_id=1, source_target_pairs={{0,6},{1,7},{2,0},{3,1},{4,2},{5,3},{6,4},{7,5},{8,14},{9,15},{10,... | collective-permute-start | bytes 393224 | tf_op jit(solution)/shard_map/ppermute | solution.py:22
  237.1 46.0 %slice-start = ((s8[5242880]{0:T(1024)(128)(4,1)}), s8[1048576]{0:T(1024)(128)(4,1)S(1)}, s32[]{:S(2)}) async-start(s8[5242880]{0:T(1024)(128)(4,1)} %bitcast.64), calls=%async_computation | async-start | bytes 2097152
  239.2 1.3 collective-permute-start.19
  240.5 3.9 %collective-permute-start.20 = (f32[64,64]{0,1:T(8,128)S(1)}, f32[64,64]{0,1:T(8,128)S(1)}, u32[]{:S(2)}, u32[]{:S(2)}) collective-permute-start(f32[64,64]{0,1:T(8,128)S(1)} %add.141), channel_id=1, source_target_pairs={{0,16},{1,17},{2,18},{3,19},{4,20},{5,21},{6,22},{7,23},{8,24},{9,... | collective-permute-start | bytes 49160 | tf_op jit(solution)/shard_map/ppermute | solution.py:71
  241.1 4.1 %collective-permute-start.21 = (f32[64,64]{0,1:T(8,128)S(1)}, f32[64,64]{0,1:T(8,128)S(1)}, u32[]{:S(2)}, u32[]{:S(2)}) collective-permute-start(f32[64,64]{0,1:T(8,128)S(1)} %add.141), channel_id=1, source_target_pairs={{0,1},{1,0},{2,3},{3,2},{4,5},{5,4},{6,7},{7,6},{8,9},{9,8},{10,11... | collective-permute-start | bytes 49160 | tf_op jit(solution)/shard_map/ppermute | solution.py:71
  242.1 4.8 %collective-permute-start.22 = (f32[64,64]{0,1:T(8,128)S(1)}, f32[64,64]{0,1:T(8,128)S(1)}, u32[]{:S(2)}, u32[]{:S(2)}) collective-permute-start(f32[64,64]{0,1:T(8,128)S(1)} %add.141), channel_id=1, source_target_pairs={{0,17},{1,16},{2,19},{3,18},{4,21},{5,20},{6,23},{7,22},{8,25},{9,... | collective-permute-start | bytes 49160 | tf_op jit(solution)/shard_map/ppermute | solution.py:71
  246.9 4.5 %collective-permute-start.23 = (f32[64,64]{0,1:T(8,128)S(1)}, f32[64,64]{0,1:T(8,128)S(1)}, u32[]{:S(2)}, u32[]{:S(2)}) collective-permute-start(f32[64,64]{0,1:T(8,128)S(1)} %add_add_fusion.3), channel_id=1, source_target_pairs={{0,2},{1,3},{2,0},{3,1},{4,6},{5,7},{6,4},{7,5},{8,10},{9,11},{10,... | collective-permute-start | bytes 49160 | tf_op jit(solution)/shard_map/ppermute | solution.py:71
  247.8 4.8 %collective-permute-start.24 = (f32[64,64]{0,1:T(8,128)S(1)}, f32[64,64]{0,1:T(8,128)S(1)}, u32[]{:S(2)}, u32[]{:S(2)}) collective-permute-start(f32[64,64]{0,1:T(8,128)S(1)} %add_add_fusion.3), channel_id=1, source_target_pairs={{0,4},{1,5},{2,6},{3,7},{4,0},{5,1},{6,2},{7,3},{8,12},{9,13},{10,... | collective-permute-start | bytes 49160 | tf_op jit(solution)/shard_map/ppermute | solution.py:71
  250.6 5.7 %collective-permute-start.25 = (f32[64,64]{0,1:T(8,128)S(1)}, f32[64,64]{0,1:T(8,128)S(1)}, u32[]{:S(2)}, u32[]{:S(2)}) collective-permute-start(f32[64,64]{0,1:T(8,128)S(1)} %add_add_fusion.3), channel_id=1, source_target_pairs={{0,6},{1,7},{2,4},{3,5},{4,2},{5,3},{6,0},{7,1},{8,14},{9,15},{10,... | collective-permute-start | bytes 49160 | tf_op jit(solution)/shard_map/ppermute | solution.py:71
  268.5 14.6 %slice-start.1 = ((s8[5242880]{0:T(1024)(128)(4,1)}), s8[4194304]{0:T(1024)(128)(4,1)S(1)}, s32[]{:S(2)}) async-start(s8[5242880]{0:T(1024)(128)(4,1)} %bitcast.64), calls=%async_computation.1 | async-start | bytes 8388608
  269.0 8.2 %collective-permute-start.26 = (bf16[1024,64]{0,1:T(8,128)(2,1)S(1)}, bf16[1024,64]{0,1:T(8,128)(2,1)S(1)}, u32[]{:S(2)}, u32[]{:S(2)}) collective-permute-start(bf16[1024,64]{0,1:T(8,128)(2,1)S(1)} %fusion.4), channel_id=1, source_target_pairs={{0,2},{1,3},{2,4},{3,5},{4,6},{5,7},{6,0},{7,1},{8,10},{9,11},{10,... | collective-permute-start | bytes 393224 | tf_op jit(solution)/shard_map/ppermute | solution.py:22
  269.1 9.3 %collective-permute-start.27 = (bf16[1024,64]{0,1:T(8,128)(2,1)S(1)}, bf16[1024,64]{0,1:T(8,128)(2,1)S(1)}, u32[]{:S(2)}, u32[]{:S(2)}) collective-permute-start(bf16[1024,64]{0,1:T(8,128)(2,1)S(1)} %fusion.4), channel_id=1, source_target_pairs={{0,1},{1,2},{2,3},{3,4},{4,5},{5,6},{6,7},{7,0},{8,9},{9,10},{10,1... | collective-permute-start | bytes 393224 | tf_op jit(solution)/shard_map/ppermute | solution.py:22
  270.7 7.7 %collective-permute-start.28 = (bf16[1024,64]{0,1:T(8,128)(2,1)S(1)}, bf16[1024,64]{0,1:T(8,128)(2,1)S(1)}, u32[]{:S(2)}, u32[]{:S(2)}) collective-permute-start(bf16[1024,64]{0,1:T(8,128)(2,1)S(1)} %fusion.4), channel_id=1, source_target_pairs={{0,7},{1,0},{2,1},{3,2},{4,3},{5,4},{6,5},{7,6},{8,15},{9,8},{10,9... | collective-permute-start | bytes 393224 | tf_op jit(solution)/shard_map/ppermute | solution.py:22
  273.9 5.0 %collective-permute-start.29 = (bf16[1024,64]{0,1:T(8,128)(2,1)S(1)}, bf16[1024,64]{0,1:T(8,128)(2,1)S(1)}, u32[]{:S(2)}, u32[]{:S(2)}) collective-permute-start(bf16[1024,64]{0,1:T(8,128)(2,1)S(1)} %fusion.4), channel_id=1, source_target_pairs={{0,6},{1,7},{2,0},{3,1},{4,2},{5,3},{6,4},{7,5},{8,14},{9,15},{10,... | collective-permute-start | bytes 393224 | tf_op jit(solution)/shard_map/ppermute | solution.py:22
  285.2 1.3 collective-permute-start.30
  286.5 3.9 %collective-permute-start.31 = (f32[64,64]{0,1:T(8,128)S(1)}, f32[64,64]{0,1:T(8,128)S(1)}, u32[]{:S(2)}, u32[]{:S(2)}) collective-permute-start(f32[64,64]{0,1:T(8,128)S(1)} %add.148), channel_id=1, source_target_pairs={{0,16},{1,17},{2,18},{3,19},{4,20},{5,21},{6,22},{7,23},{8,24},{9,... | collective-permute-start | bytes 49160 | tf_op jit(solution)/shard_map/ppermute | solution.py:71
  288.0 4.2 %collective-permute-start.32 = (f32[64,64]{0,1:T(8,128)S(1)}, f32[64,64]{0,1:T(8,128)S(1)}, u32[]{:S(2)}, u32[]{:S(2)}) collective-permute-start(f32[64,64]{0,1:T(8,128)S(1)} %add.148), channel_id=1, source_target_pairs={{0,1},{1,0},{2,3},{3,2},{4,5},{5,4},{6,7},{7,6},{8,9},{9,8},{10,11... | collective-permute-start | bytes 49160 | tf_op jit(solution)/shard_map/ppermute | solution.py:71
  289.5 4.8 %collective-permute-start.33 = (f32[64,64]{0,1:T(8,128)S(1)}, f32[64,64]{0,1:T(8,128)S(1)}, u32[]{:S(2)}, u32[]{:S(2)}) collective-permute-start(f32[64,64]{0,1:T(8,128)S(1)} %add.148), channel_id=1, source_target_pairs={{0,17},{1,16},{2,19},{3,18},{4,21},{5,20},{6,23},{7,22},{8,25},{9,... | collective-permute-start | bytes 49160 | tf_op jit(solution)/shard_map/ppermute | solution.py:71
  294.3 4.5 %collective-permute-start.34 = (f32[64,64]{0,1:T(8,128)S(1)}, f32[64,64]{0,1:T(8,128)S(1)}, u32[]{:S(2)}, u32[]{:S(2)}) collective-permute-start(f32[64,64]{0,1:T(8,128)S(1)} %add_add_fusion.1), channel_id=1, source_target_pairs={{0,2},{1,3},{2,0},{3,1},{4,6},{5,7},{6,4},{7,5},{8,10},{9,11},{10,... | collective-permute-start | bytes 49160 | tf_op jit(solution)/shard_map/ppermute | solution.py:71
  294.8 4.9 %collective-permute-start.35 = (f32[64,64]{0,1:T(8,128)S(1)}, f32[64,64]{0,1:T(8,128)S(1)}, u32[]{:S(2)}, u32[]{:S(2)}) collective-permute-start(f32[64,64]{0,1:T(8,128)S(1)} %add_add_fusion.1), channel_id=1, source_target_pairs={{0,4},{1,5},{2,6},{3,7},{4,0},{5,1},{6,2},{7,3},{8,12},{9,13},{10,... | collective-permute-start | bytes 49160 | tf_op jit(solution)/shard_map/ppermute | solution.py:71
  297.8 5.7 %collective-permute-start.36 = (f32[64,64]{0,1:T(8,128)S(1)}, f32[64,64]{0,1:T(8,128)S(1)}, u32[]{:S(2)}, u32[]{:S(2)}) collective-permute-start(f32[64,64]{0,1:T(8,128)S(1)} %add_add_fusion.1), channel_id=1, source_target_pairs={{0,6},{1,7},{2,4},{3,5},{4,2},{5,3},{6,0},{7,1},{8,14},{9,15},{10,... | collective-permute-start | bytes 49160 | tf_op jit(solution)/shard_map/ppermute | solution.py:71

commit v2 on v1

v2 whole, which is shorter than its diff:
```python
import functools
import math

import jax
import jax.numpy as jnp
from jax import lax
from jax.experimental import pallas as pl
from jax.experimental.pallas import tpu as pltpu
from jax.sharding import PartitionSpec as P

REACH = 2
ITERS = 3
BLK_DEV = 2

SHARP = 8.0
EPSILON = 1e-06

F32 = jnp.float32
BF16 = jnp.bfloat16
EXACT = lax.Precision.HIGHEST
VMEM = pl.BlockSpec(memory_space=pltpu.VMEM)
SMEM = pl.BlockSpec(memory_space=pltpu.SMEM)


def call(body, out_shape, in_specs, name, flops, moved):
    return pl.pallas_call(
        body,
        out_shape=out_shape,
        in_specs=in_specs,
        out_specs=jax.tree.map(lambda _: VMEM, out_shape),
        cost_estimate=pl.CostEstimate(flops=flops, bytes_accessed=moved, transcendentals=0),
        compiler_params=pltpu.CompilerParams(vmem_limit_bytes=56 << 20),
        name=name,
    )


def shaped(shape, dtype):
    return jax.ShapeDtypeStruct(shape, dtype)


def cross(left, right, **kw):
    return lax.dot_general(
        left, right, (((1,), (1,)), ((), ())), preferred_element_type=F32, **kw
    )


def unit_rows_body(points_ref, out_ref):
    points = points_ref[...]
    mean = jnp.mean(points * points, axis=-1, keepdims=True)
    out_ref[...] = (points * lax.rsqrt(mean + EPSILON)).astype(BF16)


def unit_rows(points, block, size):
    width = points.shape[1]
    step = 128
    per = size // step
    return pl.pallas_call(
        unit_rows_body,
        grid=(per,),
        in_specs=[pl.BlockSpec((step, width), lambda i: (block * per + i, 0))],
        out_specs=pl.BlockSpec((step, width), lambda i: (i, 0)),
        out_shape=shaped((size, width), BF16),
        cost_estimate=pl.CostEstimate(
            flops=3 * size * width, bytes_accessed=6 * size * width, transcendentals=0
        ),
        name="unit_rows",
    )(points)


def affinity(rows, cols):
    width = rows.shape[1]
    return jnp.exp(cross(rows, cols) * (SHARP / width) - SHARP)


def down(tile):
    return jnp.sum(tile, axis=0, keepdims=True)


def across(tile):
    lanes = 128
    folded = tile[:, :lanes]
    for at in range(lanes, tile.shape[1], lanes):
        folded = folded + tile[:, at : at + lanes]
    return jnp.sum(folded.T, axis=0, keepdims=True)


def own_tiles_body(b0, b1, oo, sums):
    size = b0.shape[0]
    for l, rows in enumerate((b0, b1)):
        for m, cols in enumerate((b0, b1)):
            tile = affinity(rows[...], cols[...])
            oo[l * size : (l + 1) * size, m * size : (m + 1) * size] = tile.astype(BF16)
            sums[l : l + 1, m * size : (m + 1) * size] = down(tile)


def row_tiles(rows, owns, out, sums):
    size = rows.shape[0]
    for m, cols in enumerate(owns):
        tile = affinity(rows[...], cols[...])
        out[:, m * size : (m + 1) * size] = tile.astype(BF16)
        sums[:, m * size : (m + 1) * size] = down(tile)


def col_tiles(owns, cols, out, sums, side):
    size = cols.shape[0]
    for l, rows in enumerate(owns):
        tile = affinity(rows[...], cols[...])
        out[l * size : (l + 1) * size, :] = tile.astype(BF16)
        sums[l : l + 1, :] = down(tile)
        side[:, l * size : (l + 1) * size] = across(tile)


def one_tile(rows, cols, out, sums):
    tile = affinity(rows[...], cols[...])
    out[...] = tile.astype(BF16)
    sums[...] = down(tile)


def first_tiles_body(b0, b1, x0, z0, x0o, x0o_s, oz0, oz0_s, oz0_r, x0z0, x0z0_s):
    row_tiles(x0, (b0, b1), x0o, x0o_s)
    col_tiles((b0, b1), z0, oz0, oz0_s, oz0_r)
    one_tile(x0, z0, x0z0, x0z0_s)


def last_tiles_body(
    b0, b1, x0, x1, z0, z1,
    x1o, x1o_s, oz1, oz1_s, oz1_r, x1z0, x1z0_s, x0z1, x0z1_s, x1z1, x1z1_s,
):
    row_tiles(x1, (b0, b1), x1o, x1o_s)
    one_tile(x1, z0, x1z0, x1z0_s)
    col_tiles((b0, b1), z1, oz1, oz1_s, oz1_r)
    one_tile(x0, z1, x0z1, x0z1_s)
    one_tile(x1, z1, x1z1, x1z1_s)


def kept(vectors, mask):
    return jnp.where(mask > 0.0, vectors, jnp.zeros_like(vectors))


def far_rows_body(mask, own, x, oz0, oz1, x0z0, x1z0, x0z1, x1z1, out):
    size = x0z0.shape[0]
    for m, (oz, xz) in enumerate(((oz0, (x0z0, x1z0)), (oz1, (x0z1, x1z1)))):
        total = None
        for l in range(BLK_DEV):
            here = slice(l * size, (l + 1) * size)
            part = jnp.dot(kept(own[:, here], mask[m, l]), oz[here, :], preferred_element_type=F32)
            part += jnp.dot(
                kept(x[:, here], mask[m, BLK_DEV + l]), xz[l][...], preferred_element_type=F32
            )
            total = part if total is None else total + part
        out[:, m * size : (m + 1) * size] = total


def own_rows_body(mask, own, x, z, given, root, oo, x0o, x1o, oz0, oz1, image, gram):
    size = x0o.shape[0]
    for m in range(BLK_DEV):
        there = slice(m * size, (m + 1) * size)
        total = given[:, there]
        for l, (xo, oz) in enumerate(((x0o, oz0), (x1o, oz1))):
            here = slice(l * size, (l + 1) * size)
            total += jnp.dot(
                kept(own[:, here], mask[m, l]), oo[here, there], preferred_element_type=F32
            )
            total += jnp.dot(
                kept(x[:, here], mask[m, BLK_DEV + l]), xo[:, there], preferred_element_type=F32
            )
            total += cross(kept(z[:, here], mask[m, 2 * BLK_DEV + l]), oz[there, :])
        image[:, there] = total * root[:, there]
    full = image[...]
    gram[...] = cross(full, full, precision=EXACT)


def inverse_factor(gram):
    size = gram.shape[0]
    rows = lax.broadcasted_iota(jnp.int32, (size, 2 * size), 0)
    lanes = lax.broadcasted_iota(jnp.int32, (size, 2 * size), 1)
    unit = jnp.where(rows + size == lanes, 1.0, 0.0).astype(F32)
    work = jnp.concatenate([gram, unit[:, size:]], axis=1)
    for j in range(size):
        pivot_row = work[j : j + 1, :]
        scale = 1.0 / pivot_row[:, j : j + 1]
        factor = jnp.where(rows[:, :1] > j, work[:, j : j + 1] * scale, 0.0)
        work = work - factor * pivot_row
    diagonal = jnp.sum(jnp.where(rows == lanes, work, 0.0), axis=1, keepdims=True)
    return work[:, size:] * lax.rsqrt(diagonal)


def solve_body(scale, gram, image, root, out, scaled):
    factor = inverse_factor(gram[...])
    vectors = jnp.dot(factor, image[...], preferred_element_type=F32, precision=EXACT) * scale
    out[...] = vectors
    scaled[...] = (vectors * root[...]).astype(BF16)


def exchange_masks(row_count, col_count):
    low = [1 << bit for bit in range(col_count.bit_length() - 1)]
    high = [col_count << bit for bit in range(row_count.bit_length() - 1)]
    stages = [(high[0],), (high[1], low[0]), (low[1], low[2])]
    rest = high[2:] + low[3:]
    return stages + [tuple(rest[at : at + 2]) for at in range(0, len(rest), 2)]


def total_sum(value):
    row_count = lax.axis_size("row")
    col_count = lax.axis_size("col")
    devices = row_count * col_count
    if devices & (devices - 1) or row_count < 4 or col_count < 8:
        return lax.psum(value, ("row", "col"))

    def fetched(mask):
        pairs = [(source, source ^ mask) for source in range(devices)]
        return lax.ppermute(value, ("row", "col"), pairs)

    for masks in exchange_masks(row_count, col_count):
        if len(masks) == 1:
            value = value + fetched(masks[0])
        else:
            first, second = masks
            near, far, both = fetched(first), fetched(second), fetched(first ^ second)
            value = (value + near) + (far + both)
    return value


def on_device(embeddings, neighbour_ids, start_vectors):
    col_count = lax.axis_size("col")
    col = lax.axis_index("col")
    base = lax.axis_index("row") * col_count
    points, width = embeddings.shape
    columns = start_vectors.shape[1]
    size = points // BLK_DEV
    total_rows = points * lax.axis_size("row") * col_count

    def side_of(index):
        return (index + (REACH if index % 2 == 0 else -REACH)) % col_count

    def from_x(value):
        return lax.ppermute(value, "col", [(i, i ^ 1) for i in range(col_count)])

    def from_z(value):
        return lax.ppermute(value, "col", [(side_of(i), i) for i in range(col_count)])

    def to_z(value):
        return lax.ppermute(value, "col", [(i, side_of(i)) for i in range(col_count)])

    b0 = unit_rows(embeddings, 0, size)
    z0 = from_z(b0)
    x0 = from_x(b0)
    b1 = unit_rows(embeddings, 1, size)
    z1 = from_z(b1)
    x1 = from_x(b1)
    far_ids = from_z(neighbour_ids)

    here = base + col
    x_side = base + (col ^ 1)
    z_side = base + (col + jnp.where(col % 2 == 0, REACH, col_count - REACH)) % col_count
    members = jnp.arange(BLK_DEV, dtype=jnp.int32)
    near = jnp.stack([here, x_side, z_side])[:, None] * BLK_DEV + members[None, :]
    near = near.reshape(-1)
    own_mask = jnp.max((neighbour_ids[:, :, None] == near[None, None, :]).astype(F32), axis=1)
    far_mask = jnp.max(
        (far_ids[:, :, None] == near[None, None, : 2 * BLK_DEV]).astype(F32), axis=1
    )

    half, tile = shaped((size, points), BF16), shaped((size, size), BF16)
    tall = shaped((points, size), BF16)
    line, short = shaped((1, points), F32), shaped((1, size), F32)
    two, pair = shaped((BLK_DEV, points), F32), shaped((BLK_DEV, size), F32)
    square = shaped((points, points), BF16)
    one = 2 * size * size * width
    moved = 4 * size * width
    oo, oo_s = call(own_tiles_body, (square, two), [VMEM] * 2, "own_tiles", 4 * one, 4 * moved)(
        b0, b1
    )
    x0o, x0o_s, oz0, oz0_s, oz0_r, x0z0, x0z0_s = call(
        first_tiles_body,
        (half, line, tall, pair, line, tile, short),
        [VMEM] * 4, "first_tiles", 5 * one, 5 * moved,
    )(b0, b1, x0, z0)
    x1o, x1o_s, oz1, oz1_s, oz1_r, x1z0, x1z0_s, x0z1, x0z1_s, x1z1, x1z1_s = call(
        last_tiles_body,
        (half, line, tall, pair, line, tile, short, tile, short, tile, short),
        [VMEM] * 6, "last_tiles", 7 * one, 7 * moved,
    )(b0, b1, x0, x1, z0, z1)

    lanes = jnp.repeat(own_mask.T, size, axis=1)
    sums = jnp.concatenate([oo_s, x0o_s, x1o_s, oz0_r, oz1_r], axis=0)
    own_degree = jnp.sum(jnp.where(lanes > 0, sums, 0.0), axis=0, keepdims=True)
    far_lanes = jnp.repeat(far_mask.T, size, axis=1)
    far_sums = jnp.concatenate(
        [
            jnp.concatenate([oz0_s, x0z0_s, x1z0_s], axis=0),
            jnp.concatenate([oz1_s, x0z1_s, x1z1_s], axis=0),
        ],
        axis=1,
    )
    far_degree = jnp.sum(jnp.where(far_lanes > 0, far_sums, 0.0), axis=0, keepdims=True)
    root = lax.rsqrt(own_degree + to_z(far_degree))

    across_shape = (columns, points)
    work = 2 * columns * size * size
    far_rows = call(
        far_rows_body, shaped(across_shape, F32), [SMEM] + [VMEM] * 8, "far_rows", 8 * work, 8 * work // 64
    )
    own_rows = call(
        own_rows_body,
        (shaped(across_shape, F32), shaped((columns, columns), F32)),
        [SMEM] + [VMEM] * 10, "own_rows", 12 * work, 12 * work // 64,
    )
    solve = call(
        functools.partial(solve_body, math.sqrt(total_rows)),
        (shaped(across_shape, F32), shaped(across_shape, BF16)),
        [VMEM] * 3, "solve", 4 * columns * columns * points, 4 * columns * points,
    )
    vectors = start_vectors.T
    scaled = (vectors * root).astype(BF16)
    for iteration in range(ITERS):
        x = from_x(scaled)
        z = from_z(scaled)
        given = to_z(far_rows(far_mask, scaled, x, oz0, oz1, x0z0, x1z0, x0z1, x1z1))
        image, gram = own_rows(own_mask, scaled, x, z, given, root, oo, x0o, x1o, oz0, oz1)
        vectors, scaled = solve(total_sum(gram), image, root)
    return vectors.T


def solution(mesh):
    in_specs = (P(("row", "col"), None), P(("row", "col"), None), P(("row", "col"), None))
    out_specs = P(("row", "col"), None)
    return jax.shard_map(
        on_device, mesh=mesh, in_specs=in_specs, out_specs=out_specs, check_vma=False
    )
```

time: 317 us -> 232 us (0.73)
  Pallas kernels: 0 us -> 77.9 us
  waiting for transfers between devices: 160 us -> 85.9 us
  matrix products: 40.2 us -> 0 us
  other arithmetic: 42.5 us -> 9.5 us
  starting transfers between devices: 61.5 us -> 48.7 us
  local copies, waits for them, and re-layouts: 12.4 us -> 9.16 us
    pallas_call x0 -> x14, Pallas kernels: none -> 77.9 us  [the longest x3 22.2 us: on_device(): vectors, scaled = solve(total_sum(gram), image, root)]
    ppermute x16 -> x15, waiting for transfers between devices: 131 us -> 59.3 us  [the longest x6 42.9 us: from_z(): lax.ppermute(value, 'col', [(side_of(i), i) for i in range(col_count)])]
    dot_general x11 -> x0, matrix products: 38.3 us -> none  [the longest x2 22 us: on_device(): lax.dot_general(own_blocks[member], point_rows, (((1,), (1,)), ((), ())),...]
    another operation x15 -> x0, other arithmetic: 36.2 us -> none  [the longest x9 19.6 us: orthonormal(): factor = jnp.linalg.cholesky(gram_sum)]
    ppermute x16 -> x15, starting transfers between devices: 37.5 us -> 24.9 us  [the longest x6 16.7 us: from_z(): lax.ppermute(value, 'col', [(side_of(i), i) for i in range(col_count)])]
    pallas_call x0 -> x4, other arithmetic: none -> 3.95 us  [the longest x2 2.65 us: on_device(): call(last_tiles_body, (half, line, tall, pair, line, tile, short, tile, s...]
    unnamed x33 -> x52, local copies, waits for them, and re-layouts: 10.3 us -> 7.09 us
  transfers between devices with their start and end apart: 37 -> 36, of which waited for: 29 -> 28; matrix products, arithmetic and copies ran while one was open for 4% -> 3% of each run, Pallas kernels for 0% -> 7%
where the time goes in v2:
time: 232 us; the launch traced here: 231 us
  waiting for transfers between devices  85.9 us (37%)
  Pallas kernels  77.9 us (34%)
  starting transfers between devices  48.7 us (21%)
  other arithmetic  9.5 us (4%)
  local copies, waits for them, and re-layouts  9.16 us (4%)
    ppermute x6, waiting for transfers between devices, from_z(): lax.ppermute(value, 'col', [(side_of(i), i) for i in range(col_count)])  42.9 us
    ppermute x21, waiting for transfers between devices, fetched(): return lax.ppermute(value, ('row', 'col'), pairs)  26.5 us
    ppermute x21, starting transfers between devices, fetched(): return lax.ppermute(value, ('row', 'col'), pairs)  23.8 us
    pallas_call x3, Pallas kernels, on_device(): vectors, scaled = solve(total_sum(gram), image, root)  22.2 us
    ppermute x6, starting transfers between devices, from_z(): lax.ppermute(value, 'col', [(side_of(i), i) for i in range(col_count)])  16.7 us
    pallas_call x3, Pallas kernels, on_device(): own_rows(own_mask, scaled, x, z, given, root, oo, x0o, x1o, oz0, oz1)  16.6 us
    ppermute x5, waiting for transfers between devices, from_x(): return lax.ppermute(value, 'col', [(i, i ^ 1) for i in range(col_count)])  11.6 us
    pallas_call x3, Pallas kernels, on_device(): far_rows(far_mask, scaled, x, oz0, oz1, x0z0, x1z0, x0z1, x1z1)  11.4 us
  transfers between devices with their start and end apart: 36, of which 28 were waited for; matrix products, arithmetic and copies ran while one was open for 3% of the time, Pallas kernels for 7%

profile of v2, /device:TPU:0, one launch (start us, length us, event | category | flops | bytes accessed | tf_op | source)
XLA Modules:
  0.0 231.5 jit_solution(7139588849736033260)
XLA Ops:
  0.0 3.8 %unit_rows.2.b0 = bf16[512,1024]{1,0:T(8,128)(2,1)} custom-call(f32[1024,1024]{1,0:T(8,128)} %points_ref.3), custom_call_target="tpu_custom_call" | custom-call | flops 1572864 | bytes 3145728 | tf_op jit(solution)/shard_map/unit_rows/pallas_call | solution.py:57
  3.8 3.0 %collective-permute-start = (bf16[512,1024]{1,0:T(8,128)(2,1)}, bf16[512,1024]{1,0:T(8,128)(2,1)S(1)}, u32[]{:S(2)}, u32[]{:S(2)}) collective-permute-start(bf16[512,1024]{1,0:T(8,128)(2,1)} %unit_rows.2.b0), channel_id=1, source_target_pairs={{0,1},{1,0},{2,3},{3,2},{4,5},{5,4},{6,7},{7,6},{8,9},{9,8},{10,11... | collective-permute-start | bytes 3145736 | tf_op jit(solution)/shard_map/ppermute | solution.py:237
  6.8 3.6 %collective-permute-start.1 = (bf16[512,1024]{1,0:T(8,128)(2,1)}, bf16[512,1024]{1,0:T(8,128)(2,1)S(1)}, u32[]{:S(2)}, u32[]{:S(2)}) collective-permute-start(bf16[512,1024]{1,0:T(8,128)(2,1)} %unit_rows.2.b0), channel_id=1, source_target_pairs={{2,0},{7,1},{4,2},{1,3},{6,4},{3,5},{0,6},{5,7},{10,8},{15,9},{12,... | collective-permute-start | bytes 3145736 | tf_op jit(solution)/shard_map/ppermute | solution.py:240
  10.4 3.8 %unit_rows.3.b1 = bf16[512,1024]{1,0:T(8,128)(2,1)} custom-call(f32[1024,1024]{1,0:T(8,128)} %points_ref.3), custom_call_target="tpu_custom_call" | custom-call | flops 1572864 | bytes 3145728 | tf_op jit(solution)/shard_map/unit_rows/pallas_call | solution.py:57
  14.7 2.0 collective-permute-start.4
  16.9 5.6 %own_tiles.1 = (bf16[1024,1024]{1,0:T(8,128)(2,1)}, f32[2,1024]{1,0:T(2,128)}) custom-call(bf16[512,1024]{1,0:T(8,128)(2,1)} %unit_rows.2.b0, bf16[512,1024]{1,0:T(8,128)(2,1)} %unit_rows.3.b1), custom_call_target="tpu_custom_call" | custom-call | flops 2147483648 | bytes 8388608 | tf_op jit(solution)/shard_map/own_tiles/pallas_call | solution.py:271
  23.5 31.8 %collective-permute-done.4 = s32[2,12]{1,0:T(2,128)S(1)} collective-permute-done((s32[2,12]{1,0:T(2,128)S(1)}, s32[2,12]{1,0:T(2,128)S(1)}, u32[]{:S(2)}, u32[]{:S(2)}) %collective-permute-start.4) | collective-permute-done | bytes 128 | tf_op jit(solution)/shard_map/ppermute | solution.py:240
  57.4 6.4 %first_tiles.1 = (bf16[512,1024]{1,0:T(8,128)(2,1)}, f32[1,1024]{1,0:T(1,128)}, bf16[1024,512]{1,0:T(8,128)(2,1)}, f32[2,512]{1,0:T(2,128)}, f32[1,1024]{1,0:T(1...) custom-call(bf16[512,1024]{1,0:T(8,128)(2,1)} %unit_rows.2.b0, bf16[512,1024]{1,0:T(8,128)(2,1)} %unit_rows.3.b1, ...), custom_call_target="tpu_custom_call" | custom-call | flops 2684354560 | bytes 10485760 | tf_op jit(solution)/shard_map/first_tiles/pallas_call | solution.py:274
  64.9 8.2 %last_tiles.1 = (bf16[512,1024]{1,0:T(8,128)(2,1)}, f32[1,1024]{1,0:T(1,128)}, bf16[1024,512]{1,0:T(8,128)(2,1)}, f32[2,512]{1,0:T(2,128)}, f32[1,1024]{1,0:T(1,...) custom-call(bf16[512,1024]{1,0:T(8,128)(2,1)} %unit_rows.2.b0, ...), custom_call_target="tpu_custom_call" | custom-call | flops 3758096384 | bytes 14680064 | tf_op jit(solution)/shard_map/last_tiles/pallas_call | solution.py:279
  79.9 1.9 collective-permute-start.6
  81.9 3.1 %collective-permute-done.6.x = bf16[64,1024]{1,0:T(8,128)(2,1)S(1)} collective-permute-done((bf16[64,1024]{1,0:T(8,128)(2,1)S(1)}, bf16[64,1024]{1,0:T(8,128)(2,1)S(1)}, u32[]{:S(2)}, u32[]{:S(2)}) %collective-permute-start.6) | collective-permute-done | bytes 131104 | tf_op jit(solution)/shard_map/ppermute | solution.py:237
  85.6 3.8 %far_rows.3 = f32[64,1024]{1,0:T(8,128)} custom-call(f32[2,4]{1,0:T(2,128)} %copy-done.14, bf16[64,1024]{1,0:T(8,128)(2,1)} %copy-done, bf16[64,1024]{1,0:T(8,128)(2,1)} %copy-done.4, bf16[1024,512]{1,0:T(8,128)(2,1)} %get-tuple-element.45.oz0, bf16[1024,512]{1,0:T(8,128)(2,1)} %get-tuple-element.46.oz1, bf16[512,512]{1,0:T(8,128)(2,1)} %get-tuple-element.47.x0z0, ...), custom_call_target="tpu_custom_call" | custom-call | flops 268435456 | bytes 4194304 | tf_op jit(solution)/shard_map/far_rows/pallas_call | solution.py:319
  90.3 2.9 %collective-permute-start.7 = (bf16[64,1024]{1,0:T(8,128)(2,1)}, bf16[64,1024]{1,0:T(8,128)(2,1)S(1)}, u32[]{:S(2)}, u32[]{:S(2)}) collective-permute-start(bf16[64,1024]{1,0:T(8,128)(2,1)} %copy-done), channel_id=1, source_target_pairs={{2,0},{7,1},{4,2},{1,3},{6,4},{3,5},{0,6},{5,7},{10,8},{15,9},{12,... | collective-permute-start | bytes 393224 | tf_op jit(solution)/shard_map/ppermute | solution.py:240
  93.8 6.0 %collective-permute-done.7.z = bf16[64,1024]{1,0:T(8,128)(2,1)S(1)} collective-permute-done((bf16[64,1024]{1,0:T(8,128)(2,1)}, bf16[64,1024]{1,0:T(8,128)(2,1)S(1)}, u32[]{:S(2)}, u32[]{:S(2)}) %collective-permute-start.7) | collective-permute-done | bytes 131104 | tf_op jit(solution)/shard_map/ppermute | solution.py:240
  100.6 5.5 %own_rows.3 = (f32[64,1024]{1,0:T(8,128)}, f32[64,64]{1,0:T(8,128)}) custom-call(f32[2,6]{1,0:T(2,128)} %copy.8.mask, bf16[64,1024]{1,0:T(8,128)(2,1)} %copy-done, bf16[64,1024]{1,0:T(8,128)(2,1)} %copy-done.4, bf16[64,1024]{1,0:T(8,128)(2,1)} %copy-done.12, f32[64,1024]{1,0:T(8,128)} %copy-done.8, f32[1,1024]{1,0:T(1,128)} %copy-done.6, ...), custom_call_target="tpu_custom_call" | custom-call | flops 402653184 | bytes 6291456 | tf_op jit(solution)/shard_map/own_rows/pallas_call | solution.py:320
  106.1 1.4 collective-permute-done.9
  108.3 1.5 collective-permute-start.10
  109.8 1.5 collective-permute-start.11
  112.2 1.8 collective-permute-done.11
  114.0 2.1 collective-permute-done.12
  116.6 2.0 collective-permute-start.14
  118.5 2.1 collective-permute-start.15
  121.5 2.7 %collective-permute-done.15 = f32[64,64]{1,0:T(8,128)S(1)} collective-permute-done((f32[64,64]{1,0:T(8,128)S(1)}, f32[64,64]{1,0:T(8,128)S(1)}, u32[]{:S(2)}, u32[]{:S(2)}) %collective-permute-start.15) | collective-permute-done | bytes 16416 | tf_op jit(solution)/shard_map/ppermute | solution.py:212
  124.8 7.4 %solve.3 = (f32[64,1024]{1,0:T(8,128)}, bf16[64,1024]{1,0:T(8,128)(2,1)}) custom-call(f32[64,64]{1,0:T(8,128)} %add_add_fusion.4.gram, f32[64,1024]{1,0:T(8,128)} %get-tuple-element.55.image, f32[1,1024]{1,0:T(1,128)} %copy-done.6), custom_call_target="tpu_custom_call" | custom-call | flops 16777216 | bytes 262144 | tf_op jit(solution)/shard_map/solve/pallas_call | solution.py:321
  132.5 4.9 %collective-permute-done.16.x = bf16[64,1024]{1,0:T(8,128)(2,1)S(1)} collective-permute-done((bf16[64,1024]{1,0:T(8,128)(2,1)}, bf16[64,1024]{1,0:T(8,128)(2,1)S(1)}, u32[]{:S(2)}, u32[]{:S(2)}) %collective-permute-start.16) | collective-permute-done | bytes 131104 | tf_op jit(solution)/shard_map/ppermute | solution.py:237
  138.1 3.8 %far_rows.4 = f32[64,1024]{1,0:T(8,128)} custom-call(f32[2,4]{1,0:T(2,128)} %copy-done.14, bf16[64,1024]{1,0:T(8,128)(2,1)} %get-tuple-element.56.own, bf16[64,1024]{1,0:T(8,128)(2,1)} %copy-done.5, bf16[1024,512]{1,0:T(8,128)(2,1)} %get-tuple-element.45.oz0, bf16[1024,512]{1,0:T(8,128)(2,1)} %get-tuple-element.46.oz1, ...), custom_call_target="tpu_custom_call" | custom-call | flops 268435456 | bytes 4194304 | tf_op jit(solution)/shard_map/far_rows/pallas_call | solution.py:319
  141.9 3.8 %collective-permute-start.17 = (bf16[64,1024]{1,0:T(8,128)(2,1)S(1)}, bf16[64,1024]{1,0:T(8,128)(2,1)S(1)}, u32[]{:S(2)}, u32[]{:S(2)}) collective-permute-start(bf16[64,1024]{1,0:T(8,128)(2,1)S(1)} %copy-done.3), channel_id=1, source_target_pairs={{2,0},{7,1},{4,2},{1,3},{6,4},{3,5},{0,6},{5,7},{10,8},{15,9},{12,... | collective-permute-start | bytes 393224 | tf_op jit(solution)/shard_map/ppermute | solution.py:240
  145.7 2.5 %collective-permute-done.17.z = bf16[64,1024]{1,0:T(8,128)(2,1)S(1)} collective-permute-done((bf16[64,1024]{1,0:T(8,128)(2,1)S(1)}, bf16[64,1024]{1,0:T(8,128)(2,1)S(1)}, u32[]{:S(2)}, u32[]{:S(2)}) %collective-permute-start.17) | collective-permute-done | bytes 131104 | tf_op jit(solution)/shard_map/ppermute | solution.py:240
  148.2 2.1 collective-permute-done.18.given
  151.0 5.5 %own_rows.4 = (f32[64,1024]{1,0:T(8,128)}, f32[64,64]{1,0:T(8,128)}) custom-call(f32[2,6]{1,0:T(2,128)} %copy.8.mask, bf16[64,1024]{1,0:T(8,128)(2,1)} %get-tuple-element.56.own, bf16[64,1024]{1,0:T(8,128)(2,1)} %copy-done.5, bf16[64,1024]{1,0:T(8,128)(2,1)} %copy-done.13, f32[64,1024]{1,0:T(8,128)} %copy-done.9, f32[1,1024]{1,0:T(1,128)} %copy-done.6, ...), custom_call_target="tpu_custom_call" | custom-call | flops 402653184 | bytes 6291456 | tf_op jit(solution)/shard_map/own_rows/pallas_call | solution.py:320
  159.2 1.6 collective-permute-start.21
  163.1 2.5 %collective-permute-done.22 = f32[64,64]{1,0:T(8,128)S(1)} collective-permute-done((f32[64,64]{1,0:T(8,128)S(1)}, f32[64,64]{1,0:T(8,128)S(1)}, u32[]{:S(2)}, u32[]{:S(2)}) %collective-permute-start.22) | collective-permute-done | bytes 16416 | tf_op jit(solution)/shard_map/ppermute | solution.py:212
  167.9 2.2 collective-permute-start.25
  170.1 1.6 collective-permute-done.24
  171.8 1.9 collective-permute-done.25
  174.2 7.4 %solve.4 = (f32[64,1024]{1,0:T(8,128)}, bf16[64,1024]{1,0:T(8,128)(2,1)}) custom-call(f32[64,64]{1,0:T(8,128)} %add_add_fusion.2.gram, f32[64,1024]{1,0:T(8,128)} %get-tuple-element.58.image, f32[1,1024]{1,0:T(1,128)} %copy-done.6), custom_call_target="tpu_custom_call" | custom-call | flops 16777216 | bytes 262144 | tf_op jit(solution)/shard_map/solve/pallas_call | solution.py:321
  181.6 1.6 collective-permute-start.26
  183.2 3.6 %collective-permute-done.26.x = bf16[64,1024]{1,0:T(8,128)(2,1)S(1)} collective-permute-done((bf16[64,1024]{1,0:T(8,128)(2,1)}, bf16[64,1024]{1,0:T(8,128)(2,1)S(1)}, u32[]{:S(2)}, u32[]{:S(2)}) %collective-permute-start.26) | collective-permute-done | bytes 131104 | tf_op jit(solution)/shard_map/ppermute | solution.py:237
  187.5 3.8 %far_rows.5 = f32[64,1024]{1,0:T(8,128)} custom-call(f32[2,4]{1,0:T(2,128)} %copy-done.14, bf16[64,1024]{1,0:T(8,128)(2,1)} %get-tuple-element.59.own, bf16[64,1024]{1,0:T(8,128)(2,1)} %copy-done.2, bf16[1024,512]{1,0:T(8,128)(2,1)} %get-tuple-element.45.oz0, bf16[1024,512]{1,0:T(8,128)(2,1)} %get-tuple-element.46.oz1, ...), custom_call_target="tpu_custom_call" | custom-call | flops 268435456 | bytes 4194304 | tf_op jit(solution)/shard_map/far_rows/pallas_call | solution.py:319
  191.3 3.8 %collective-permute-start.27 = (bf16[64,1024]{1,0:T(8,128)(2,1)S(1)}, bf16[64,1024]{1,0:T(8,128)(2,1)S(1)}, u32[]{:S(2)}, u32[]{:S(2)}) collective-permute-start(bf16[64,1024]{1,0:T(8,128)(2,1)S(1)} %copy-done.1), channel_id=1, source_target_pairs={{2,0},{7,1},{4,2},{1,3},{6,4},{3,5},{0,6},{5,7},{10,8},{15,9},{12,... | collective-permute-start | bytes 393224 | tf_op jit(solution)/shard_map/ppermute | solution.py:240
  195.1 2.5 %collective-permute-done.27.z = bf16[64,1024]{1,0:T(8,128)(2,1)S(1)} collective-permute-done((bf16[64,1024]{1,0:T(8,128)(2,1)S(1)}, bf16[64,1024]{1,0:T(8,128)(2,1)S(1)}, u32[]{:S(2)}, u32[]{:S(2)}) %collective-permute-start.27) | collective-permute-done | bytes 131104 | tf_op jit(solution)/shard_map/ppermute | solution.py:240
  197.6 2.1 collective-permute-done.28.given
  200.5 5.5 %own_rows.5 = (f32[64,1024]{1,0:T(8,128)}, f32[64,64]{1,0:T(8,128)}) custom-call(f32[2,6]{1,0:T(2,128)} %copy.8.mask, bf16[64,1024]{1,0:T(8,128)(2,1)} %get-tuple-element.59.own, bf16[64,1024]{1,0:T(8,128)(2,1)} %copy-done.2, bf16[64,1024]{1,0:T(8,128)(2,1)} %copy-done.11, f32[64,1024]{1,0:T(8,128)} %copy-done.7, f32[1,1024]{1,0:T(1,128)} %copy-done.6, ...), custom_call_target="tpu_custom_call" | custom-call | flops 402653184 | bytes 6291456 | tf_op jit(solution)/shard_map/own_rows/pallas_call | solution.py:320
  209.3 2.0 collective-permute-start.31
  213.3 2.9 %collective-permute-done.32 = f32[64,64]{1,0:T(8,128)S(1)} collective-permute-done((f32[64,64]{1,0:T(8,128)S(1)}, f32[64,64]{1,0:T(8,128)S(1)}, u32[]{:S(2)}, u32[]{:S(2)}) %collective-permute-start.32) | collective-permute-done | bytes 16416 | tf_op jit(solution)/shard_map/ppermute | solution.py:212
  217.8 2.9 %collective-permute-start.35 = (f32[64,64]{1,0:T(8,128)S(1)}, f32[64,64]{1,0:T(8,128)S(1)}, u32[]{:S(2)}, u32[]{:S(2)}) collective-permute-start(f32[64,64]{1,0:T(8,128)S(1)} %add_add_fusion.1), channel_id=1, source_target_pairs={{0,6},{1,7},{2,4},{3,5},{4,2},{5,3},{6,0},{7,1},{8,14},{9,15},{10,... | collective-permute-start | bytes 49160 | tf_op jit(solution)/shard_map/ppermute | solution.py:212
  220.6 1.6 collective-permute-done.34
  224.1 7.4 %solve.5 = (f32[64,1024]{1,0:T(8,128)}, bf16[64,1024]{1,0:T(8,128)(2,1)}) custom-call(f32[64,64]{1,0:T(8,128)} %add_add_fusion.gram, f32[64,1024]{1,0:T(8,128)} %get-tuple-element.61.image, f32[1,1024]{1,0:T(1,128)} %copy-done.6), custom_call_target="tpu_custom_call" | custom-call | flops 16777216 | bytes 262144 | tf_op jit(solution)/shard_map/solve/pallas_call | solution.py:321
  (125 shorter events, 37.6 us)
Async XLA Ops:
  0.0 14.7 %copy-start.19 = (s32[2,12]{1,0:T(2,128)S(1)}, s32[2,12]{1,0:T(2,128)}, u32[]{:S(2)}) copy-start(s32[2,12]{1,0:T(2,128)} %param.4) | copy-start | bytes 292
  3.8 51.7 %collective-permute-start = (bf16[512,1024]{1,0:T(8,128)(2,1)}, bf16[512,1024]{1,0:T(8,128)(2,1)S(1)}, u32[]{:S(2)}, u32[]{:S(2)}) collective-permute-start(bf16[512,1024]{1,0:T(8,128)(2,1)} %unit_rows.2.b0), channel_id=1, source_target_pairs={{0,1},{1,0},{2,3},{3,2},{4,5},{5,4},{6,7},{7,6},{8,9},{9,8},{10,11... | collective-permute-start | bytes 3145736 | tf_op jit(solution)/shard_map/ppermute | solution.py:237
  6.8 48.7 %collective-permute-start.1 = (bf16[512,1024]{1,0:T(8,128)(2,1)}, bf16[512,1024]{1,0:T(8,128)(2,1)S(1)}, u32[]{:S(2)}, u32[]{:S(2)}) collective-permute-start(bf16[512,1024]{1,0:T(8,128)(2,1)} %unit_rows.2.b0), channel_id=1, source_target_pairs={{2,0},{7,1},{4,2},{1,3},{6,4},{3,5},{0,6},{5,7},{10,8},{15,9},{12,... | collective-permute-start | bytes 3145736 | tf_op jit(solution)/shard_map/ppermute | solution.py:240
  14.2 49.7 %collective-permute-start.2 = (bf16[512,1024]{1,0:T(8,128)(2,1)}, bf16[512,1024]{1,0:T(8,128)(2,1)S(1)}, u32[]{:S(2)}, u32[]{:S(2)}) collective-permute-start(bf16[512,1024]{1,0:T(8,128)(2,1)} %unit_rows.3.b1), channel_id=1, source_target_pairs={{0,1},{1,0},{2,3},{3,2},{4,5},{5,4},{6,7},{7,6},{8,9},{9,8},{10,11... | collective-permute-start | bytes 3145736 | tf_op jit(solution)/shard_map/ppermute | solution.py:237
  14.2 49.7 %collective-permute-start.3 = (bf16[512,1024]{1,0:T(8,128)(2,1)}, bf16[512,1024]{1,0:T(8,128)(2,1)}, u32[]{:S(2)}, u32[]{:S(2)}) collective-permute-start(bf16[512,1024]{1,0:T(8,128)(2,1)} %unit_rows.3.b1), channel_id=1, source_target_pairs={{2,0},{7,1},{4,2},{1,3},{6,4},{3,5},{0,6},{5,7},{10,8},{15,9},{12,... | collective-permute-start | bytes 3145736 | tf_op jit(solution)/shard_map/ppermute | solution.py:240
  14.7 40.6 %collective-permute-start.4 = (s32[2,12]{1,0:T(2,128)S(1)}, s32[2,12]{1,0:T(2,128)S(1)}, u32[]{:S(2)}, u32[]{:S(2)}) collective-permute-start(s32[2,12]{1,0:T(2,128)S(1)} %copy-done.19), channel_id=1, source_target_pairs={{2,0},{7,1},{4,2},{1,3},{6,4},{3,5},{0,6},{5,7},{10,8},{15,9},{12,... | collective-permute-start | bytes 296 | tf_op jit(solution)/shard_map/ppermute | solution.py:240
  55.5 8.4 %copy-start.14 = (f32[2,4]{1,0:T(2,128)}, f32[2,4]{1,0:T(2,128)S(1)}, u32[]{:S(2)}) copy-start(f32[2,4]{1,0:T(2,128)S(1)} %convert_reduce_fusion.mask) | copy-start | bytes 100
  63.8 9.3 %copy-start.17 = (f32[2,512]{1,0:T(2,128)S(1)}, f32[2,512]{1,0:T(2,128)}, u32[]{:S(2)}) copy-start(f32[2,512]{1,0:T(2,128)} %get-tuple-element.39) | copy-start | bytes 12292
  63.8 9.3 %copy-start.18 = (f32[1,512]{1,0:T(1,128)S(1)}, f32[1,512]{1,0:T(1,128)}, u32[]{:S(2)}) copy-start(f32[1,512]{1,0:T(1,128)} %get-tuple-element.40) | copy-start | bytes 6148
  63.8 12.5 %copy-start.16 = (f32[1,1024]{1,0:T(1,128)S(1)}, f32[1,1024]{1,0:T(1,128)}, u32[]{:S(2)}) copy-start(f32[1,1024]{1,0:T(1,128)} %get-tuple-element.35) | copy-start | bytes 12292
  63.8 13.1 %copy-start.15 = (f32[1,1024]{1,0:T(1,128)S(1)}, f32[1,1024]{1,0:T(1,128)}, u32[]{:S(2)}) copy-start(f32[1,1024]{1,0:T(1,128)} %get-tuple-element.37) | copy-start | bytes 12292
  63.9 16.0 %copy-start.10 = (f32[1024,64]{0,1:T(8,128)S(1)}, f32[1024,64]{0,1:T(8,128)}, u32[]{:S(2)}) copy-start(f32[1024,64]{0,1:T(8,128)} %param.5) | copy-start | bytes 786436
  73.9 5.9 %collective-permute-start.5 = (f32[1,1024]{1,0:T(1,128)S(1)}, f32[1,1024]{1,0:T(1,128)S(1)}, u32[]{:S(2)}, u32[]{:S(2)}) collective-permute-start(f32[1,1024]{1,0:T(1,128)S(1)} %bitcast.25), channel_id=1, source_target_pairs={{0,2},{1,7},{2,4},{3,1},{4,6},{5,3},{6,0},{7,5},{8,10},{9,15},{10,... | collective-permute-start | bytes 12296 | tf_op jit(solution)/shard_map/ppermute | solution.py:243
  79.8 20.0 %copy-start.6 = (f32[1,1024]{1,0:T(1,128)}, f32[1,1024]{1,0:T(1,128)S(1)}, u32[]{:S(2)}) copy-start(f32[1,1024]{1,0:T(1,128)S(1)} %add_rsqrt_fusion.root) | copy-start | bytes 12292
  79.9 5.0 %copy-start = (bf16[64,1024]{1,0:T(8,128)(2,1)}, bf16[64,1024]{1,0:T(8,128)(2,1)S(1)}, u32[]{:S(2)}) copy-start(bf16[64,1024]{1,0:T(8,128)(2,1)S(1)} %fusion.own) | copy-start | bytes 393220
  79.9 5.0 %collective-permute-start.6 = (bf16[64,1024]{1,0:T(8,128)(2,1)S(1)}, bf16[64,1024]{1,0:T(8,128)(2,1)S(1)}, u32[]{:S(2)}, u32[]{:S(2)}) collective-permute-start(bf16[64,1024]{1,0:T(8,128)(2,1)S(1)} %fusion.own), channel_id=1, source_target_pairs={{0,1},{1,0},{2,3},{3,2},{4,5},{5,4},{6,7},{7,6},{8,9},{9,8},{10,11... | collective-permute-start | bytes 393224 | tf_op jit(solution)/shard_map/ppermute | solution.py:237
  89.4 10.5 %collective-permute-start.8 = (f32[64,1024]{1,0:T(8,128)}, f32[64,1024]{1,0:T(8,128)S(1)}, u32[]{:S(2)}, u32[]{:S(2)}) collective-permute-start(f32[64,1024]{1,0:T(8,128)} %far_rows.3), channel_id=1, source_target_pairs={{0,2},{1,7},{2,4},{3,1},{4,6},{5,3},{6,0},{7,5},{8,10},{9,15},{10,... | collective-permute-start | bytes 786440 | tf_op jit(solution)/shard_map/ppermute | solution.py:243
  90.3 9.5 %collective-permute-start.7 = (bf16[64,1024]{1,0:T(8,128)(2,1)}, bf16[64,1024]{1,0:T(8,128)(2,1)S(1)}, u32[]{:S(2)}, u32[]{:S(2)}) collective-permute-start(bf16[64,1024]{1,0:T(8,128)(2,1)} %copy-done), channel_id=1, source_target_pairs={{2,0},{7,1},{4,2},{1,3},{6,4},{3,5},{0,6},{5,7},{10,8},{15,9},{12,... | collective-permute-start | bytes 393224 | tf_op jit(solution)/shard_map/ppermute | solution.py:240
  106.1 1.4 collective-permute-start.9
  108.3 3.9 %collective-permute-start.10 = (f32[64,64]{1,0:T(8,128)S(1)}, f32[64,64]{1,0:T(8,128)S(1)}, u32[]{:S(2)}, u32[]{:S(2)}) collective-permute-start(f32[64,64]{1,0:T(8,128)S(1)} %add.116), channel_id=1, source_target_pairs={{0,16},{1,17},{2,18},{3,19},{4,20},{5,21},{6,22},{7,23},{8,24},{9,... | collective-permute-start | bytes 49160 | tf_op jit(solution)/shard_map/ppermute | solution.py:212
  109.8 4.2 %collective-permute-start.11 = (f32[64,64]{1,0:T(8,128)S(1)}, f32[64,64]{1,0:T(8,128)S(1)}, u32[]{:S(2)}, u32[]{:S(2)}) collective-permute-start(f32[64,64]{1,0:T(8,128)S(1)} %add.116), channel_id=1, source_target_pairs={{0,1},{1,0},{2,3},{3,2},{4,5},{5,4},{6,7},{7,6},{8,9},{9,8},{10,11... | collective-permute-start | bytes 49160 | tf_op jit(solution)/shard_map/ppermute | solution.py:212
  111.3 4.8 %collective-permute-start.12 = (f32[64,64]{1,0:T(8,128)S(1)}, f32[64,64]{1,0:T(8,128)S(1)}, u32[]{:S(2)}, u32[]{:S(2)}) collective-permute-start(f32[64,64]{1,0:T(8,128)S(1)} %add.116), channel_id=1, source_target_pairs={{0,17},{1,16},{2,19},{3,18},{4,21},{5,20},{6,23},{7,22},{8,25},{9,... | collective-permute-start | bytes 49160 | tf_op jit(solution)/shard_map/ppermute | solution.py:212
  116.2 4.5 %collective-permute-start.13 = (f32[64,64]{1,0:T(8,128)S(1)}, f32[64,64]{1,0:T(8,128)S(1)}, u32[]{:S(2)}, u32[]{:S(2)}) collective-permute-start(f32[64,64]{1,0:T(8,128)S(1)} %add_add_fusion.5), channel_id=1, source_target_pairs={{0,2},{1,3},{2,0},{3,1},{4,6},{5,7},{6,4},{7,5},{8,10},{9,11},{10,... | collective-permute-start | bytes 49160 | tf_op jit(solution)/shard_map/ppermute | solution.py:212
  116.6 5.0 %collective-permute-start.14 = (f32[64,64]{1,0:T(8,128)S(1)}, f32[64,64]{1,0:T(8,128)S(1)}, u32[]{:S(2)}, u32[]{:S(2)}) collective-permute-start(f32[64,64]{1,0:T(8,128)S(1)} %add_add_fusion.5), channel_id=1, source_target_pairs={{0,4},{1,5},{2,6},{3,7},{4,0},{5,1},{6,2},{7,3},{8,12},{9,13},{10,... | collective-permute-start | bytes 49160 | tf_op jit(solution)/shard_map/ppermute | solution.py:212
  118.5 5.7 %collective-permute-start.15 = (f32[64,64]{1,0:T(8,128)S(1)}, f32[64,64]{1,0:T(8,128)S(1)}, u32[]{:S(2)}, u32[]{:S(2)}) collective-permute-start(f32[64,64]{1,0:T(8,128)S(1)} %add_add_fusion.5), channel_id=1, source_target_pairs={{0,6},{1,7},{2,4},{3,5},{4,2},{5,3},{6,0},{7,1},{8,14},{9,15},{10,... | collective-permute-start | bytes 49160 | tf_op jit(solution)/shard_map/ppermute | solution.py:212
  132.2 9.6 %copy-start.3 = (bf16[64,1024]{1,0:T(8,128)(2,1)S(1)}, bf16[64,1024]{1,0:T(8,128)(2,1)}, u32[]{:S(2)}) copy-start(bf16[64,1024]{1,0:T(8,128)(2,1)} %get-tuple-element.56.own) | copy-start | bytes 393220
  132.2 5.2 %collective-permute-start.16 = (bf16[64,1024]{1,0:T(8,128)(2,1)}, bf16[64,1024]{1,0:T(8,128)(2,1)S(1)}, u32[]{:S(2)}, u32[]{:S(2)}) collective-permute-start(bf16[64,1024]{1,0:T(8,128)(2,1)} %get-tuple-element.56.own), channel_id=1, source_target_pairs={{0,1},{1,0},{2,3},{3,2},{4,5},{5,4},{6,7},{7,6},{8,9},{9,8},{10,11... | collective-permute-start | bytes 393224 | tf_op jit(solution)/shard_map/ppermute | solution.py:237
  141.9 8.4 %collective-permute-start.18 = (f32[64,1024]{1,0:T(8,128)}, f32[64,1024]{1,0:T(8,128)S(1)}, u32[]{:S(2)}, u32[]{:S(2)}) collective-permute-start(f32[64,1024]{1,0:T(8,128)} %far_rows.4), channel_id=1, source_target_pairs={{0,2},{1,7},{2,4},{3,1},{4,6},{5,3},{6,0},{7,5},{8,10},{9,15},{10,... | collective-permute-start | bytes 786440 | tf_op jit(solution)/shard_map/ppermute | solution.py:243
  141.9 6.3 %collective-permute-start.17 = (bf16[64,1024]{1,0:T(8,128)(2,1)S(1)}, bf16[64,1024]{1,0:T(8,128)(2,1)S(1)}, u32[]{:S(2)}, u32[]{:S(2)}) collective-permute-start(bf16[64,1024]{1,0:T(8,128)(2,1)S(1)} %copy-done.3), channel_id=1, source_target_pairs={{2,0},{7,1},{4,2},{1,3},{6,4},{3,5},{0,6},{5,7},{10,8},{15,9},{12,... | collective-permute-start | bytes 393224 | tf_op jit(solution)/shard_map/ppermute | solution.py:240
  156.5 1.4 collective-permute-start.19
  158.7 3.9 %collective-permute-start.20 = (f32[64,64]{1,0:T(8,128)S(1)}, f32[64,64]{1,0:T(8,128)S(1)}, u32[]{:S(2)}, u32[]{:S(2)}) collective-permute-start(f32[64,64]{1,0:T(8,128)S(1)} %add.123), channel_id=1, source_target_pairs={{0,16},{1,17},{2,18},{3,19},{4,20},{5,21},{6,22},{7,23},{8,24},{9,... | collective-permute-start | bytes 49160 | tf_op jit(solution)/shard_map/ppermute | solution.py:212
  159.2 3.9 %collective-permute-start.21 = (f32[64,64]{1,0:T(8,128)S(1)}, f32[64,64]{1,0:T(8,128)S(1)}, u32[]{:S(2)}, u32[]{:S(2)}) collective-permute-start(f32[64,64]{1,0:T(8,128)S(1)} %add.123), channel_id=1, source_target_pairs={{0,1},{1,0},{2,3},{3,2},{4,5},{5,4},{6,7},{7,6},{8,9},{9,8},{10,11... | collective-permute-start | bytes 49160 | tf_op jit(solution)/shard_map/ppermute | solution.py:212
  160.8 4.8 %collective-permute-start.22 = (f32[64,64]{1,0:T(8,128)S(1)}, f32[64,64]{1,0:T(8,128)S(1)}, u32[]{:S(2)}, u32[]{:S(2)}) collective-permute-start(f32[64,64]{1,0:T(8,128)S(1)} %add.123), channel_id=1, source_target_pairs={{0,17},{1,16},{2,19},{3,18},{4,21},{5,20},{6,23},{7,22},{8,25},{9,... | collective-permute-start | bytes 49160 | tf_op jit(solution)/shard_map/ppermute | solution.py:212
  165.7 4.5 %collective-permute-start.23 = (f32[64,64]{1,0:T(8,128)S(1)}, f32[64,64]{1,0:T(8,128)S(1)}, u32[]{:S(2)}, u32[]{:S(2)}) collective-permute-start(f32[64,64]{1,0:T(8,128)S(1)} %add_add_fusion.3), channel_id=1, source_target_pairs={{0,2},{1,3},{2,0},{3,1},{4,6},{5,7},{6,4},{7,5},{8,10},{9,11},{10,... | collective-permute-start | bytes 49160 | tf_op jit(solution)/shard_map/ppermute | solution.py:212
  166.9 4.8 %collective-permute-start.24 = (f32[64,64]{1,0:T(8,128)S(1)}, f32[64,64]{1,0:T(8,128)S(1)}, u32[]{:S(2)}, u32[]{:S(2)}) collective-permute-start(f32[64,64]{1,0:T(8,128)S(1)} %add_add_fusion.3), channel_id=1, source_target_pairs={{0,4},{1,5},{2,6},{3,7},{4,0},{5,1},{6,2},{7,3},{8,12},{9,13},{10,... | collective-permute-start | bytes 49160 | tf_op jit(solution)/shard_map/ppermute | solution.py:212
  167.9 5.7 %collective-permute-start.25 = (f32[64,64]{1,0:T(8,128)S(1)}, f32[64,64]{1,0:T(8,128)S(1)}, u32[]{:S(2)}, u32[]{:S(2)}) collective-permute-start(f32[64,64]{1,0:T(8,128)S(1)} %add_add_fusion.3), channel_id=1, source_target_pairs={{0,6},{1,7},{2,4},{3,5},{4,2},{5,3},{6,0},{7,1},{8,14},{9,15},{10,... | collective-permute-start | bytes 49160 | tf_op jit(solution)/shard_map/ppermute | solution.py:212
  181.6 9.6 %copy-start.1 = (bf16[64,1024]{1,0:T(8,128)(2,1)S(1)}, bf16[64,1024]{1,0:T(8,128)(2,1)}, u32[]{:S(2)}) copy-start(bf16[64,1024]{1,0:T(8,128)(2,1)} %get-tuple-element.59.own) | copy-start | bytes 393220
  181.6 5.2 %collective-permute-start.26 = (bf16[64,1024]{1,0:T(8,128)(2,1)}, bf16[64,1024]{1,0:T(8,128)(2,1)S(1)}, u32[]{:S(2)}, u32[]{:S(2)}) collective-permute-start(bf16[64,1024]{1,0:T(8,128)(2,1)} %get-tuple-element.59.own), channel_id=1, source_target_pairs={{0,1},{1,0},{2,3},{3,2},{4,5},{5,4},{6,7},{7,6},{8,9},{9,8},{10,11... | collective-permute-start | bytes 393224 | tf_op jit(solution)/shard_map/ppermute | solution.py:237
  191.3 8.5 %collective-permute-start.28 = (f32[64,1024]{1,0:T(8,128)}, f32[64,1024]{1,0:T(8,128)S(1)}, u32[]{:S(2)}, u32[]{:S(2)}) collective-permute-start(f32[64,1024]{1,0:T(8,128)} %far_rows.5), channel_id=1, source_target_pairs={{0,2},{1,7},{2,4},{3,1},{4,6},{5,3},{6,0},{7,5},{8,10},{9,15},{10,... | collective-permute-start | bytes 786440 | tf_op jit(solution)/shard_map/ppermute | solution.py:243
  191.3 6.3 %collective-permute-start.27 = (bf16[64,1024]{1,0:T(8,128)(2,1)S(1)}, bf16[64,1024]{1,0:T(8,128)(2,1)S(1)}, u32[]{:S(2)}, u32[]{:S(2)}) collective-permute-start(bf16[64,1024]{1,0:T(8,128)(2,1)S(1)} %copy-done.1), channel_id=1, source_target_pairs={{2,0},{7,1},{4,2},{1,3},{6,4},{3,5},{0,6},{5,7},{10,8},{15,9},{12,... | collective-permute-start | bytes 393224 | tf_op jit(solution)/shard_map/ppermute | solution.py:240
  197.6 2.1 copy-start.11
  206.0 1.4 collective-permute-start.29
  208.2 3.9 %collective-permute-start.30 = (f32[64,64]{1,0:T(8,128)S(1)}, f32[64,64]{1,0:T(8,128)S(1)}, u32[]{:S(2)}, u32[]{:S(2)}) collective-permute-start(f32[64,64]{1,0:T(8,128)S(1)} %add.130), channel_id=1, source_target_pairs={{0,16},{1,17},{2,18},{3,19},{4,20},{5,21},{6,22},{7,23},{8,24},{9,... | collective-permute-start | bytes 49160 | tf_op jit(solution)/shard_map/ppermute | solution.py:212
  209.3 3.9 %collective-permute-start.31 = (f32[64,64]{1,0:T(8,128)S(1)}, f32[64,64]{1,0:T(8,128)S(1)}, u32[]{:S(2)}, u32[]{:S(2)}) collective-permute-start(f32[64,64]{1,0:T(8,128)S(1)} %add.130), channel_id=1, source_target_pairs={{0,1},{1,0},{2,3},{3,2},{4,5},{5,4},{6,7},{7,6},{8,9},{9,8},{10,11... | collective-permute-start | bytes 49160 | tf_op jit(solution)/shard_map/ppermute | solution.py:212
  211.3 4.8 %collective-permute-start.32 = (f32[64,64]{1,0:T(8,128)S(1)}, f32[64,64]{1,0:T(8,128)S(1)}, u32[]{:S(2)}, u32[]{:S(2)}) collective-permute-start(f32[64,64]{1,0:T(8,128)S(1)} %add.130), channel_id=1, source_target_pairs={{0,17},{1,16},{2,19},{3,18},{4,21},{5,20},{6,23},{7,22},{8,25},{9,... | collective-permute-start | bytes 49160 | tf_op jit(solution)/shard_map/ppermute | solution.py:212
  216.1 4.5 %collective-permute-start.33 = (f32[64,64]{1,0:T(8,128)S(1)}, f32[64,64]{1,0:T(8,128)S(1)}, u32[]{:S(2)}, u32[]{:S(2)}) collective-permute-start(f32[64,64]{1,0:T(8,128)S(1)} %add_add_fusion.1), channel_id=1, source_target_pairs={{0,2},{1,3},{2,0},{3,1},{4,6},{5,7},{6,4},{7,5},{8,10},{9,11},{10,... | collective-permute-start | bytes 49160 | tf_op jit(solution)/shard_map/ppermute | solution.py:212
  217.4 4.8 %collective-permute-start.34 = (f32[64,64]{1,0:T(8,128)S(1)}, f32[64,64]{1,0:T(8,128)S(1)}, u32[]{:S(2)}, u32[]{:S(2)}) collective-permute-start(f32[64,64]{1,0:T(8,128)S(1)} %add_add_fusion.1), channel_id=1, source_target_pairs={{0,4},{1,5},{2,6},{3,7},{4,0},{5,1},{6,2},{7,3},{8,12},{9,13},{10,... | collective-permute-start | bytes 49160 | tf_op jit(solution)/shard_map/ppermute | solution.py:212
  217.8 5.7 %collective-permute-start.35 = (f32[64,64]{1,0:T(8,128)S(1)}, f32[64,64]{1,0:T(8,128)S(1)}, u32[]{:S(2)}, u32[]{:S(2)}) collective-permute-start(f32[64,64]{1,0:T(8,128)S(1)} %add_add_fusion.1), channel_id=1, source_target_pairs={{0,6},{1,7},{2,4},{3,5},{4,2},{5,3},{6,0},{7,1},{8,14},{9,15},{10,... | collective-permute-start | bytes 49160 | tf_op jit(solution)/shard_map/ppermute | solution.py:212
  (11 other events, 9.8 us)

commit v3 on v2

v3 whole, which is shorter than its diff:
```python
import functools
import math

import jax
import jax.numpy as jnp
from jax import lax
from jax.experimental import pallas as pl
from jax.experimental.pallas import tpu as pltpu
from jax.sharding import PartitionSpec as P

REACH = 2
ITERS = 3
BLK_DEV = 2

SHARP = 8.0
EPSILON = 1e-06

F32 = jnp.float32
BF16 = jnp.bfloat16
EXACT = lax.Precision.HIGHEST
VMEM = pl.BlockSpec(memory_space=pltpu.VMEM)
SMEM = pl.BlockSpec(memory_space=pltpu.SMEM)


def call(body, out_shape, in_specs, flops, moved, room=6, aliases=None):
    return pl.pallas_call(
        body,
        out_shape=out_shape,
        in_specs=in_specs,
        out_specs=jax.tree.map(lambda _: VMEM, out_shape),
        input_output_aliases=aliases or {},
        cost_estimate=pl.CostEstimate(flops=flops, bytes_accessed=moved, transcendentals=0),
        compiler_params=pltpu.CompilerParams(vmem_limit_bytes=room << 20),
    )


def shaped(shape, dtype):
    return jax.ShapeDtypeStruct(shape, dtype)


def cross(left, right, **kw):
    return lax.dot_general(
        left, right, (((1,), (1,)), ((), ())), preferred_element_type=F32, **kw
    )


STEPS = 8


def unit_rows_body(block, points_ref, out_ref, held, arrived):
    size = out_ref.shape[0]
    step = size // STEPS
    copies = []
    for at in range(STEPS):
        rows = pl.ds(at * step, step)
        source = points_ref.at[pl.ds(block * size + at * step, step)]
        copies.append(pltpu.make_async_copy(source, held.at[rows], arrived.at[at]))
        copies[-1].start()
    for at in range(STEPS):
        copies[at].wait()
        rows = pl.ds(at * step, step)
        points = held[rows, :]
        mean = jnp.mean(points * points, axis=-1, keepdims=True)
        out_ref[rows, :] = (points * lax.rsqrt(mean + EPSILON)).astype(BF16)


def unit_rows(points, block, size):
    width = points.shape[1]
    return pl.pallas_call(
        functools.partial(unit_rows_body, block),
        in_specs=[pl.BlockSpec(memory_space=pltpu.HBM)],
        out_specs=VMEM,
        out_shape=shaped((size, width), BF16),
        scratch_shapes=[pltpu.VMEM((size, width), F32), pltpu.SemaphoreType.DMA((STEPS,))],
        cost_estimate=pl.CostEstimate(
            flops=3 * size * width, bytes_accessed=6 * size * width, transcendentals=0
        ),
        compiler_params=pltpu.CompilerParams(vmem_limit_bytes=61 << 20),
        name="unit_rows",
    )(points)


def affinity(rows, cols):
    width = rows.shape[1]
    return jnp.exp(cross(rows, cols) * (SHARP / width) - SHARP)


def down(tile):
    return jnp.sum(tile, axis=0, keepdims=True)


def across(tile):
    lanes = 128
    folded = tile[:, :lanes]
    for at in range(lanes, tile.shape[1], lanes):
        folded = folded + tile[:, at : at + lanes]
    return jnp.sum(folded.T, axis=0, keepdims=True)


def gated(mask, sums):
    return jnp.where(mask > 0.0, sums, 0.0)


def span(index, size):
    return slice(index * size, (index + 1) * size)


def x_own(own_mask, l, x, owns, near, first, degree):
    size = x.shape[0]
    for m, cols in enumerate(owns):
        tile = affinity(x[...], cols[...])
        near[span(l - first, size), span(m, size)] = tile.astype(BF16)
        degree[:, span(m, size)] += gated(own_mask[m, l], down(tile))


def own_z(own_mask, owns, m, z, far, degree):
    size = z.shape[0]
    sums = []
    for l, rows in enumerate(owns):
        tile = affinity(rows[...], z[...])
        far[span(l, size), :] = tile.astype(BF16)
        degree[:, span(l, size)] += gated(own_mask[l, 2 * BLK_DEV + m], across(tile))
        sums.append(down(tile))
    return sums


def x_z(x, z, far, at):
    tile = affinity(x[...], z[...])
    far[span(at, z.shape[0]), :] = tile.astype(BF16)
    return down(tile)


def first_tiles_body(own_mask, b0, b1, x0, z0, near, far, degree, far_sums):
    degree[...] = jnp.zeros_like(degree)
    for l, rows in enumerate((b0, b1, x0)):
        x_own(own_mask, l, rows, (b0, b1), near, 0, degree)
    sums = own_z(own_mask, (b0, b1), 0, z0, far, degree)
    sums.append(x_z(x0, z0, far, BLK_DEV))
    for l, line in enumerate(sums):
        far_sums[l : l + 1, :] = line


def last_tiles_body(
    own_mask, far_mask, b0, b1, x0, x1, z0, z1, degree_in, far_sums,
    near, corner, far, degree, far_degree,
):
    size = z0.shape[0]
    degree[...] = degree_in[...]
    x_own(own_mask, BLK_DEV + 1, x1, (b0, b1), near, BLK_DEV + 1, degree)
    early = [far_sums[l : l + 1, :] for l in range(far_sums.shape[0])]
    early.append(x_z(x1, z0, corner, 0))
    late = own_z(own_mask, (b0, b1), 1, z1, far, degree)
    late.append(x_z(x0, z1, far, BLK_DEV))
    late.append(x_z(x1, z1, far, BLK_DEV + 1))
    for m, sums in enumerate((early, late)):
        total = jnp.zeros((1, size), F32)
        for l, line in enumerate(sums):
            total += gated(far_mask[m, l], line)
        far_degree[:, span(m, size)] = total


def kept(mask, m, first, *vectors):
    parts = []
    at = first
    for value in vectors:
        size = value.shape[1] // BLK_DEV
        for l in range(BLK_DEV):
            part = value[:, span(l, size)]
            parts.append(jnp.where(mask[m, at] > 0.0, part, jnp.zeros_like(part)))
            at += 1
    return jnp.concatenate(parts, axis=1)


def apart(left, right):
    return jnp.dot(left, right, preferred_element_type=F32)


def far_rows_body(mask, own, x, far0, corner, far1, out):
    size = own.shape[1] // BLK_DEV
    cut = far0.shape[0]
    left = kept(mask, 0, 0, own, x)
    out[:, span(0, size)] = apart(left[:, :cut], far0[...]) + apart(left[:, cut:], corner[...])
    out[:, span(1, size)] = apart(kept(mask, 1, 0, own, x), far1[...])


def own_rows_body(mask, own, x, z, given, root, near0, near1, far0, far1, image, gram):
    size = own.shape[1] // BLK_DEV
    cut = near0.shape[0]
    for m in range(BLK_DEV):
        there = span(m, size)
        left = kept(mask, m, 0, own, x)
        side = kept(mask, m, 2 * BLK_DEV, z)
        total = given[:, there] + apart(left[:, :cut], near0[:, there])
        total += apart(left[:, cut:], near1[:, there])
        total += cross(side[:, :size], far0[there, :]) + cross(side[:, size:], far1[there, :])
        image[:, there] = total * root[:, there]
    full = image[...]
    gram[...] = cross(full, full, precision=EXACT)


def inverse_factor(gram):
    size = gram.shape[0]
    rows = lax.broadcasted_iota(jnp.int32, (size, 2 * size), 0)
    lanes = lax.broadcasted_iota(jnp.int32, (size, 2 * size), 1)
    unit = jnp.where(rows + size == lanes, 1.0, 0.0).astype(F32)
    work = jnp.concatenate([gram, unit[:, size:]], axis=1)
    for j in range(size):
        pivot_row = work[j : j + 1, :]
        scale = 1.0 / pivot_row[:, j : j + 1]
        factor = jnp.where(rows[:, :1] > j, work[:, j : j + 1] * scale, 0.0)
        work = work - factor * pivot_row
    diagonal = jnp.sum(jnp.where(rows == lanes, work, 0.0), axis=1, keepdims=True)
    return work[:, size:] * lax.rsqrt(diagonal)


def solve_body(scale, gram, image, root, out, scaled):
    factor = inverse_factor(gram[...])
    vectors = jnp.dot(factor, image[...], preferred_element_type=F32, precision=EXACT) * scale
    out[...] = vectors
    scaled[...] = (vectors * root[...]).astype(BF16)


def exchange_masks(row_count, col_count):
    low = [1 << bit for bit in range(col_count.bit_length() - 1)]
    high = [col_count << bit for bit in range(row_count.bit_length() - 1)]
    stages = [(high[0],), (high[1], low[0]), (low[1], low[2])]
    rest = high[2:] + low[3:]
    return stages + [tuple(rest[at : at + 2]) for at in range(0, len(rest), 2)]


def total_sum(value):
    row_count = lax.axis_size("row")
    col_count = lax.axis_size("col")
    devices = row_count * col_count
    if devices & (devices - 1) or row_count < 4 or col_count < 8:
        return lax.psum(value, ("row", "col"))

    def fetched(mask):
        pairs = [(source, source ^ mask) for source in range(devices)]
        return lax.ppermute(value, ("row", "col"), pairs)

    for masks in exchange_masks(row_count, col_count):
        if len(masks) == 1:
            value = value + fetched(masks[0])
        else:
            first, second = masks
            near, far, both = fetched(first), fetched(second), fetched(first ^ second)
            value = (value + near) + (far + both)
    return value


def listed(ids, blocks):
    found = jnp.zeros((ids.shape[0], blocks.shape[0]), bool)
    for slot in range(ids.shape[1]):
        found = found | (ids[:, slot : slot + 1] == blocks[None, :])
    return found.astype(F32)


def on_device(embeddings, neighbour_ids, start_vectors):
    col_count = lax.axis_size("col")
    col = lax.axis_index("col")
    base = lax.axis_index("row") * col_count
    points, width = embeddings.shape
    columns = start_vectors.shape[1]
    size = points // BLK_DEV
    total_rows = points * lax.axis_size("row") * col_count

    def side_of(index):
        return (index + (REACH if index % 2 == 0 else -REACH)) % col_count

    def from_x(value):
        return lax.ppermute(value, "col", [(i, i ^ 1) for i in range(col_count)])

    def from_z(value):
        return lax.ppermute(value, "col", [(side_of(i), i) for i in range(col_count)])

    def to_z(value):
        return lax.ppermute(value, "col", [(i, side_of(i)) for i in range(col_count)])

    b0 = unit_rows(embeddings, 0, size)
    z0 = from_z(b0)
    x0 = from_x(b0)
    b1 = unit_rows(embeddings, 1, size)
    z1 = from_z(b1)
    x1 = from_x(b1)
    far_ids = from_z(neighbour_ids)

    here = base + col
    x_side = base + (col ^ 1)
    z_side = base + (col + jnp.where(col % 2 == 0, REACH, col_count - REACH)) % col_count
    members = jnp.arange(BLK_DEV, dtype=jnp.int32)
    nearby = jnp.stack([here, x_side, z_side])[:, None] * BLK_DEV + members[None, :]
    nearby = nearby.reshape(-1)
    own_mask = listed(neighbour_ids, nearby)
    far_mask = listed(far_ids, nearby[: 2 * BLK_DEV])

    line = shaped((1, points), F32)
    one = 2 * size * size * width
    moved = 4 * size * width
    most = 2 * BLK_DEV - 1
    near0, far0, degree, far_sums = call(
        first_tiles_body,
        (
            shaped((most * size, points), BF16), shaped((most * size, size), BF16), line,
            shaped((most, size), F32),
        ),
        [SMEM] + [VMEM] * 4, 9 * one, 9 * moved,
    )(own_mask, b0, b1, x0, z0)
    near1, corner, far1, degree, far_degree = call(
        last_tiles_body,
        (
            shaped((size, points), BF16), shaped((size, size), BF16),
            shaped((2 * points, size), BF16), line, line,
        ),
        [SMEM] * 2 + [VMEM] * 8, 7 * one, 7 * moved,
    )(own_mask, far_mask, b0, b1, x0, x1, z0, z1, degree, far_sums)
    root = lax.rsqrt(degree + to_z(far_degree))

    across_shape = (columns, points)
    work = 2 * columns * size * size
    far_rows = call(
        far_rows_body, shaped(across_shape, F32), [SMEM] + [VMEM] * 5, 8 * work, 8 * work // 64
    )
    own_rows = call(
        own_rows_body,
        (shaped(across_shape, F32), shaped((columns, columns), F32)),
        [SMEM] + [VMEM] * 9, 12 * work, 12 * work // 64,
    )
    solve = call(
        functools.partial(solve_body, math.sqrt(total_rows)),
        (shaped(across_shape, F32), shaped(across_shape, BF16)),
        [VMEM] * 3, 4 * columns * columns * points, 4 * columns * points,
    )
    vectors = start_vectors.T
    scaled = (vectors * root).astype(BF16)
    for _ in range(ITERS):
        x = from_x(scaled)
        z = from_z(scaled)
        given = to_z(far_rows(far_mask, scaled, x, far0, corner, far1))
        image, gram = own_rows(own_mask, scaled, x, z, given, root, near0, near1, far0, far1)
        vectors, scaled = solve(total_sum(gram), image, root)
    return vectors.T


def solution(mesh):
    in_specs = (P(("row", "col"), None), P(("row", "col"), None), P(("row", "col"), None))
    out_specs = P(("row", "col"), None)
    return jax.shard_map(on_device, mesh=mesh, in_specs=in_specs, out_specs=out_specs, check_vma=False)
```

time: 232 us -> 192 us (0.83)
  Pallas kernels: 77.9 us -> 50.2 us
  other arithmetic: 9.5 us -> 0.43 us
  local copies, waits for them, and re-layouts: 9.16 us -> 2.12 us
  waiting for transfers between devices: 85.9 us -> 88.5 us
    pallas_call x11 -> x10, Pallas kernels: 55.8 us -> 31 us  [the longest x3 7.27 us: on_device(): own_rows(own_mask, scaled, x, z, given, root, near0, near1, far0, far1)]
    ppermute x21, waiting for transfers between devices: 26.5 us -> 20.3 us  [fetched(): return lax.ppermute(value, ('row', 'col'), pairs)]
    unnamed x52 -> x10, local copies, waits for them, and re-layouts: 7.09 us -> 1.24 us
    ppermute x6, waiting for transfers between devices: 42.9 us -> 48.6 us  [from_z(): lax.ppermute(value, 'col', [(side_of(i), i) for i in range(col_count)])]
    pallas_call x4 -> x0, other arithmetic: 3.95 us -> none  [the longest x2 2.65 us: on_device(): call(last_tiles_body, (half, line, tall, pair, line, tile, short, tile, s...]
    ppermute x5, starting transfers between devices: 6.77 us -> 3.28 us  [from_x(): return lax.ppermute(value, 'col', [(i, i ^ 1) for i in range(col_count)])]
    pallas_call x3, Pallas kernels: 22.2 us -> 19.2 us  [on_device(): vectors, scaled = solve(total_sum(gram), image, root)]
    ppermute x6, starting transfers between devices: 16.7 us -> 19.6 us  [from_z(): lax.ppermute(value, 'col', [(side_of(i), i) for i in range(col_count)])]
  transfers between devices with their start and end apart: 36 -> 36, of which waited for: 28 -> 28; matrix products, arithmetic and copies ran while one was open for 3% -> 1% of each run, Pallas kernels for 7% -> 5%
where the time goes in v3:
time: 192 us
  waiting for transfers between devices  88.5 us (46%)
  Pallas kernels  50.2 us (26%)
  starting transfers between devices  50 us (26%)
  local copies, waits for them, and re-layouts  2.12 us (1%)
    ppermute x6, waiting for transfers between devices, from_z(): lax.ppermute(value, 'col', [(side_of(i), i) for i in range(col_count)])  48.6 us
    ppermute x21, starting transfers between devices, fetched(): return lax.ppermute(value, ('row', 'col'), pairs)  24 us
    ppermute x21, waiting for transfers between devices, fetched(): return lax.ppermute(value, ('row', 'col'), pairs)  20.3 us
    ppermute x6, starting transfers between devices, from_z(): lax.ppermute(value, 'col', [(side_of(i), i) for i in range(col_count)])  19.6 us
    pallas_call x3, Pallas kernels, on_device(): vectors, scaled = solve(total_sum(gram), image, root)  19.2 us
    ppermute x5, waiting for transfers between devices, from_x(): return lax.ppermute(value, 'col', [(i, i ^ 1) for i in range(col_count)])  12.1 us
    ppermute x4, waiting for transfers between devices, to_z(): lax.ppermute(value, 'col', [(i, side_of(i)) for i in range(col_count)])  7.47 us
    pallas_call x3, Pallas kernels, on_device(): own_rows(own_mask, scaled, x, z, given, root, near0, near1, far0, far1)  7.27 us
  transfers between devices with their start and end apart: 36, of which 28 were waited for; matrix products, arithmetic and copies ran while one was open for 1% of the time, Pallas kernels for 5%

profile of v3, /device:TPU:0, one launch (start us, length us, event | category | flops | bytes accessed | tf_op | source)
XLA Modules:
  0.0 191.5 jit_solution(9829246618191648737)
XLA Ops:
  0.0 3.0 %unit_rows.2.b0 = bf16[512,1024]{1,0:T(8,128)(2,1)} custom-call(f32[1024,1024]{1,0:T(8,128)} %points_ref.3), custom_call_target="tpu_custom_call" | custom-call | flops 1572864 | bytes 3145728 | tf_op jit(solution)/shard_map/unit_rows/pallas_call | solution.py:69
  3.0 5.1 %collective-permute-start.3 = (bf16[512,1024]{1,0:T(8,128)(2,1)}, bf16[512,1024]{1,0:T(8,128)(2,1)S(1)}, u32[]{:S(2)}, u32[]{:S(2)}) collective-permute-start(bf16[512,1024]{1,0:T(8,128)(2,1)} %unit_rows.2.b0), channel_id=1, source_target_pairs={{2,0},{7,1},{4,2},{1,3},{6,4},{3,5},{0,6},{5,7},{10,8},{15,9},{12,... | collective-permute-start | bytes 3145736 | tf_op jit(solution)/shard_map/ppermute | solution.py:275
  8.1 2.9 %unit_rows.3.b1 = bf16[512,1024]{1,0:T(8,128)(2,1)} custom-call(f32[1024,1024]{1,0:T(8,128)} %points_ref.3), custom_call_target="tpu_custom_call" | custom-call | flops 1572864 | bytes 3145728 | tf_op jit(solution)/shard_map/unit_rows/pallas_call | solution.py:69
  11.0 1.8 collective-permute-start.4
  13.2 3.7 %collective-permute-start = (s32[2,12]{1,0:T(2,128)S(1)}, s32[2,12]{1,0:T(2,128)S(1)}, u32[]{:S(2)}, u32[]{:S(2)}) collective-permute-start(s32[2,12]{1,0:T(2,128)S(1)} %copy-done.4), channel_id=1, source_target_pairs={{2,0},{7,1},{4,2},{1,3},{6,4},{3,5},{0,6},{5,7},{10,8},{15,9},{12,... | collective-permute-start | bytes 296 | tf_op jit(solution)/shard_map/ppermute | solution.py:275
  17.7 35.6 %collective-permute-done = s32[2,12]{1,0:T(2,128)S(1)} collective-permute-done((s32[2,12]{1,0:T(2,128)S(1)}, s32[2,12]{1,0:T(2,128)S(1)}, u32[]{:S(2)}, u32[]{:S(2)}) %collective-permute-start) | collective-permute-done | bytes 128 | tf_op jit(solution)/shard_map/ppermute | solution.py:275
  55.0 7.2 %shard_map.37 = (bf16[1536,1024]{1,0:T(8,128)(2,1)S(1)}, bf16[1536,512]{1,0:T(8,128)(2,1)S(1)}, f32[1,1024]{1,0:T(1,128)S(1)}, f32[3,512]{1,0:T(4,128)S(1)}) custom-call(f32[2,6]{1,0:T(2,128)S(1)} %or_convert_fusion.1.own_mask.mask, bf16[512,1024]{1,0:T(8,128)(2,1)S(1)} %copy-done, bf16[512,1024]{1,0:T(8,128)(2,1)S(1)} %copy-done.1, ...), custom_call_target="tpu_custom_call" | custom-call | flops 4831838208 | bytes 18874368 | tf_op jit(solution)/shard_map/pallas_call | solution.py:301
  62.2 6.5 %shard_map.38 = (bf16[512,1024]{1,0:T(8,128)(2,1)S(1)}, bf16[512,512]{1,0:T(8,128)(2,1)S(1)}, bf16[2048,512]{1,0:T(8,128)(2,1)S(1)}, f32[1,1024]{1,0:T(1,128)S(1)}, f32[1,1024]{1,0:T(1,128)S(1)}) custom-call(f32[2,6]{1,0:T(2,128)S(1)} %or_convert_fusion.1.own_mask.mask, f32[2,4]{1,0:T(2,128)S(1)} %or_convert_fusion.far_mask.mask, ...), custom_call_target="tpu_custom_call" | custom-call | flops 3758096384 | bytes 14680064 | tf_op jit(solution)/shard_map/pallas_call | solution.py:309
  69.3 5.4 %collective-permute-done.5 = f32[1,1024]{1,0:T(1,128)S(1)} collective-permute-done((f32[1,1024]{1,0:T(1,128)S(1)}, f32[1,1024]{1,0:T(1,128)S(1)}, u32[]{:S(2)}, u32[]{:S(2)}) %collective-permute-start.5) | collective-permute-done | bytes 4128 | tf_op jit(solution)/shard_map/ppermute | solution.py:278
  74.8 5.0 %collective-permute-done.6.x = bf16[64,1024]{1,0:T(8,128)(2,1)S(1)} collective-permute-done((bf16[64,1024]{1,0:T(8,128)(2,1)S(1)}, bf16[64,1024]{1,0:T(8,128)(2,1)S(1)}, u32[]{:S(2)}, u32[]{:S(2)}) %collective-permute-start.6) | collective-permute-done | bytes 131104 | tf_op jit(solution)/shard_map/ppermute | solution.py:272
  79.8 1.4 shard_map.39
  81.2 3.8 %collective-permute-start.7 = (bf16[64,1024]{1,0:T(8,128)(2,1)S(1)}, bf16[64,1024]{1,0:T(8,128)(2,1)S(1)}, u32[]{:S(2)}, u32[]{:S(2)}) collective-permute-start(bf16[64,1024]{1,0:T(8,128)(2,1)S(1)} %fusion.own), channel_id=1, source_target_pairs={{2,0},{7,1},{4,2},{1,3},{6,4},{3,5},{0,6},{5,7},{10,8},{15,9},{12,... | collective-permute-start | bytes 393224 | tf_op jit(solution)/shard_map/ppermute | solution.py:275
  85.1 2.5 %collective-permute-done.7.z = bf16[64,1024]{1,0:T(8,128)(2,1)S(1)} collective-permute-done((bf16[64,1024]{1,0:T(8,128)(2,1)S(1)}, bf16[64,1024]{1,0:T(8,128)(2,1)S(1)}, u32[]{:S(2)}, u32[]{:S(2)}) %collective-permute-start.7) | collective-permute-done | bytes 131104 | tf_op jit(solution)/shard_map/ppermute | solution.py:275
  87.6 2.1 %collective-permute-done.8.given = f32[64,1024]{1,0:T(8,128)S(1)} collective-permute-done((f32[64,1024]{1,0:T(8,128)S(1)}, f32[64,1024]{1,0:T(8,128)S(1)}, u32[]{:S(2)}, u32[]{:S(2)}) %collective-permute-start.8) | collective-permute-done | bytes 262176 | tf_op jit(solution)/shard_map/ppermute | solution.py:278
  89.6 2.4 %shard_map.40 = (f32[64,1024]{1,0:T(8,128)S(1)}, f32[64,64]{1,0:T(8,128)S(1)}) custom-call(f32[2,6]{1,0:T(2,128)S(1)} %or_convert_fusion.1.own_mask.mask, bf16[64,1024]{1,0:T(8,128)(2,1)S(1)} %fusion.own, bf16[64,1024]{1,0:T(8,128)(2,1)S(1)} %collective-permute-done.6.x, bf16[64,1024]{1,0:T(8,128)(2,1)S(1)} %collective-permute-done.7.z, ...), custom_call_target="tpu_custom_call" | custom-call | flops 402653184 | bytes 6291456 | tf_op jit(solution)/shard_map/pallas_call | solution.py:340
  93.3 2.8 %collective-permute-start.12 = (f32[64,64]{1,0:T(8,128)S(1)}, f32[64,64]{1,0:T(8,128)S(1)}, u32[]{:S(2)}, u32[]{:S(2)}) collective-permute-start(f32[64,64]{1,0:T(8,128)S(1)} %add.116), channel_id=1, source_target_pairs={{0,17},{1,16},{2,19},{3,18},{4,21},{5,20},{6,23},{7,22},{8,25},{9,... | collective-permute-start | bytes 49160 | tf_op jit(solution)/shard_map/ppermute | solution.py:240
  96.8 1.3 collective-permute-done.12
  98.1 1.9 %collective-permute-done.11 = f32[64,64]{1,0:T(8,128)S(1)} collective-permute-done((f32[64,64]{1,0:T(8,128)S(1)}, f32[64,64]{1,0:T(8,128)S(1)}, u32[]{:S(2)}, u32[]{:S(2)}) %collective-permute-start.11) | collective-permute-done | bytes 16416 | tf_op jit(solution)/shard_map/ppermute | solution.py:240
  100.2 2.3 %collective-permute-start.15 = (f32[64,64]{1,0:T(8,128)S(1)}, f32[64,64]{1,0:T(8,128)S(1)}, u32[]{:S(2)}, u32[]{:S(2)}) collective-permute-start(f32[64,64]{1,0:T(8,128)S(1)} %add_add_fusion.5), channel_id=1, source_target_pairs={{0,6},{1,7},{2,4},{3,5},{4,2},{5,3},{6,0},{7,1},{8,14},{9,15},{10,... | collective-permute-start | bytes 49160 | tf_op jit(solution)/shard_map/ppermute | solution.py:240
  102.6 2.0 %collective-permute-start.13 = (f32[64,64]{1,0:T(8,128)S(1)}, f32[64,64]{1,0:T(8,128)S(1)}, u32[]{:S(2)}, u32[]{:S(2)}) collective-permute-start(f32[64,64]{1,0:T(8,128)S(1)} %add_add_fusion.5), channel_id=1, source_target_pairs={{0,2},{1,3},{2,0},{3,1},{4,6},{5,7},{6,4},{7,5},{8,10},{9,11},{10,... | collective-permute-start | bytes 49160 | tf_op jit(solution)/shard_map/ppermute | solution.py:240
  104.7 1.4 collective-permute-done.15
  106.1 1.3 collective-permute-done.14
  107.5 6.4 %shard_map.41 = (f32[64,1024]{1,0:T(8,128)}, bf16[64,1024]{1,0:T(8,128)(2,1)S(1)}) custom-call(f32[64,64]{1,0:T(8,128)S(1)} %add_add_fusion.4.gram, f32[64,1024]{1,0:T(8,128)S(1)} %get-tuple-element.33.image, f32[1,1024]{1,0:T(1,128)S(1)} %add_rsqrt_fusion.root), custom_call_target="tpu_custom_call" | custom-call | flops 16777216 | bytes 262144 | tf_op jit(solution)/shard_map/pallas_call | solution.py:341
  113.9 1.5 collective-permute-start.16
  115.3 3.5 %collective-permute-done.16.x = bf16[64,1024]{1,0:T(8,128)(2,1)S(1)} collective-permute-done((bf16[64,1024]{1,0:T(8,128)(2,1)S(1)}, bf16[64,1024]{1,0:T(8,128)(2,1)S(1)}, u32[]{:S(2)}, u32[]{:S(2)}) %collective-permute-start.16) | collective-permute-done | bytes 131104 | tf_op jit(solution)/shard_map/ppermute | solution.py:272
  118.8 1.4 shard_map.42
  121.4 2.7 %collective-permute-start.17 = (bf16[64,1024]{1,0:T(8,128)(2,1)S(1)}, bf16[64,1024]{1,0:T(8,128)(2,1)S(1)}, u32[]{:S(2)}, u32[]{:S(2)}) collective-permute-start(bf16[64,1024]{1,0:T(8,128)(2,1)S(1)} %get-tuple-element.34.own), channel_id=1, source_target_pairs={{2,0},{7,1},{4,2},{1,3},{6,4},{3,5},{0,6},{5,7},{10,8},{15,9},{12,... | collective-permute-start | bytes 393224 | tf_op jit(solution)/shard_map/ppermute | solution.py:275
  124.1 5.1 %collective-permute-done.17.z = bf16[64,1024]{1,0:T(8,128)(2,1)S(1)} collective-permute-done((bf16[64,1024]{1,0:T(8,128)(2,1)S(1)}, bf16[64,1024]{1,0:T(8,128)(2,1)S(1)}, u32[]{:S(2)}, u32[]{:S(2)}) %collective-permute-start.17) | collective-permute-done | bytes 131104 | tf_op jit(solution)/shard_map/ppermute | solution.py:275
  129.2 2.4 %shard_map.43 = (f32[64,1024]{1,0:T(8,128)S(1)}, f32[64,64]{1,0:T(8,128)S(1)}) custom-call(f32[2,6]{1,0:T(2,128)S(1)} %or_convert_fusion.1.own_mask.mask, bf16[64,1024]{1,0:T(8,128)(2,1)S(1)} %get-tuple-element.34.own, bf16[64,1024]{1,0:T(8,128)(2,1)S(1)} %collective-permute-done.16.x, bf16[64,1024]{1,0:T(8,128)(2,1)S(1)} %collective-permute-done.17.z, ...), custom_call_target="tpu_custom_call" | custom-call | flops 402653184 | bytes 6291456 | tf_op jit(solution)/shard_map/pallas_call | solution.py:340
  134.9 1.5 collective-permute-start.20
  136.4 1.4 collective-permute-done.22
  138.8 1.9 collective-permute-start.25
  141.5 1.7 collective-permute-start.23
  143.3 1.3 collective-permute-done.25
  145.8 6.4 %shard_map.44 = (f32[64,1024]{1,0:T(8,128)}, bf16[64,1024]{1,0:T(8,128)(2,1)S(1)}) custom-call(f32[64,64]{1,0:T(8,128)S(1)} %add_add_fusion.2.gram, f32[64,1024]{1,0:T(8,128)S(1)} %get-tuple-element.36.image, f32[1,1024]{1,0:T(1,128)S(1)} %add_rsqrt_fusion.root), custom_call_target="tpu_custom_call" | custom-call | flops 16777216 | bytes 262144 | tf_op jit(solution)/shard_map/pallas_call | solution.py:341
  152.2 1.3 collective-permute-start.26
  153.6 3.6 %collective-permute-done.26.x = bf16[64,1024]{1,0:T(8,128)(2,1)S(1)} collective-permute-done((bf16[64,1024]{1,0:T(8,128)(2,1)S(1)}, bf16[64,1024]{1,0:T(8,128)(2,1)S(1)}, u32[]{:S(2)}, u32[]{:S(2)}) %collective-permute-start.26) | collective-permute-done | bytes 131104 | tf_op jit(solution)/shard_map/ppermute | solution.py:272
  157.2 1.4 shard_map.45
  158.6 1.4 collective-permute-start.28
  160.0 2.4 %collective-permute-start.27 = (bf16[64,1024]{1,0:T(8,128)(2,1)S(1)}, bf16[64,1024]{1,0:T(8,128)(2,1)S(1)}, u32[]{:S(2)}, u32[]{:S(2)}) collective-permute-start(bf16[64,1024]{1,0:T(8,128)(2,1)S(1)} %get-tuple-element.37.own), channel_id=1, source_target_pairs={{2,0},{7,1},{4,2},{1,3},{6,4},{3,5},{0,6},{5,7},{10,8},{15,9},{12,... | collective-permute-start | bytes 393224 | tf_op jit(solution)/shard_map/ppermute | solution.py:275
  162.5 5.3 %collective-permute-done.27.z = bf16[64,1024]{1,0:T(8,128)(2,1)S(1)} collective-permute-done((bf16[64,1024]{1,0:T(8,128)(2,1)S(1)}, bf16[64,1024]{1,0:T(8,128)(2,1)S(1)}, u32[]{:S(2)}, u32[]{:S(2)}) %collective-permute-start.27) | collective-permute-done | bytes 131104 | tf_op jit(solution)/shard_map/ppermute | solution.py:275
  167.8 2.4 %shard_map.46 = (f32[64,1024]{1,0:T(8,128)S(1)}, f32[64,64]{1,0:T(8,128)S(1)}) custom-call(f32[2,6]{1,0:T(2,128)S(1)} %or_convert_fusion.1.own_mask.mask, bf16[64,1024]{1,0:T(8,128)(2,1)S(1)} %get-tuple-element.37.own, bf16[64,1024]{1,0:T(8,128)(2,1)S(1)} %collective-permute-done.26.x, bf16[64,1024]{1,0:T(8,128)(2,1)S(1)} %collective-permute-done.27.z, ...), custom_call_target="tpu_custom_call" | custom-call | flops 402653184 | bytes 6291456 | tf_op jit(solution)/shard_map/pallas_call | solution.py:340
  171.5 2.2 %collective-permute-start.32 = (f32[64,64]{1,0:T(8,128)S(1)}, f32[64,64]{1,0:T(8,128)S(1)}, u32[]{:S(2)}, u32[]{:S(2)}) collective-permute-start(f32[64,64]{1,0:T(8,128)S(1)} %add.130), channel_id=1, source_target_pairs={{0,17},{1,16},{2,19},{3,18},{4,21},{5,20},{6,23},{7,22},{8,25},{9,... | collective-permute-start | bytes 49160 | tf_op jit(solution)/shard_map/ppermute | solution.py:240
  175.0 1.5 collective-permute-done.32
  178.4 1.9 collective-permute-start.35
  180.8 2.0 %collective-permute-start.33 = (f32[64,64]{1,0:T(8,128)S(1)}, f32[64,64]{1,0:T(8,128)S(1)}, u32[]{:S(2)}, u32[]{:S(2)}) collective-permute-start(f32[64,64]{1,0:T(8,128)S(1)} %add_add_fusion.1), channel_id=1, source_target_pairs={{0,2},{1,3},{2,0},{3,1},{4,6},{5,7},{6,4},{7,5},{8,10},{9,11},{10,... | collective-permute-start | bytes 49160 | tf_op jit(solution)/shard_map/ppermute | solution.py:240
  182.9 1.3 collective-permute-done.35
  185.1 6.4 %shard_map.47 = (f32[64,1024]{1,0:T(8,128)}, bf16[64,1024]{1,0:T(8,128)(2,1)}) custom-call(f32[64,64]{1,0:T(8,128)S(1)} %add_add_fusion.gram, f32[64,1024]{1,0:T(8,128)S(1)} %get-tuple-element.39.image, f32[1,1024]{1,0:T(1,128)S(1)} %add_rsqrt_fusion.root), custom_call_target="tpu_custom_call" | custom-call | flops 16777216 | bytes 262144 | tf_op jit(solution)/shard_map/pallas_call | solution.py:341
  (67 shorter events, 19.0 us)
Async XLA Ops:
  3.0 10.2 %copy-start.4 = (s32[2,12]{1,0:T(2,128)S(1)}, s32[2,12]{1,0:T(2,128)}, u32[]{:S(2)}) copy-start(s32[2,12]{1,0:T(2,128)} %param.4) | copy-start | bytes 292
  3.0 50.8 %copy-start = (bf16[512,1024]{1,0:T(8,128)(2,1)S(1)}, bf16[512,1024]{1,0:T(8,128)(2,1)}, u32[]{:S(2)}) copy-start(bf16[512,1024]{1,0:T(8,128)(2,1)} %unit_rows.2.b0) | copy-start | bytes 3145732
  3.0 50.8 %collective-permute-start.3 = (bf16[512,1024]{1,0:T(8,128)(2,1)}, bf16[512,1024]{1,0:T(8,128)(2,1)S(1)}, u32[]{:S(2)}, u32[]{:S(2)}) collective-permute-start(bf16[512,1024]{1,0:T(8,128)(2,1)} %unit_rows.2.b0), channel_id=1, source_target_pairs={{2,0},{7,1},{4,2},{1,3},{6,4},{3,5},{0,6},{5,7},{10,8},{15,9},{12,... | collective-permute-start | bytes 3145736 | tf_op jit(solution)/shard_map/ppermute | solution.py:275
  8.1 45.7 %collective-permute-start.1 = (bf16[512,1024]{1,0:T(8,128)(2,1)}, bf16[512,1024]{1,0:T(8,128)(2,1)}, u32[]{:S(2)}, u32[]{:S(2)}) collective-permute-start(bf16[512,1024]{1,0:T(8,128)(2,1)} %unit_rows.2.b0), channel_id=1, source_target_pairs={{0,1},{1,0},{2,3},{3,2},{4,5},{5,4},{6,7},{7,6},{8,9},{9,8},{10,11... | collective-permute-start | bytes 3145736 | tf_op jit(solution)/shard_map/ppermute | solution.py:272
  11.0 51.2 %collective-permute-start.4 = (bf16[512,1024]{1,0:T(8,128)(2,1)}, bf16[512,1024]{1,0:T(8,128)(2,1)}, u32[]{:S(2)}, u32[]{:S(2)}) collective-permute-start(bf16[512,1024]{1,0:T(8,128)(2,1)} %unit_rows.3.b1), channel_id=1, source_target_pairs={{2,0},{7,1},{4,2},{1,3},{6,4},{3,5},{0,6},{5,7},{10,8},{15,9},{12,... | collective-permute-start | bytes 3145736 | tf_op jit(solution)/shard_map/ppermute | solution.py:275
  12.8 49.4 %collective-permute-start.2 = (bf16[512,1024]{1,0:T(8,128)(2,1)}, bf16[512,1024]{1,0:T(8,128)(2,1)}, u32[]{:S(2)}, u32[]{:S(2)}) collective-permute-start(bf16[512,1024]{1,0:T(8,128)(2,1)} %unit_rows.3.b1), channel_id=1, source_target_pairs={{0,1},{1,0},{2,3},{3,2},{4,5},{5,4},{6,7},{7,6},{8,9},{9,8},{10,11... | collective-permute-start | bytes 3145736 | tf_op jit(solution)/shard_map/ppermute | solution.py:272
  13.2 40.2 %collective-permute-start = (s32[2,12]{1,0:T(2,128)S(1)}, s32[2,12]{1,0:T(2,128)S(1)}, u32[]{:S(2)}, u32[]{:S(2)}) collective-permute-start(s32[2,12]{1,0:T(2,128)S(1)} %copy-done.4), channel_id=1, source_target_pairs={{2,0},{7,1},{4,2},{1,3},{6,4},{3,5},{0,6},{5,7},{10,8},{15,9},{12,... | collective-permute-start | bytes 296 | tf_op jit(solution)/shard_map/ppermute | solution.py:275
  53.8 1.2 copy-start.1
  55.0 7.2 %copy-start.2 = (bf16[512,1024]{1,0:T(8,128)(2,1)S(1)}, bf16[512,1024]{1,0:T(8,128)(2,1)}, u32[]{:S(2)}) copy-start(bf16[512,1024]{1,0:T(8,128)(2,1)} %unit_rows.3.b1) | copy-start | bytes 3145732
  62.2 12.5 %copy-start.3 = (f32[1024,64]{0,1:T(8,128)S(1)}, f32[1024,64]{0,1:T(8,128)}, u32[]{:S(2)}) copy-start(f32[1024,64]{0,1:T(8,128)} %param.5) | copy-start | bytes 786436
  68.8 5.9 %collective-permute-start.5 = (f32[1,1024]{1,0:T(1,128)S(1)}, f32[1,1024]{1,0:T(1,128)S(1)}, u32[]{:S(2)}, u32[]{:S(2)}) collective-permute-start(f32[1,1024]{1,0:T(1,128)S(1)} %get-tuple-element.26), channel_id=1, source_target_pairs={{0,2},{1,7},{2,4},{3,1},{4,6},{5,3},{6,0},{7,5},{8,10},{9,15},{10,... | collective-permute-start | bytes 12296 | tf_op jit(solution)/shard_map/ppermute | solution.py:278
  74.8 5.0 %collective-permute-start.6 = (bf16[64,1024]{1,0:T(8,128)(2,1)S(1)}, bf16[64,1024]{1,0:T(8,128)(2,1)S(1)}, u32[]{:S(2)}, u32[]{:S(2)}) collective-permute-start(bf16[64,1024]{1,0:T(8,128)(2,1)S(1)} %fusion.own), channel_id=1, source_target_pairs={{0,1},{1,0},{2,3},{3,2},{4,5},{5,4},{6,7},{7,6},{8,9},{9,8},{10,11... | collective-permute-start | bytes 393224 | tf_op jit(solution)/shard_map/ppermute | solution.py:272
  81.2 8.5 %collective-permute-start.8 = (f32[64,1024]{1,0:T(8,128)S(1)}, f32[64,1024]{1,0:T(8,128)S(1)}, u32[]{:S(2)}, u32[]{:S(2)}) collective-permute-start(f32[64,1024]{1,0:T(8,128)S(1)} %shard_map.39), channel_id=1, source_target_pairs={{0,2},{1,7},{2,4},{3,1},{4,6},{5,3},{6,0},{7,5},{8,10},{9,15},{10,... | collective-permute-start | bytes 786440 | tf_op jit(solution)/shard_map/ppermute | solution.py:278
  81.2 6.3 %collective-permute-start.7 = (bf16[64,1024]{1,0:T(8,128)(2,1)S(1)}, bf16[64,1024]{1,0:T(8,128)(2,1)S(1)}, u32[]{:S(2)}, u32[]{:S(2)}) collective-permute-start(bf16[64,1024]{1,0:T(8,128)(2,1)S(1)} %fusion.own), channel_id=1, source_target_pairs={{2,0},{7,1},{4,2},{1,3},{6,4},{3,5},{0,6},{5,7},{10,8},{15,9},{12,... | collective-permute-start | bytes 393224 | tf_op jit(solution)/shard_map/ppermute | solution.py:275
  92.1 1.3 collective-permute-start.9
  93.3 4.8 %collective-permute-start.12 = (f32[64,64]{1,0:T(8,128)S(1)}, f32[64,64]{1,0:T(8,128)S(1)}, u32[]{:S(2)}, u32[]{:S(2)}) collective-permute-start(f32[64,64]{1,0:T(8,128)S(1)} %add.116), channel_id=1, source_target_pairs={{0,17},{1,16},{2,19},{3,18},{4,21},{5,20},{6,23},{7,22},{8,25},{9,... | collective-permute-start | bytes 49160 | tf_op jit(solution)/shard_map/ppermute | solution.py:240
  96.2 3.9 %collective-permute-start.11 = (f32[64,64]{1,0:T(8,128)S(1)}, f32[64,64]{1,0:T(8,128)S(1)}, u32[]{:S(2)}, u32[]{:S(2)}) collective-permute-start(f32[64,64]{1,0:T(8,128)S(1)} %add.116), channel_id=1, source_target_pairs={{0,1},{1,0},{2,3},{3,2},{4,5},{5,4},{6,7},{7,6},{8,9},{9,8},{10,11... | collective-permute-start | bytes 49160 | tf_op jit(solution)/shard_map/ppermute | solution.py:240
  96.3 3.9 %collective-permute-start.10 = (f32[64,64]{1,0:T(8,128)S(1)}, f32[64,64]{1,0:T(8,128)S(1)}, u32[]{:S(2)}, u32[]{:S(2)}) collective-permute-start(f32[64,64]{1,0:T(8,128)S(1)} %add.116), channel_id=1, source_target_pairs={{0,16},{1,17},{2,18},{3,19},{4,20},{5,21},{6,22},{7,23},{8,24},{9,... | collective-permute-start | bytes 49160 | tf_op jit(solution)/shard_map/ppermute | solution.py:240
  100.2 5.9 %collective-permute-start.15 = (f32[64,64]{1,0:T(8,128)S(1)}, f32[64,64]{1,0:T(8,128)S(1)}, u32[]{:S(2)}, u32[]{:S(2)}) collective-permute-start(f32[64,64]{1,0:T(8,128)S(1)} %add_add_fusion.5), channel_id=1, source_target_pairs={{0,6},{1,7},{2,4},{3,5},{4,2},{5,3},{6,0},{7,1},{8,14},{9,15},{10,... | collective-permute-start | bytes 49160 | tf_op jit(solution)/shard_map/ppermute | solution.py:240
  102.5 4.9 %collective-permute-start.14 = (f32[64,64]{1,0:T(8,128)S(1)}, f32[64,64]{1,0:T(8,128)S(1)}, u32[]{:S(2)}, u32[]{:S(2)}) collective-permute-start(f32[64,64]{1,0:T(8,128)S(1)} %add_add_fusion.5), channel_id=1, source_target_pairs={{0,4},{1,5},{2,6},{3,7},{4,0},{5,1},{6,2},{7,3},{8,12},{9,13},{10,... | collective-permute-start | bytes 49160 | tf_op jit(solution)/shard_map/ppermute | solution.py:240
  102.6 4.8 %collective-permute-start.13 = (f32[64,64]{1,0:T(8,128)S(1)}, f32[64,64]{1,0:T(8,128)S(1)}, u32[]{:S(2)}, u32[]{:S(2)}) collective-permute-start(f32[64,64]{1,0:T(8,128)S(1)} %add_add_fusion.5), channel_id=1, source_target_pairs={{0,2},{1,3},{2,0},{3,1},{4,6},{5,7},{6,4},{7,5},{8,10},{9,11},{10,... | collective-permute-start | bytes 49160 | tf_op jit(solution)/shard_map/ppermute | solution.py:240
  113.9 5.0 %collective-permute-start.16 = (bf16[64,1024]{1,0:T(8,128)(2,1)S(1)}, bf16[64,1024]{1,0:T(8,128)(2,1)S(1)}, u32[]{:S(2)}, u32[]{:S(2)}) collective-permute-start(bf16[64,1024]{1,0:T(8,128)(2,1)S(1)} %get-tuple-element.34.own), channel_id=1, source_target_pairs={{0,1},{1,0},{2,3},{3,2},{4,5},{5,4},{6,7},{7,6},{8,9},{9,8},{10,11... | collective-permute-start | bytes 393224 | tf_op jit(solution)/shard_map/ppermute | solution.py:272
  120.2 9.0 %collective-permute-start.18 = (f32[64,1024]{1,0:T(8,128)S(1)}, f32[64,1024]{1,0:T(8,128)S(1)}, u32[]{:S(2)}, u32[]{:S(2)}) collective-permute-start(f32[64,1024]{1,0:T(8,128)S(1)} %shard_map.42), channel_id=1, source_target_pairs={{0,2},{1,7},{2,4},{3,1},{4,6},{5,3},{6,0},{7,5},{8,10},{9,15},{10,... | collective-permute-start | bytes 786440 | tf_op jit(solution)/shard_map/ppermute | solution.py:278
  121.4 7.8 %collective-permute-start.17 = (bf16[64,1024]{1,0:T(8,128)(2,1)S(1)}, bf16[64,1024]{1,0:T(8,128)(2,1)S(1)}, u32[]{:S(2)}, u32[]{:S(2)}) collective-permute-start(bf16[64,1024]{1,0:T(8,128)(2,1)S(1)} %get-tuple-element.34.own), channel_id=1, source_target_pairs={{2,0},{7,1},{4,2},{1,3},{6,4},{3,5},{0,6},{5,7},{10,8},{15,9},{12,... | collective-permute-start | bytes 393224 | tf_op jit(solution)/shard_map/ppermute | solution.py:275
  131.6 1.3 collective-permute-start.19
  132.9 4.9 %collective-permute-start.22 = (f32[64,64]{1,0:T(8,128)S(1)}, f32[64,64]{1,0:T(8,128)S(1)}, u32[]{:S(2)}, u32[]{:S(2)}) collective-permute-start(f32[64,64]{1,0:T(8,128)S(1)} %add.123), channel_id=1, source_target_pairs={{0,17},{1,16},{2,19},{3,18},{4,21},{5,20},{6,23},{7,22},{8,25},{9,... | collective-permute-start | bytes 49160 | tf_op jit(solution)/shard_map/ppermute | solution.py:240
  134.2 3.9 %collective-permute-start.21 = (f32[64,64]{1,0:T(8,128)S(1)}, f32[64,64]{1,0:T(8,128)S(1)}, u32[]{:S(2)}, u32[]{:S(2)}) collective-permute-start(f32[64,64]{1,0:T(8,128)S(1)} %add.123), channel_id=1, source_target_pairs={{0,1},{1,0},{2,3},{3,2},{4,5},{5,4},{6,7},{7,6},{8,9},{9,8},{10,11... | collective-permute-start | bytes 49160 | tf_op jit(solution)/shard_map/ppermute | solution.py:240
  134.9 3.9 %collective-permute-start.20 = (f32[64,64]{1,0:T(8,128)S(1)}, f32[64,64]{1,0:T(8,128)S(1)}, u32[]{:S(2)}, u32[]{:S(2)}) collective-permute-start(f32[64,64]{1,0:T(8,128)S(1)} %add.123), channel_id=1, source_target_pairs={{0,16},{1,17},{2,18},{3,19},{4,20},{5,21},{6,22},{7,23},{8,24},{9,... | collective-permute-start | bytes 49160 | tf_op jit(solution)/shard_map/ppermute | solution.py:240
  138.8 5.8 %collective-permute-start.25 = (f32[64,64]{1,0:T(8,128)S(1)}, f32[64,64]{1,0:T(8,128)S(1)}, u32[]{:S(2)}, u32[]{:S(2)}) collective-permute-start(f32[64,64]{1,0:T(8,128)S(1)} %add_add_fusion.3), channel_id=1, source_target_pairs={{0,6},{1,7},{2,4},{3,5},{4,2},{5,3},{6,0},{7,1},{8,14},{9,15},{10,... | collective-permute-start | bytes 49160 | tf_op jit(solution)/shard_map/ppermute | solution.py:240
  140.7 4.9 %collective-permute-start.24 = (f32[64,64]{1,0:T(8,128)S(1)}, f32[64,64]{1,0:T(8,128)S(1)}, u32[]{:S(2)}, u32[]{:S(2)}) collective-permute-start(f32[64,64]{1,0:T(8,128)S(1)} %add_add_fusion.3), channel_id=1, source_target_pairs={{0,4},{1,5},{2,6},{3,7},{4,0},{5,1},{6,2},{7,3},{8,12},{9,13},{10,... | collective-permute-start | bytes 49160 | tf_op jit(solution)/shard_map/ppermute | solution.py:240
  141.5 4.3 %collective-permute-start.23 = (f32[64,64]{1,0:T(8,128)S(1)}, f32[64,64]{1,0:T(8,128)S(1)}, u32[]{:S(2)}, u32[]{:S(2)}) collective-permute-start(f32[64,64]{1,0:T(8,128)S(1)} %add_add_fusion.3), channel_id=1, source_target_pairs={{0,2},{1,3},{2,0},{3,1},{4,6},{5,7},{6,4},{7,5},{8,10},{9,11},{10,... | collective-permute-start | bytes 49160 | tf_op jit(solution)/shard_map/ppermute | solution.py:240
  152.2 5.0 %collective-permute-start.26 = (bf16[64,1024]{1,0:T(8,128)(2,1)S(1)}, bf16[64,1024]{1,0:T(8,128)(2,1)S(1)}, u32[]{:S(2)}, u32[]{:S(2)}) collective-permute-start(bf16[64,1024]{1,0:T(8,128)(2,1)S(1)} %get-tuple-element.37.own), channel_id=1, source_target_pairs={{0,1},{1,0},{2,3},{3,2},{4,5},{5,4},{6,7},{7,6},{8,9},{9,8},{10,11... | collective-permute-start | bytes 393224 | tf_op jit(solution)/shard_map/ppermute | solution.py:272
  158.6 9.2 %collective-permute-start.28 = (f32[64,1024]{1,0:T(8,128)S(1)}, f32[64,1024]{1,0:T(8,128)S(1)}, u32[]{:S(2)}, u32[]{:S(2)}) collective-permute-start(f32[64,1024]{1,0:T(8,128)S(1)} %shard_map.45), channel_id=1, source_target_pairs={{0,2},{1,7},{2,4},{3,1},{4,6},{5,3},{6,0},{7,5},{8,10},{9,15},{10,... | collective-permute-start | bytes 786440 | tf_op jit(solution)/shard_map/ppermute | solution.py:278
  160.0 7.8 %collective-permute-start.27 = (bf16[64,1024]{1,0:T(8,128)(2,1)S(1)}, bf16[64,1024]{1,0:T(8,128)(2,1)S(1)}, u32[]{:S(2)}, u32[]{:S(2)}) collective-permute-start(bf16[64,1024]{1,0:T(8,128)(2,1)S(1)} %get-tuple-element.37.own), channel_id=1, source_target_pairs={{2,0},{7,1},{4,2},{1,3},{6,4},{3,5},{0,6},{5,7},{10,8},{15,9},{12,... | collective-permute-start | bytes 393224 | tf_op jit(solution)/shard_map/ppermute | solution.py:275
  170.2 1.3 collective-permute-start.29
  171.5 5.0 %collective-permute-start.32 = (f32[64,64]{1,0:T(8,128)S(1)}, f32[64,64]{1,0:T(8,128)S(1)}, u32[]{:S(2)}, u32[]{:S(2)}) collective-permute-start(f32[64,64]{1,0:T(8,128)S(1)} %add.130), channel_id=1, source_target_pairs={{0,17},{1,16},{2,19},{3,18},{4,21},{5,20},{6,23},{7,22},{8,25},{9,... | collective-permute-start | bytes 49160 | tf_op jit(solution)/shard_map/ppermute | solution.py:240
  173.7 3.9 %collective-permute-start.31 = (f32[64,64]{1,0:T(8,128)S(1)}, f32[64,64]{1,0:T(8,128)S(1)}, u32[]{:S(2)}, u32[]{:S(2)}) collective-permute-start(f32[64,64]{1,0:T(8,128)S(1)} %add.130), channel_id=1, source_target_pairs={{0,1},{1,0},{2,3},{3,2},{4,5},{5,4},{6,7},{7,6},{8,9},{9,8},{10,11... | collective-permute-start | bytes 49160 | tf_op jit(solution)/shard_map/ppermute | solution.py:240
  174.5 3.9 %collective-permute-start.30 = (f32[64,64]{1,0:T(8,128)S(1)}, f32[64,64]{1,0:T(8,128)S(1)}, u32[]{:S(2)}, u32[]{:S(2)}) collective-permute-start(f32[64,64]{1,0:T(8,128)S(1)} %add.130), channel_id=1, source_target_pairs={{0,16},{1,17},{2,18},{3,19},{4,20},{5,21},{6,22},{7,23},{8,24},{9,... | collective-permute-start | bytes 49160 | tf_op jit(solution)/shard_map/ppermute | solution.py:240
  178.4 5.8 %collective-permute-start.35 = (f32[64,64]{1,0:T(8,128)S(1)}, f32[64,64]{1,0:T(8,128)S(1)}, u32[]{:S(2)}, u32[]{:S(2)}) collective-permute-start(f32[64,64]{1,0:T(8,128)S(1)} %add_add_fusion.1), channel_id=1, source_target_pairs={{0,6},{1,7},{2,4},{3,5},{4,2},{5,3},{6,0},{7,1},{8,14},{9,15},{10,... | collective-permute-start | bytes 49160 | tf_op jit(solution)/shard_map/ppermute | solution.py:240
  180.3 4.8 %collective-permute-start.34 = (f32[64,64]{1,0:T(8,128)S(1)}, f32[64,64]{1,0:T(8,128)S(1)}, u32[]{:S(2)}, u32[]{:S(2)}) collective-permute-start(f32[64,64]{1,0:T(8,128)S(1)} %add_add_fusion.1), channel_id=1, source_target_pairs={{0,4},{1,5},{2,6},{3,7},{4,0},{5,1},{6,2},{7,3},{8,12},{9,13},{10,... | collective-permute-start | bytes 49160 | tf_op jit(solution)/shard_map/ppermute | solution.py:240
  180.8 4.3 %collective-permute-start.33 = (f32[64,64]{1,0:T(8,128)S(1)}, f32[64,64]{1,0:T(8,128)S(1)}, u32[]{:S(2)}, u32[]{:S(2)}) collective-permute-start(f32[64,64]{1,0:T(8,128)S(1)} %add_add_fusion.1), channel_id=1, source_target_pairs={{0,2},{1,3},{2,0},{3,1},{4,6},{5,7},{6,4},{7,5},{8,10},{9,11},{10,... | collective-permute-start | bytes 49160 | tf_op jit(solution)/shard_map/ppermute | solution.py:240

commit v4 on v3

--- a/solution.py
+++ b/solution.py
@@ -183,19 +183,26 @@
     out[:, span(1, size)] = apart(kept(mask, 1, 0, own, x), far1[...])
 
 
-def own_rows_body(mask, own, x, z, given, root, near0, near1, far0, far1, image, gram):
+def near_rows_body(mask, own, x, z, near0, near1, far0, far1, out):
     size = own.shape[1] // BLK_DEV
     cut = near0.shape[0]
     for m in range(BLK_DEV):
         there = span(m, size)
         left = kept(mask, m, 0, own, x)
         side = kept(mask, m, 2 * BLK_DEV, z)
-        total = given[:, there] + apart(left[:, :cut], near0[:, there])
-        total += apart(left[:, cut:], near1[:, there])
+        total = apart(left[:, :cut], near0[:, there]) + apart(left[:, cut:], near1[:, there])
         total += cross(side[:, :size], far0[there, :]) + cross(side[:, size:], far1[there, :])
-        image[:, there] = total * root[:, there]
-    full = image[...]
+        out[:, there] = total
+
+
+def join_body(near, given, root, image, ahead, gram):
+    full = (near[...] + given[...]) * root[...]
+    image[...] = full
+    ahead[...] = full * root[...]
     gram[...] = cross(full, full, precision=EXACT)
+
+
+GROUP = 8
 
 
 def inverse_factor(gram):
@@ -203,27 +210,42 @@
     rows = lax.broadcasted_iota(jnp.int32, (size, 2 * size), 0)
     lanes = lax.broadcasted_iota(jnp.int32, (size, 2 * size), 1)
     unit = jnp.where(rows + size == lanes, 1.0, 0.0).astype(F32)
-    work = jnp.concatenate([gram, unit[:, size:]], axis=1)
-    for j in range(size):
-        pivot_row = work[j : j + 1, :]
-        scale = 1.0 / pivot_row[:, j : j + 1]
-        factor = jnp.where(rows[:, :1] > j, work[:, j : j + 1] * scale, 0.0)
-        work = work - factor * pivot_row
-    diagonal = jnp.sum(jnp.where(rows == lanes, work, 0.0), axis=1, keepdims=True)
-    return work[:, size:] * lax.rsqrt(diagonal)
-
-
-def solve_body(scale, gram, image, root, out, scaled):
-    factor = inverse_factor(gram[...])
-    vectors = jnp.dot(factor, image[...], preferred_element_type=F32, precision=EXACT) * scale
-    out[...] = vectors
-    scaled[...] = (vectors * root[...]).astype(BF16)
+    live = jnp.concatenate([gram, unit[:, size:]], axis=1)
+    finished = []
+    for first in range(0, size, GROUP):
+        cols = [
+            jnp.broadcast_to(live[:, first + b : first + b + 1], live.shape) for b in range(GROUP)
+        ]
+        lines = [live[a : a + 1, :] for a in range(GROUP)]
+        pivots = {(a, b): cols[b][a : a + 1, :] for a in range(GROUP) for b in range(a, GROUP)}
+        change = jnp.zeros_like(live)
+        for a in range(GROUP):
+            inverse = 1.0 / pivots[a, a]
+            for b in range(a + 1, GROUP):
+                ratio = pivots[a, b] * inverse
+                lines[b] = lines[b] - ratio * lines[a]
+                cols[b] = cols[b] - ratio * cols[a]
+                for c in range(b, GROUP):
+                    pivots[b, c] = pivots[b, c] - ratio * pivots[a, c]
+            change += cols[a] * inverse * lines[a]
+            finished.append(lines[a] * lax.rsqrt(pivots[a, a]))
+        if first + GROUP < size:
+            live = (live - change)[GROUP:, :]
+    return jnp.concatenate(finished, axis=0)[:, size:]
+
+
+def solve_body(scale, gram, *refs):
+    factor = inverse_factor(gram[...]) * scale
+    count = len(refs) // 2
+    for value, out in zip(refs[:count], refs[count:]):
+        solved = jnp.dot(factor, value[...], preferred_element_type=F32, precision=EXACT)
+        out[...] = solved.astype(out.dtype)
 
 
 def exchange_masks(row_count, col_count):
     low = [1 << bit for bit in range(col_count.bit_length() - 1)]
     high = [col_count << bit for bit in range(row_count.bit_length() - 1)]
-    stages = [(high[0],), (high[1], low[0]), (low[1], low[2])]
+    stages = [(high[0], low[0]), (high[1],), (low[1], low[2])]
     rest = high[2:] + low[3:]
     return stages + [tuple(rest[at : at + 2]) for at in range(0, len(rest), 2)]
 
@@ -318,27 +340,36 @@
 
     across_shape = (columns, points)
     work = 2 * columns * size * size
-    far_rows = call(
-        far_rows_body, shaped(across_shape, F32), [SMEM] + [VMEM] * 5, 8 * work, 8 * work // 64
+    wide = shaped(across_shape, F32)
+    far_rows = call(far_rows_body, wide, [SMEM] + [VMEM] * 5, 8 * work, 8 * work // 64)
+    near_rows = call(near_rows_body, wide, [SMEM] + [VMEM] * 7, 12 * work, 12 * work // 64)
+    join = call(
+        join_body,
+        (wide, wide, shaped((columns, columns), F32)),
+        [VMEM] * 3, 2 * columns * columns * points, 4 * columns * points,
     )
-    own_rows = call(
-        own_rows_body,
-        (shaped(across_shape, F32), shaped((columns, columns), F32)),
-        [SMEM] + [VMEM] * 9, 12 * work, 12 * work // 64,
-    )
-    solve = call(
-        functools.partial(solve_body, math.sqrt(total_rows)),
-        (shaped(across_shape, F32), shaped(across_shape, BF16)),
-        [VMEM] * 3, 4 * columns * columns * points, 4 * columns * points,
-    )
-    vectors = start_vectors.T
-    scaled = (vectors * root).astype(BF16)
-    for _ in range(ITERS):
-        x = from_x(scaled)
-        z = from_z(scaled)
-        given = to_z(far_rows(far_mask, scaled, x, far0, corner, far1))
-        image, gram = own_rows(own_mask, scaled, x, z, given, root, near0, near1, far0, far1)
-        vectors, scaled = solve(total_sum(gram), image, root)
+
+    def solve(dtype, gram, *values):
+        return call(
+            functools.partial(solve_body, math.sqrt(total_rows)),
+            tuple(shaped(across_shape, dtype) for _ in values),
+            [VMEM] * (1 + len(values)),
+            4 * columns * columns * points, 4 * columns * points,
+        )(gram, *values)
+
+    own = (start_vectors.T * root).astype(BF16)
+    x = from_x(own)
+    z = from_z(own)
+    for iteration in range(ITERS):
+        sent = far_rows(far_mask, own, x, far0, corner, far1)
+        given = to_z(sent)
+        held = near_rows(own_mask, own, x, z, near0, near1, far0, far1)
+        image, ahead, gram = join(held, given, root)
+        if iteration < ITERS - 1:
+            ahead_x, ahead_z = from_x(ahead), from_z(ahead)
+            total = total_sum(gram)
+            own, x, z = solve(BF16, total, ahead, ahead_x, ahead_z)
+    (vectors,) = solve(F32, total_sum(gram), image)
     return vectors.T
 
 

time: 192 us -> 167 us (0.87)
  waiting for transfers between devices: 88.5 us -> 77.2 us
  Pallas kernels: 50.2 us -> 39.6 us
  starting transfers between devices: 50 us -> 46.9 us
    pallas_call x9 -> x12, Pallas kernels: 30.7 us -> 20 us  [the longest x3 7.38 us: solve(): call(functools.partial(solve_body, math.sqrt(total_rows)), tuple((shaped(...]
    ppermute x6, waiting for transfers between devices: 48.6 us -> 38.2 us  [from_z(): lax.ppermute(value, 'col', [(side_of(i), i) for i in range(col_count)])]
    ppermute x4, waiting for transfers between devices: 7.47 us -> 15.5 us  [to_z(): lax.ppermute(value, 'col', [(i, side_of(i)) for i in range(col_count)])]
    ppermute x5, waiting for transfers between devices: 12.1 us -> 4.96 us  [from_x(): return lax.ppermute(value, 'col', [(i, i ^ 1) for i in range(col_count)])]
    ppermute x6, starting transfers between devices: 19.6 us -> 17.2 us  [from_z(): lax.ppermute(value, 'col', [(side_of(i), i) for i in range(col_count)])]
    ppermute x5, starting transfers between devices: 3.28 us -> 1.11 us  [from_x(): return lax.ppermute(value, 'col', [(i, i ^ 1) for i in range(col_count)])]
  transfers between devices with their start and end apart: 36 -> 36, of which waited for: 28 -> 19; matrix products, arithmetic and copies ran while one was open for 1% -> 1% of each run, Pallas kernels for 5% -> 10%
where the time goes in v4:
time: 167 us
  waiting for transfers between devices  77.2 us (46%)
  starting transfers between devices  46.9 us (28%)
  Pallas kernels  39.6 us (24%)
  local copies, waits for them, and re-layouts  2.12 us (1%)
    ppermute x6, waiting for transfers between devices, from_z(): lax.ppermute(value, 'col', [(side_of(i), i) for i in range(col_count)])  38.2 us
    ppermute x21, starting transfers between devices, fetched(): return lax.ppermute(value, ('row', 'col'), pairs)  25.7 us
    ppermute x21, waiting for transfers between devices, fetched(): return lax.ppermute(value, ('row', 'col'), pairs)  18.6 us
    ppermute x6, starting transfers between devices, from_z(): lax.ppermute(value, 'col', [(side_of(i), i) for i in range(col_count)])  17.2 us
    ppermute x4, waiting for transfers between devices, to_z(): lax.ppermute(value, 'col', [(i, side_of(i)) for i in range(col_count)])  15.5 us
    pallas_call x3, Pallas kernels, solve(): call(functools.partial(solve_body, math.sqrt(total_rows)), tuple((shaped(...  7.38 us
    pallas_call x1, Pallas kernels, on_device(): call(first_tiles_body, (shaped((most * size, points), BF16), shaped((most...  7.16 us
    pallas_call x1, Pallas kernels, on_device(): call(last_tiles_body, (shaped((size, points), BF16), shaped((size, size),...  6.54 us
  transfers between devices with their start and end apart: 36, of which 19 were waited for; matrix products, arithmetic and copies ran while one was open for 1% of the time, Pallas kernels for 10%

profile of v4, /device:TPU:0, one launch (start us, length us, event | category | flops | bytes accessed | tf_op | source)
XLA Modules:
  0.0 166.5 jit_solution(10206145183971765330)
XLA Ops:
  0.0 3.0 %unit_rows.2.b0 = bf16[512,1024]{1,0:T(8,128)(2,1)} custom-call(f32[1024,1024]{1,0:T(8,128)} %points_ref.3), custom_call_target="tpu_custom_call" | custom-call | flops 1572864 | bytes 3145728 | tf_op jit(solution)/shard_map/unit_rows/pallas_call | solution.py:69
  3.0 5.1 %collective-permute-start.3 = (bf16[512,1024]{1,0:T(8,128)(2,1)}, bf16[512,1024]{1,0:T(8,128)(2,1)S(1)}, u32[]{:S(2)}, u32[]{:S(2)}) collective-permute-start(bf16[512,1024]{1,0:T(8,128)(2,1)} %unit_rows.2.b0), channel_id=1, source_target_pairs={{2,0},{7,1},{4,2},{1,3},{6,4},{3,5},{0,6},{5,7},{10,8},{15,9},{12,... | collective-permute-start | bytes 3145736 | tf_op jit(solution)/shard_map/ppermute | solution.py:297
  8.1 2.9 %unit_rows.3.b1 = bf16[512,1024]{1,0:T(8,128)(2,1)} custom-call(f32[1024,1024]{1,0:T(8,128)} %points_ref.3), custom_call_target="tpu_custom_call" | custom-call | flops 1572864 | bytes 3145728 | tf_op jit(solution)/shard_map/unit_rows/pallas_call | solution.py:69
  11.0 1.8 %collective-permute-start.4 = (bf16[512,1024]{1,0:T(8,128)(2,1)}, bf16[512,1024]{1,0:T(8,128)(2,1)}, u32[]{:S(2)}, u32[]{:S(2)}) collective-permute-start(bf16[512,1024]{1,0:T(8,128)(2,1)} %unit_rows.3.b1), channel_id=1, source_target_pairs={{2,0},{7,1},{4,2},{1,3},{6,4},{3,5},{0,6},{5,7},{10,8},{15,9},{12,... | collective-permute-start | bytes 3145736 | tf_op jit(solution)/shard_map/ppermute | solution.py:297
  13.2 3.7 %collective-permute-start = (s32[2,12]{1,0:T(2,128)S(1)}, s32[2,12]{1,0:T(2,128)S(1)}, u32[]{:S(2)}, u32[]{:S(2)}) collective-permute-start(s32[2,12]{1,0:T(2,128)S(1)} %copy-done.4), channel_id=1, source_target_pairs={{2,0},{7,1},{4,2},{1,3},{6,4},{3,5},{0,6},{5,7},{10,8},{15,9},{12,... | collective-permute-start | bytes 296 | tf_op jit(solution)/shard_map/ppermute | solution.py:297
  17.7 35.6 %collective-permute-done = s32[2,12]{1,0:T(2,128)S(1)} collective-permute-done((s32[2,12]{1,0:T(2,128)S(1)}, s32[2,12]{1,0:T(2,128)S(1)}, u32[]{:S(2)}, u32[]{:S(2)}) %collective-permute-start) | collective-permute-done | bytes 128 | tf_op jit(solution)/shard_map/ppermute | solution.py:297
  53.8 1.2 copy-done.1
  55.0 7.2 %shard_map.37 = (bf16[1536,1024]{1,0:T(8,128)(2,1)S(1)}, bf16[1536,512]{1,0:T(8,128)(2,1)S(1)}, f32[1,1024]{1,0:T(1,128)S(1)}, f32[3,512]{1,0:T(4,128)S(1)}) custom-call(f32[2,6]{1,0:T(2,128)S(1)} %or_convert_fusion.1.own_mask.mask, bf16[512,1024]{1,0:T(8,128)(2,1)S(1)} %copy-done, bf16[512,1024]{1,0:T(8,128)(2,1)S(1)} %copy-done.1, ...), custom_call_target="tpu_custom_call" | custom-call | flops 4831838208 | bytes 18874368 | tf_op jit(solution)/shard_map/pallas_call | solution.py:323
  62.2 6.5 %shard_map.38 = (bf16[512,1024]{1,0:T(8,128)(2,1)S(1)}, bf16[512,512]{1,0:T(8,128)(2,1)S(1)}, bf16[2048,512]{1,0:T(8,128)(2,1)S(1)}, f32[1,1024]{1,0:T(1,128)S(1)}, f32[1,1024]{1,0:T(1,128)S(1)}) custom-call(f32[2,6]{1,0:T(2,128)S(1)} %or_convert_fusion.1.own_mask.mask, f32[2,4]{1,0:T(2,128)S(1)} %or_convert_fusion.far_mask.mask, ...), custom_call_target="tpu_custom_call" | custom-call | flops 3758096384 | bytes 14680064 | tf_op jit(solution)/shard_map/pallas_call | solution.py:331
  69.3 5.4 %collective-permute-done.5 = f32[1,1024]{1,0:T(1,128)S(1)} collective-permute-done((f32[1,1024]{1,0:T(1,128)S(1)}, f32[1,1024]{1,0:T(1,128)S(1)}, u32[]{:S(2)}, u32[]{:S(2)}) %collective-permute-start.5) | collective-permute-done | bytes 4128 | tf_op jit(solution)/shard_map/ppermute | solution.py:300
  74.8 5.0 %collective-permute-done.6.x = bf16[64,1024]{1,0:T(8,128)(2,1)S(1)} collective-permute-done((bf16[64,1024]{1,0:T(8,128)(2,1)S(1)}, bf16[64,1024]{1,0:T(8,128)(2,1)S(1)}, u32[]{:S(2)}, u32[]{:S(2)}) %collective-permute-start.6) | collective-permute-done | bytes 131104 | tf_op jit(solution)/shard_map/ppermute | solution.py:294
  79.8 1.4 shard_map.40
  81.2 3.8 %collective-permute-start.7 = (bf16[64,1024]{1,0:T(8,128)(2,1)S(1)}, bf16[64,1024]{1,0:T(8,128)(2,1)S(1)}, u32[]{:S(2)}, u32[]{:S(2)}) collective-permute-start(bf16[64,1024]{1,0:T(8,128)(2,1)S(1)} %fusion.own), channel_id=1, source_target_pairs={{2,0},{7,1},{4,2},{1,3},{6,4},{3,5},{0,6},{5,7},{10,8},{15,9},{12,... | collective-permute-start | bytes 393224 | tf_op jit(solution)/shard_map/ppermute | solution.py:297
  85.1 2.5 %collective-permute-done.7.z = bf16[64,1024]{1,0:T(8,128)(2,1)S(1)} collective-permute-done((bf16[64,1024]{1,0:T(8,128)(2,1)S(1)}, bf16[64,1024]{1,0:T(8,128)(2,1)S(1)}, u32[]{:S(2)}, u32[]{:S(2)}) %collective-permute-start.7) | collective-permute-done | bytes 131104 | tf_op jit(solution)/shard_map/ppermute | solution.py:297
  87.6 2.0 %shard_map.39.near = f32[64,1024]{1,0:T(8,128)S(1)} custom-call(f32[2,6]{1,0:T(2,128)S(1)} %or_convert_fusion.1.own_mask.mask, bf16[64,1024]{1,0:T(8,128)(2,1)S(1)} %fusion.own, bf16[64,1024]{1,0:T(8,128)(2,1)S(1)} %collective-permute-done.6.x, bf16[64,1024]{1,0:T(8,128)(2,1)S(1)} %collective-permute-done.7.z, ...), custom_call_target="tpu_custom_call" | custom-call | flops 402653184 | bytes 6291456 | tf_op jit(solution)/shard_map/pallas_call | solution.py:366
  89.6 0.8 shard_map.41
  90.4 3.9 %collective-permute-start.10 = (f32[64,64]{1,0:T(8,128)S(1)}, f32[64,64]{1,0:T(8,128)S(1)}, u32[]{:S(2)}, u32[]{:S(2)}) collective-permute-start(f32[64,64]{1,0:T(8,128)S(1)} %get-tuple-element.35), channel_id=1, source_target_pairs={{0,1},{1,0},{2,3},{3,2},{4,5},{5,4},{6,7},{7,6},{8,9},{9,8},{10,11... | collective-permute-start | bytes 49160 | tf_op jit(solution)/shard_map/ppermute | solution.py:262
  94.5 2.1 %collective-permute-start.17 = (f32[64,1024]{1,0:T(8,128)S(1)}, f32[64,1024]{1,0:T(8,128)S(1)}, u32[]{:S(2)}, u32[]{:S(2)}) collective-permute-start(f32[64,1024]{1,0:T(8,128)S(1)} %get-tuple-element.36.refs_0_), channel_id=1, source_target_pairs={{2,0},{7,1},{4,2},{1,3},{6,4},{3,5},{0,6},{5,7},{10,8},{15,9},{12,... | collective-permute-start | bytes 786440 | tf_op jit(solution)/shard_map/ppermute | solution.py:297
  97.3 1.6 collective-permute-start.12
  98.8 2.4 %collective-permute-done.12 = f32[64,64]{1,0:T(8,128)S(1)} collective-permute-done((f32[64,64]{1,0:T(8,128)S(1)}, f32[64,64]{1,0:T(8,128)S(1)}, u32[]{:S(2)}, u32[]{:S(2)}) %collective-permute-start.12) | collective-permute-done | bytes 16416 | tf_op jit(solution)/shard_map/ppermute | solution.py:262
  101.2 2.8 %collective-permute-start.15 = (f32[64,64]{1,0:T(8,128)S(1)}, f32[64,64]{1,0:T(8,128)S(1)}, u32[]{:S(2)}, u32[]{:S(2)}) collective-permute-start(f32[64,64]{1,0:T(8,128)S(1)} %add.119), channel_id=1, source_target_pairs={{0,6},{1,7},{2,4},{3,5},{4,2},{5,3},{6,0},{7,1},{8,14},{9,15},{10,... | collective-permute-start | bytes 49160 | tf_op jit(solution)/shard_map/ppermute | solution.py:262
  104.1 1.6 collective-permute-start.13
  105.6 1.3 collective-permute-done.15
  107.0 1.9 %collective-permute-done.14 = f32[64,64]{1,0:T(8,128)S(1)} collective-permute-done((f32[64,64]{1,0:T(8,128)S(1)}, f32[64,64]{1,0:T(8,128)S(1)}, u32[]{:S(2)}, u32[]{:S(2)}) %collective-permute-start.14) | collective-permute-done | bytes 16416 | tf_op jit(solution)/shard_map/ppermute | solution.py:262
  108.9 2.4 %shard_map.42 = (bf16[64,1024]{1,0:T(8,128)(2,1)S(1)}, bf16[64,1024]{1,0:T(8,128)(2,1)S(1)}, bf16[64,1024]{1,0:T(8,128)(2,1)S(1)}) custom-call(f32[64,64]{1,0:T(8,128)S(1)} %add_add_fusion.4.gram, f32[64,1024]{1,0:T(8,128)S(1)} %get-tuple-element.36.refs_0_, f32[64,1024]{1,0:T(8,128)S(1)} %collective-permute-done.16.refs_1_, ...), custom_call_target="tpu_custom_call" | custom-call | flops 16777216 | bytes 262144 | tf_op jit(solution)/shard_map/pallas_call | solution.py:353
  111.3 1.4 shard_map.44
  113.4 2.0 %shard_map.43.near = f32[64,1024]{1,0:T(8,128)S(1)} custom-call(f32[2,6]{1,0:T(2,128)S(1)} %or_convert_fusion.1.own_mask.mask, bf16[64,1024]{1,0:T(8,128)(2,1)S(1)} %get-tuple-element.37.own, bf16[64,1024]{1,0:T(8,128)(2,1)S(1)} %get-tuple-element.38.x, bf16[64,1024]{1,0:T(8,128)(2,1)S(1)} %get-tuple-element.39.z, ...), custom_call_target="tpu_custom_call" | custom-call | flops 402653184 | bytes 6291456 | tf_op jit(solution)/shard_map/pallas_call | solution.py:366
  115.4 5.5 %collective-permute-done.18.given = f32[64,1024]{1,0:T(8,128)S(1)} collective-permute-done((f32[64,1024]{1,0:T(8,128)S(1)}, f32[64,1024]{1,0:T(8,128)S(1)}, u32[]{:S(2)}, u32[]{:S(2)}) %collective-permute-start.18) | collective-permute-done | bytes 262176 | tf_op jit(solution)/shard_map/ppermute | solution.py:300
  121.7 1.9 %collective-permute-start.19 = (f32[64,64]{1,0:T(8,128)S(1)}, f32[64,64]{1,0:T(8,128)S(1)}, u32[]{:S(2)}, u32[]{:S(2)}) collective-permute-start(f32[64,64]{1,0:T(8,128)S(1)} %get-tuple-element.40), channel_id=1, source_target_pairs={{0,8},{1,9},{2,10},{3,11},{4,12},{5,13},{6,14},{7,15},{8,0},{9,1},... | collective-permute-start | bytes 49160 | tf_op jit(solution)/shard_map/ppermute | solution.py:262
  124.2 0.8 collective-permute-done.21
  125.8 1.6 collective-permute-start.22
  127.4 2.4 %collective-permute-done.22 = f32[64,64]{1,0:T(8,128)S(1)} collective-permute-done((f32[64,64]{1,0:T(8,128)S(1)}, f32[64,64]{1,0:T(8,128)S(1)}, u32[]{:S(2)}, u32[]{:S(2)}) %collective-permute-start.22) | collective-permute-done | bytes 16416 | tf_op jit(solution)/shard_map/ppermute | solution.py:262
  129.7 1.9 %collective-permute-start.25 = (f32[64,64]{1,0:T(8,128)S(1)}, f32[64,64]{1,0:T(8,128)S(1)}, u32[]{:S(2)}, u32[]{:S(2)}) collective-permute-start(f32[64,64]{1,0:T(8,128)S(1)} %add.126), channel_id=1, source_target_pairs={{0,6},{1,7},{2,4},{3,5},{4,2},{5,3},{6,0},{7,1},{8,14},{9,15},{10,... | collective-permute-start | bytes 49160 | tf_op jit(solution)/shard_map/ppermute | solution.py:262
  131.7 2.4 %collective-permute-start.23 = (f32[64,64]{1,0:T(8,128)S(1)}, f32[64,64]{1,0:T(8,128)S(1)}, u32[]{:S(2)}, u32[]{:S(2)}) collective-permute-start(f32[64,64]{1,0:T(8,128)S(1)} %add.126), channel_id=1, source_target_pairs={{0,2},{1,3},{2,0},{3,1},{4,6},{5,7},{6,4},{7,5},{8,10},{9,11},{10,... | collective-permute-start | bytes 49160 | tf_op jit(solution)/shard_map/ppermute | solution.py:262
  134.1 1.7 %collective-permute-done.25 = f32[64,64]{1,0:T(8,128)S(1)} collective-permute-done((f32[64,64]{1,0:T(8,128)S(1)}, f32[64,64]{1,0:T(8,128)S(1)}, u32[]{:S(2)}, u32[]{:S(2)}) %collective-permute-start.25) | collective-permute-done | bytes 16416 | tf_op jit(solution)/shard_map/ppermute | solution.py:262
  136.5 2.4 %shard_map.46 = (bf16[64,1024]{1,0:T(8,128)(2,1)S(1)}, bf16[64,1024]{1,0:T(8,128)(2,1)S(1)}, bf16[64,1024]{1,0:T(8,128)(2,1)S(1)}) custom-call(f32[64,64]{1,0:T(8,128)S(1)} %add_add_fusion.2.gram, f32[64,1024]{1,0:T(8,128)S(1)} %get-tuple-element.41.refs_0_, f32[64,1024]{1,0:T(8,128)S(1)} %collective-permute-done.26.refs_1_, ...), custom_call_target="tpu_custom_call" | custom-call | flops 16777216 | bytes 262144 | tf_op jit(solution)/shard_map/pallas_call | solution.py:353
  138.9 1.4 shard_map.48
  140.3 1.6 collective-permute-start.28
  141.9 2.0 %shard_map.47.near = f32[64,1024]{1,0:T(8,128)S(1)} custom-call(f32[2,6]{1,0:T(2,128)S(1)} %or_convert_fusion.1.own_mask.mask, bf16[64,1024]{1,0:T(8,128)(2,1)S(1)} %get-tuple-element.42.own, bf16[64,1024]{1,0:T(8,128)(2,1)S(1)} %get-tuple-element.43.x, bf16[64,1024]{1,0:T(8,128)(2,1)S(1)} %get-tuple-element.44.z, ...), custom_call_target="tpu_custom_call" | custom-call | flops 402653184 | bytes 6291456 | tf_op jit(solution)/shard_map/pallas_call | solution.py:366
  143.9 4.6 %collective-permute-done.28.given = f32[64,1024]{1,0:T(8,128)S(1)} collective-permute-done((f32[64,1024]{1,0:T(8,128)S(1)}, f32[64,1024]{1,0:T(8,128)S(1)}, u32[]{:S(2)}, u32[]{:S(2)}) %collective-permute-start.28) | collective-permute-done | bytes 262176 | tf_op jit(solution)/shard_map/ppermute | solution.py:300
  149.4 1.9 %collective-permute-start.29 = (f32[64,64]{1,0:T(8,128)S(1)}, f32[64,64]{1,0:T(8,128)S(1)}, u32[]{:S(2)}, u32[]{:S(2)}) collective-permute-start(f32[64,64]{1,0:T(8,128)S(1)} %get-tuple-element.45), channel_id=1, source_target_pairs={{0,8},{1,9},{2,10},{3,11},{4,12},{5,13},{6,14},{7,15},{8,0},{9,1},... | collective-permute-start | bytes 49160 | tf_op jit(solution)/shard_map/ppermute | solution.py:262
  151.2 1.5 collective-permute-done.31
  153.4 1.6 collective-permute-start.32
  155.0 2.4 %collective-permute-done.32 = f32[64,64]{1,0:T(8,128)S(1)} collective-permute-done((f32[64,64]{1,0:T(8,128)S(1)}, f32[64,64]{1,0:T(8,128)S(1)}, u32[]{:S(2)}, u32[]{:S(2)}) %collective-permute-start.32) | collective-permute-done | bytes 16416 | tf_op jit(solution)/shard_map/ppermute | solution.py:262
  157.4 0.9 collective-permute-start.35
  158.6 3.2 %collective-permute-start.33 = (f32[64,64]{1,0:T(8,128)S(1)}, f32[64,64]{1,0:T(8,128)S(1)}, u32[]{:S(2)}, u32[]{:S(2)}) collective-permute-start(f32[64,64]{1,0:T(8,128)S(1)} %add.133), channel_id=1, source_target_pairs={{0,2},{1,3},{2,0},{3,1},{4,6},{5,7},{6,4},{7,5},{8,10},{9,11},{10,... | collective-permute-start | bytes 49160 | tf_op jit(solution)/shard_map/ppermute | solution.py:262
  161.8 1.5 collective-permute-done.35
  163.9 2.7 %shard_map.50 = f32[64,1024]{1,0:T(8,128)} custom-call(f32[64,64]{1,0:T(8,128)S(1)} %add_add_fusion.gram, f32[64,1024]{1,0:T(8,128)S(1)} %get-tuple-element.46.refs_0_), custom_call_target="tpu_custom_call" | custom-call | flops 16777216 | bytes 262144 | tf_op jit(solution)/shard_map/pallas_call | solution.py:353
  (70 shorter events, 9.2 us)
Async XLA Ops:
  3.0 10.2 %copy-start.4 = (s32[2,12]{1,0:T(2,128)S(1)}, s32[2,12]{1,0:T(2,128)}, u32[]{:S(2)}) copy-start(s32[2,12]{1,0:T(2,128)} %param.4) | copy-start | bytes 292
  3.0 50.8 %copy-start = (bf16[512,1024]{1,0:T(8,128)(2,1)S(1)}, bf16[512,1024]{1,0:T(8,128)(2,1)}, u32[]{:S(2)}) copy-start(bf16[512,1024]{1,0:T(8,128)(2,1)} %unit_rows.2.b0) | copy-start | bytes 3145732
  3.0 50.8 %collective-permute-start.3 = (bf16[512,1024]{1,0:T(8,128)(2,1)}, bf16[512,1024]{1,0:T(8,128)(2,1)S(1)}, u32[]{:S(2)}, u32[]{:S(2)}) collective-permute-start(bf16[512,1024]{1,0:T(8,128)(2,1)} %unit_rows.2.b0), channel_id=1, source_target_pairs={{2,0},{7,1},{4,2},{1,3},{6,4},{3,5},{0,6},{5,7},{10,8},{15,9},{12,... | collective-permute-start | bytes 3145736 | tf_op jit(solution)/shard_map/ppermute | solution.py:297
  8.1 45.7 %collective-permute-start.1 = (bf16[512,1024]{1,0:T(8,128)(2,1)}, bf16[512,1024]{1,0:T(8,128)(2,1)}, u32[]{:S(2)}, u32[]{:S(2)}) collective-permute-start(bf16[512,1024]{1,0:T(8,128)(2,1)} %unit_rows.2.b0), channel_id=1, source_target_pairs={{0,1},{1,0},{2,3},{3,2},{4,5},{5,4},{6,7},{7,6},{8,9},{9,8},{10,11... | collective-permute-start | bytes 3145736 | tf_op jit(solution)/shard_map/ppermute | solution.py:294
  11.0 51.2 %collective-permute-start.4 = (bf16[512,1024]{1,0:T(8,128)(2,1)}, bf16[512,1024]{1,0:T(8,128)(2,1)}, u32[]{:S(2)}, u32[]{:S(2)}) collective-permute-start(bf16[512,1024]{1,0:T(8,128)(2,1)} %unit_rows.3.b1), channel_id=1, source_target_pairs={{2,0},{7,1},{4,2},{1,3},{6,4},{3,5},{0,6},{5,7},{10,8},{15,9},{12,... | collective-permute-start | bytes 3145736 | tf_op jit(solution)/shard_map/ppermute | solution.py:297
  12.8 49.4 %collective-permute-start.2 = (bf16[512,1024]{1,0:T(8,128)(2,1)}, bf16[512,1024]{1,0:T(8,128)(2,1)}, u32[]{:S(2)}, u32[]{:S(2)}) collective-permute-start(bf16[512,1024]{1,0:T(8,128)(2,1)} %unit_rows.3.b1), channel_id=1, source_target_pairs={{0,1},{1,0},{2,3},{3,2},{4,5},{5,4},{6,7},{7,6},{8,9},{9,8},{10,11... | collective-permute-start | bytes 3145736 | tf_op jit(solution)/shard_map/ppermute | solution.py:294
  13.2 40.2 %collective-permute-start = (s32[2,12]{1,0:T(2,128)S(1)}, s32[2,12]{1,0:T(2,128)S(1)}, u32[]{:S(2)}, u32[]{:S(2)}) collective-permute-start(s32[2,12]{1,0:T(2,128)S(1)} %copy-done.4), channel_id=1, source_target_pairs={{2,0},{7,1},{4,2},{1,3},{6,4},{3,5},{0,6},{5,7},{10,8},{15,9},{12,... | collective-permute-start | bytes 296 | tf_op jit(solution)/shard_map/ppermute | solution.py:297
  53.8 1.2 copy-start.1
  55.0 7.2 %copy-start.2 = (bf16[512,1024]{1,0:T(8,128)(2,1)S(1)}, bf16[512,1024]{1,0:T(8,128)(2,1)}, u32[]{:S(2)}) copy-start(bf16[512,1024]{1,0:T(8,128)(2,1)} %unit_rows.3.b1) | copy-start | bytes 3145732
  62.2 12.5 %copy-start.3 = (f32[1024,64]{0,1:T(8,128)S(1)}, f32[1024,64]{0,1:T(8,128)}, u32[]{:S(2)}) copy-start(f32[1024,64]{0,1:T(8,128)} %param.5) | copy-start | bytes 786436
  68.8 5.9 %collective-permute-start.5 = (f32[1,1024]{1,0:T(1,128)S(1)}, f32[1,1024]{1,0:T(1,128)S(1)}, u32[]{:S(2)}, u32[]{:S(2)}) collective-permute-start(f32[1,1024]{1,0:T(1,128)S(1)} %get-tuple-element.29), channel_id=1, source_target_pairs={{0,2},{1,7},{2,4},{3,1},{4,6},{5,3},{6,0},{7,5},{8,10},{9,15},{10,... | collective-permute-start | bytes 12296 | tf_op jit(solution)/shard_map/ppermute | solution.py:300
  74.8 5.0 %collective-permute-start.6 = (bf16[64,1024]{1,0:T(8,128)(2,1)S(1)}, bf16[64,1024]{1,0:T(8,128)(2,1)S(1)}, u32[]{:S(2)}, u32[]{:S(2)}) collective-permute-start(bf16[64,1024]{1,0:T(8,128)(2,1)S(1)} %fusion.own), channel_id=1, source_target_pairs={{0,1},{1,0},{2,3},{3,2},{4,5},{5,4},{6,7},{7,6},{8,9},{9,8},{10,11... | collective-permute-start | bytes 393224 | tf_op jit(solution)/shard_map/ppermute | solution.py:294
  81.2 8.4 %collective-permute-start.8 = (f32[64,1024]{1,0:T(8,128)S(1)}, f32[64,1024]{1,0:T(8,128)S(1)}, u32[]{:S(2)}, u32[]{:S(2)}) collective-permute-start(f32[64,1024]{1,0:T(8,128)S(1)} %shard_map.40), channel_id=1, source_target_pairs={{0,2},{1,7},{2,4},{3,1},{4,6},{5,3},{6,0},{7,5},{8,10},{9,15},{10,... | collective-permute-start | bytes 786440 | tf_op jit(solution)/shard_map/ppermute | solution.py:300
  81.2 6.3 %collective-permute-start.7 = (bf16[64,1024]{1,0:T(8,128)(2,1)S(1)}, bf16[64,1024]{1,0:T(8,128)(2,1)S(1)}, u32[]{:S(2)}, u32[]{:S(2)}) collective-permute-start(bf16[64,1024]{1,0:T(8,128)(2,1)S(1)} %fusion.own), channel_id=1, source_target_pairs={{2,0},{7,1},{4,2},{1,3},{6,4},{3,5},{0,6},{5,7},{10,8},{15,9},{12,... | collective-permute-start | bytes 393224 | tf_op jit(solution)/shard_map/ppermute | solution.py:297
  90.4 6.8 %collective-permute-start.11 = (f32[64,64]{1,0:T(8,128)S(1)}, f32[64,64]{1,0:T(8,128)S(1)}, u32[]{:S(2)}, u32[]{:S(2)}) collective-permute-start(f32[64,64]{1,0:T(8,128)S(1)} %get-tuple-element.35), channel_id=1, source_target_pairs={{0,9},{1,8},{2,11},{3,10},{4,13},{5,12},{6,15},{7,14},{8,1},{9,0},... | collective-permute-start | bytes 49160 | tf_op jit(solution)/shard_map/ppermute | solution.py:262
  90.4 6.8 %collective-permute-start.10 = (f32[64,64]{1,0:T(8,128)S(1)}, f32[64,64]{1,0:T(8,128)S(1)}, u32[]{:S(2)}, u32[]{:S(2)}) collective-permute-start(f32[64,64]{1,0:T(8,128)S(1)} %get-tuple-element.35), channel_id=1, source_target_pairs={{0,1},{1,0},{2,3},{3,2},{4,5},{5,4},{6,7},{7,6},{8,9},{9,8},{10,11... | collective-permute-start | bytes 49160 | tf_op jit(solution)/shard_map/ppermute | solution.py:262
  94.3 2.9 %collective-permute-start.9 = (f32[64,64]{1,0:T(8,128)S(1)}, f32[64,64]{1,0:T(8,128)S(1)}, u32[]{:S(2)}, u32[]{:S(2)}) collective-permute-start(f32[64,64]{1,0:T(8,128)S(1)} %get-tuple-element.35), channel_id=1, source_target_pairs={{0,8},{1,9},{2,10},{3,11},{4,12},{5,13},{6,14},{7,15},{8,0},{9,1},... | collective-permute-start | bytes 49160 | tf_op jit(solution)/shard_map/ppermute | solution.py:262
  94.5 14.4 %collective-permute-start.17 = (f32[64,1024]{1,0:T(8,128)S(1)}, f32[64,1024]{1,0:T(8,128)S(1)}, u32[]{:S(2)}, u32[]{:S(2)}) collective-permute-start(f32[64,1024]{1,0:T(8,128)S(1)} %get-tuple-element.36.refs_0_), channel_id=1, source_target_pairs={{2,0},{7,1},{4,2},{1,3},{6,4},{3,5},{0,6},{5,7},{10,8},{15,9},{12,... | collective-permute-start | bytes 786440 | tf_op jit(solution)/shard_map/ppermute | solution.py:297
  96.6 12.3 %collective-permute-start.16 = (f32[64,1024]{1,0:T(8,128)S(1)}, f32[64,1024]{1,0:T(8,128)S(1)}, u32[]{:S(2)}, u32[]{:S(2)}) collective-permute-start(f32[64,1024]{1,0:T(8,128)S(1)} %get-tuple-element.36.refs_0_), channel_id=1, source_target_pairs={{0,1},{1,0},{2,3},{3,2},{4,5},{5,4},{6,7},{7,6},{8,9},{9,8},{10,11... | collective-permute-start | bytes 786440 | tf_op jit(solution)/shard_map/ppermute | solution.py:294
  97.3 4.0 %collective-permute-start.12 = (f32[64,64]{1,0:T(8,128)S(1)}, f32[64,64]{1,0:T(8,128)S(1)}, u32[]{:S(2)}, u32[]{:S(2)}) collective-permute-start(f32[64,64]{1,0:T(8,128)S(1)} %add_add_fusion.5), channel_id=1, source_target_pairs={{0,16},{1,17},{2,18},{3,19},{4,20},{5,21},{6,22},{7,23},{8,24},{9,... | collective-permute-start | bytes 49160 | tf_op jit(solution)/shard_map/ppermute | solution.py:262
  101.2 5.7 %collective-permute-start.15 = (f32[64,64]{1,0:T(8,128)S(1)}, f32[64,64]{1,0:T(8,128)S(1)}, u32[]{:S(2)}, u32[]{:S(2)}) collective-permute-start(f32[64,64]{1,0:T(8,128)S(1)} %add.119), channel_id=1, source_target_pairs={{0,6},{1,7},{2,4},{3,5},{4,2},{5,3},{6,0},{7,1},{8,14},{9,15},{10,... | collective-permute-start | bytes 49160 | tf_op jit(solution)/shard_map/ppermute | solution.py:262
  104.1 4.8 %collective-permute-start.14 = (f32[64,64]{1,0:T(8,128)S(1)}, f32[64,64]{1,0:T(8,128)S(1)}, u32[]{:S(2)}, u32[]{:S(2)}) collective-permute-start(f32[64,64]{1,0:T(8,128)S(1)} %add.119), channel_id=1, source_target_pairs={{0,4},{1,5},{2,6},{3,7},{4,0},{5,1},{6,2},{7,3},{8,12},{9,13},{10,... | collective-permute-start | bytes 49160 | tf_op jit(solution)/shard_map/ppermute | solution.py:262
  104.1 4.8 %collective-permute-start.13 = (f32[64,64]{1,0:T(8,128)S(1)}, f32[64,64]{1,0:T(8,128)S(1)}, u32[]{:S(2)}, u32[]{:S(2)}) collective-permute-start(f32[64,64]{1,0:T(8,128)S(1)} %add.119), channel_id=1, source_target_pairs={{0,2},{1,3},{2,0},{3,1},{4,6},{5,7},{6,4},{7,5},{8,10},{9,11},{10,... | collective-permute-start | bytes 49160 | tf_op jit(solution)/shard_map/ppermute | solution.py:262
  112.7 8.2 %collective-permute-start.18 = (f32[64,1024]{1,0:T(8,128)S(1)}, f32[64,1024]{1,0:T(8,128)S(1)}, u32[]{:S(2)}, u32[]{:S(2)}) collective-permute-start(f32[64,1024]{1,0:T(8,128)S(1)} %shard_map.44), channel_id=1, source_target_pairs={{0,2},{1,7},{2,4},{3,1},{4,6},{5,3},{6,0},{7,5},{8,10},{9,15},{10,... | collective-permute-start | bytes 786440 | tf_op jit(solution)/shard_map/ppermute | solution.py:300
  121.7 3.3 %collective-permute-start.21 = (f32[64,64]{1,0:T(8,128)S(1)}, f32[64,64]{1,0:T(8,128)S(1)}, u32[]{:S(2)}, u32[]{:S(2)}) collective-permute-start(f32[64,64]{1,0:T(8,128)S(1)} %get-tuple-element.40), channel_id=1, source_target_pairs={{0,9},{1,8},{2,11},{3,10},{4,13},{5,12},{6,15},{7,14},{8,1},{9,0},... | collective-permute-start | bytes 49160 | tf_op jit(solution)/shard_map/ppermute | solution.py:262
  121.7 4.0 %collective-permute-start.20 = (f32[64,64]{1,0:T(8,128)S(1)}, f32[64,64]{1,0:T(8,128)S(1)}, u32[]{:S(2)}, u32[]{:S(2)}) collective-permute-start(f32[64,64]{1,0:T(8,128)S(1)} %get-tuple-element.40), channel_id=1, source_target_pairs={{0,1},{1,0},{2,3},{3,2},{4,5},{5,4},{6,7},{7,6},{8,9},{9,8},{10,11... | collective-permute-start | bytes 49160 | tf_op jit(solution)/shard_map/ppermute | solution.py:262
  121.7 4.0 %collective-permute-start.19 = (f32[64,64]{1,0:T(8,128)S(1)}, f32[64,64]{1,0:T(8,128)S(1)}, u32[]{:S(2)}, u32[]{:S(2)}) collective-permute-start(f32[64,64]{1,0:T(8,128)S(1)} %get-tuple-element.40), channel_id=1, source_target_pairs={{0,8},{1,9},{2,10},{3,11},{4,12},{5,13},{6,14},{7,15},{8,0},{9,1},... | collective-permute-start | bytes 49160 | tf_op jit(solution)/shard_map/ppermute | solution.py:262
  123.6 13.0 %collective-permute-start.27 = (f32[64,1024]{1,0:T(8,128)S(1)}, f32[64,1024]{1,0:T(8,128)S(1)}, u32[]{:S(2)}, u32[]{:S(2)}) collective-permute-start(f32[64,1024]{1,0:T(8,128)S(1)} %get-tuple-element.41.refs_0_), channel_id=1, source_target_pairs={{2,0},{7,1},{4,2},{1,3},{6,4},{3,5},{0,6},{5,7},{10,8},{15,9},{12,... | collective-permute-start | bytes 786440 | tf_op jit(solution)/shard_map/ppermute | solution.py:297
  124.2 12.3 %collective-permute-start.26 = (f32[64,1024]{1,0:T(8,128)S(1)}, f32[64,1024]{1,0:T(8,128)S(1)}, u32[]{:S(2)}, u32[]{:S(2)}) collective-permute-start(f32[64,1024]{1,0:T(8,128)S(1)} %get-tuple-element.41.refs_0_), channel_id=1, source_target_pairs={{0,1},{1,0},{2,3},{3,2},{4,5},{5,4},{6,7},{7,6},{8,9},{9,8},{10,11... | collective-permute-start | bytes 786440 | tf_op jit(solution)/shard_map/ppermute | solution.py:294
  125.8 4.0 %collective-permute-start.22 = (f32[64,64]{1,0:T(8,128)S(1)}, f32[64,64]{1,0:T(8,128)S(1)}, u32[]{:S(2)}, u32[]{:S(2)}) collective-permute-start(f32[64,64]{1,0:T(8,128)S(1)} %add_add_fusion.3), channel_id=1, source_target_pairs={{0,16},{1,17},{2,18},{3,19},{4,20},{5,21},{6,22},{7,23},{8,24},{9,... | collective-permute-start | bytes 49160 | tf_op jit(solution)/shard_map/ppermute | solution.py:262
  129.7 6.1 %collective-permute-start.25 = (f32[64,64]{1,0:T(8,128)S(1)}, f32[64,64]{1,0:T(8,128)S(1)}, u32[]{:S(2)}, u32[]{:S(2)}) collective-permute-start(f32[64,64]{1,0:T(8,128)S(1)} %add.126), channel_id=1, source_target_pairs={{0,6},{1,7},{2,4},{3,5},{4,2},{5,3},{6,0},{7,1},{8,14},{9,15},{10,... | collective-permute-start | bytes 49160 | tf_op jit(solution)/shard_map/ppermute | solution.py:262
  131.7 4.8 %collective-permute-start.24 = (f32[64,64]{1,0:T(8,128)S(1)}, f32[64,64]{1,0:T(8,128)S(1)}, u32[]{:S(2)}, u32[]{:S(2)}) collective-permute-start(f32[64,64]{1,0:T(8,128)S(1)} %add.126), channel_id=1, source_target_pairs={{0,4},{1,5},{2,6},{3,7},{4,0},{5,1},{6,2},{7,3},{8,12},{9,13},{10,... | collective-permute-start | bytes 49160 | tf_op jit(solution)/shard_map/ppermute | solution.py:262
  131.7 4.8 %collective-permute-start.23 = (f32[64,64]{1,0:T(8,128)S(1)}, f32[64,64]{1,0:T(8,128)S(1)}, u32[]{:S(2)}, u32[]{:S(2)}) collective-permute-start(f32[64,64]{1,0:T(8,128)S(1)} %add.126), channel_id=1, source_target_pairs={{0,2},{1,3},{2,0},{3,1},{4,6},{5,7},{6,4},{7,5},{8,10},{9,11},{10,... | collective-permute-start | bytes 49160 | tf_op jit(solution)/shard_map/ppermute | solution.py:262
  140.3 8.2 %collective-permute-start.28 = (f32[64,1024]{1,0:T(8,128)S(1)}, f32[64,1024]{1,0:T(8,128)S(1)}, u32[]{:S(2)}, u32[]{:S(2)}) collective-permute-start(f32[64,1024]{1,0:T(8,128)S(1)} %shard_map.48), channel_id=1, source_target_pairs={{0,2},{1,7},{2,4},{3,1},{4,6},{5,3},{6,0},{7,5},{8,10},{9,15},{10,... | collective-permute-start | bytes 786440 | tf_op jit(solution)/shard_map/ppermute | solution.py:300
  149.4 3.3 %collective-permute-start.31 = (f32[64,64]{1,0:T(8,128)S(1)}, f32[64,64]{1,0:T(8,128)S(1)}, u32[]{:S(2)}, u32[]{:S(2)}) collective-permute-start(f32[64,64]{1,0:T(8,128)S(1)} %get-tuple-element.45), channel_id=1, source_target_pairs={{0,9},{1,8},{2,11},{3,10},{4,13},{5,12},{6,15},{7,14},{8,1},{9,0},... | collective-permute-start | bytes 49160 | tf_op jit(solution)/shard_map/ppermute | solution.py:262
  149.4 4.0 %collective-permute-start.30 = (f32[64,64]{1,0:T(8,128)S(1)}, f32[64,64]{1,0:T(8,128)S(1)}, u32[]{:S(2)}, u32[]{:S(2)}) collective-permute-start(f32[64,64]{1,0:T(8,128)S(1)} %get-tuple-element.45), channel_id=1, source_target_pairs={{0,1},{1,0},{2,3},{3,2},{4,5},{5,4},{6,7},{7,6},{8,9},{9,8},{10,11... | collective-permute-start | bytes 49160 | tf_op jit(solution)/shard_map/ppermute | solution.py:262
  149.4 4.0 %collective-permute-start.29 = (f32[64,64]{1,0:T(8,128)S(1)}, f32[64,64]{1,0:T(8,128)S(1)}, u32[]{:S(2)}, u32[]{:S(2)}) collective-permute-start(f32[64,64]{1,0:T(8,128)S(1)} %get-tuple-element.45), channel_id=1, source_target_pairs={{0,8},{1,9},{2,10},{3,11},{4,12},{5,13},{6,14},{7,15},{8,0},{9,1},... | collective-permute-start | bytes 49160 | tf_op jit(solution)/shard_map/ppermute | solution.py:262
  153.4 4.0 %collective-permute-start.32 = (f32[64,64]{1,0:T(8,128)S(1)}, f32[64,64]{1,0:T(8,128)S(1)}, u32[]{:S(2)}, u32[]{:S(2)}) collective-permute-start(f32[64,64]{1,0:T(8,128)S(1)} %add_add_fusion.1), channel_id=1, source_target_pairs={{0,16},{1,17},{2,18},{3,19},{4,20},{5,21},{6,22},{7,23},{8,24},{9,... | collective-permute-start | bytes 49160 | tf_op jit(solution)/shard_map/ppermute | solution.py:262
  157.4 5.8 %collective-permute-start.35 = (f32[64,64]{1,0:T(8,128)S(1)}, f32[64,64]{1,0:T(8,128)S(1)}, u32[]{:S(2)}, u32[]{:S(2)}) collective-permute-start(f32[64,64]{1,0:T(8,128)S(1)} %add.133), channel_id=1, source_target_pairs={{0,6},{1,7},{2,4},{3,5},{4,2},{5,3},{6,0},{7,1},{8,14},{9,15},{10,... | collective-permute-start | bytes 49160 | tf_op jit(solution)/shard_map/ppermute | solution.py:262
  158.3 5.6 %collective-permute-start.34 = (f32[64,64]{1,0:T(8,128)S(1)}, f32[64,64]{1,0:T(8,128)S(1)}, u32[]{:S(2)}, u32[]{:S(2)}) collective-permute-start(f32[64,64]{1,0:T(8,128)S(1)} %add.133), channel_id=1, source_target_pairs={{0,4},{1,5},{2,6},{3,7},{4,0},{5,1},{6,2},{7,3},{8,12},{9,13},{10,... | collective-permute-start | bytes 49160 | tf_op jit(solution)/shard_map/ppermute | solution.py:262
  158.6 5.3 %collective-permute-start.33 = (f32[64,64]{1,0:T(8,128)S(1)}, f32[64,64]{1,0:T(8,128)S(1)}, u32[]{:S(2)}, u32[]{:S(2)}) collective-permute-start(f32[64,64]{1,0:T(8,128)S(1)} %add.133), channel_id=1, source_target_pairs={{0,2},{1,3},{2,0},{3,1},{4,6},{5,7},{6,4},{7,5},{8,10},{9,11},{10,... | collective-permute-start | bytes 49160 | tf_op jit(solution)/shard_map/ppermute | solution.py:262

commit v5 on v4

--- a/solution.py
+++ b/solution.py
@@ -159,6 +159,22 @@
         far_degree[:, span(m, size)] = total
 
 
+def bfloat_rows(value):
+    if value.dtype == BF16:
+        return value
+    high = value.astype(BF16)
+    rest = value - high.astype(F32)
+    middle = rest.astype(BF16)
+    low = (rest - middle.astype(F32)).astype(BF16)
+    return jnp.concatenate([high, middle, low], axis=0)
+
+
+def whole_rows(value, count):
+    if value.shape[0] == count:
+        return value
+    return (value[2 * count :] + value[count : 2 * count]) + value[:count]
+
+
 def kept(mask, m, first, *vectors):
     parts = []
     at = first
@@ -175,15 +191,19 @@
     return jnp.dot(left, right, preferred_element_type=F32)
 
 
-def far_rows_body(mask, own, x, far0, corner, far1, out):
+def far_rows_body(mask, own_ref, x_ref, far0, corner, far1, out):
+    own, x = bfloat_rows(own_ref[...]), bfloat_rows(x_ref[...])
     size = own.shape[1] // BLK_DEV
+    count = out.shape[0]
     cut = far0.shape[0]
     left = kept(mask, 0, 0, own, x)
-    out[:, span(0, size)] = apart(left[:, :cut], far0[...]) + apart(left[:, cut:], corner[...])
-    out[:, span(1, size)] = apart(kept(mask, 1, 0, own, x), far1[...])
-
-
-def near_rows_body(mask, own, x, z, near0, near1, far0, far1, out):
+    first = apart(left[:, :cut], far0[...]) + apart(left[:, cut:], corner[...])
+    out[:, span(0, size)] = whole_rows(first, count)
+    out[:, span(1, size)] = whole_rows(apart(kept(mask, 1, 0, own, x), far1[...]), count)
+
+
+def near_rows_body(mask, own_ref, x_ref, z_ref, near0, near1, far0, far1, out):
+    own, x, z = bfloat_rows(own_ref[...]), bfloat_rows(x_ref[...]), bfloat_rows(z_ref[...])
     size = own.shape[1] // BLK_DEV
     cut = near0.shape[0]
     for m in range(BLK_DEV):
@@ -192,14 +212,24 @@
         side = kept(mask, m, 2 * BLK_DEV, z)
         total = apart(left[:, :cut], near0[:, there]) + apart(left[:, cut:], near1[:, there])
         total += cross(side[:, :size], far0[there, :]) + cross(side[:, size:], far1[there, :])
-        out[:, there] = total
-
-
-def join_body(near, given, root, image, ahead, gram):
-    full = (near[...] + given[...]) * root[...]
+        out[:, there] = whole_rows(total, out.shape[0])
+
+
+def finish(full, root, image, ahead, gram):
     image[...] = full
     ahead[...] = full * root[...]
     gram[...] = cross(full, full, precision=EXACT)
+
+
+def join_body(near, given, root, image, ahead, gram):
+    finish((near[...] + given[...]) * root[...], root, image, ahead, gram)
+
+
+def advance_body(scale, total, near, given, root, image, ahead, gram):
+    factor = inverse_factor(total[...]) * scale
+    full = (near[...] + given[...]) * root[...]
+    solved = jnp.dot(factor, full, preferred_element_type=F32, precision=EXACT)
+    finish(solved, root, image, ahead, gram)
 
 
 GROUP = 8
@@ -234,18 +264,15 @@
     return jnp.concatenate(finished, axis=0)[:, size:]
 
 
-def solve_body(scale, gram, *refs):
-    factor = inverse_factor(gram[...]) * scale
-    count = len(refs) // 2
-    for value, out in zip(refs[:count], refs[count:]):
-        solved = jnp.dot(factor, value[...], preferred_element_type=F32, precision=EXACT)
-        out[...] = solved.astype(out.dtype)
+def solve_body(scale, total, image, out):
+    factor = inverse_factor(total[...]) * scale
+    out[...] = jnp.dot(factor, image[...], preferred_element_type=F32, precision=EXACT)
 
 
 def exchange_masks(row_count, col_count):
     low = [1 << bit for bit in range(col_count.bit_length() - 1)]
     high = [col_count << bit for bit in range(row_count.bit_length() - 1)]
-    stages = [(high[0], low[0]), (high[1],), (low[1], low[2])]
+    stages = [(low[1], low[2]), (high[0], high[1]), (low[0],)]
     rest = high[2:] + low[3:]
     return stages + [tuple(rest[at : at + 2]) for at in range(0, len(rest), 2)]
 
@@ -343,34 +370,26 @@
     wide = shaped(across_shape, F32)
     far_rows = call(far_rows_body, wide, [SMEM] + [VMEM] * 5, 8 * work, 8 * work // 64)
     near_rows = call(near_rows_body, wide, [SMEM] + [VMEM] * 7, 12 * work, 12 * work // 64)
-    join = call(
-        join_body,
-        (wide, wide, shaped((columns, columns), F32)),
-        [VMEM] * 3, 2 * columns * columns * points, 4 * columns * points,
-    )
-
-    def solve(dtype, gram, *values):
-        return call(
-            functools.partial(solve_body, math.sqrt(total_rows)),
-            tuple(shaped(across_shape, dtype) for _ in values),
-            [VMEM] * (1 + len(values)),
-            4 * columns * columns * points, 4 * columns * points,
-        )(gram, *values)
+    results = (wide, wide, shaped((columns, columns), F32))
+    effort = 2 * columns * columns * points, 4 * columns * points
+    scale = math.sqrt(total_rows)
+    join = call(join_body, results, [VMEM] * 3, *effort)
+    advance = call(functools.partial(advance_body, scale), results, [VMEM] * 4, *effort)
+    solve = call(functools.partial(solve_body, scale), wide, [VMEM] * 2, *effort)
 
     own = (start_vectors.T * root).astype(BF16)
-    x = from_x(own)
-    z = from_z(own)
-    for iteration in range(ITERS):
+    for step in range(ITERS):
+        x = from_x(own)
+        z = from_z(own)
         sent = far_rows(far_mask, own, x, far0, corner, far1)
         given = to_z(sent)
         held = near_rows(own_mask, own, x, z, near0, near1, far0, far1)
-        image, ahead, gram = join(held, given, root)
-        if iteration < ITERS - 1:
-            ahead_x, ahead_z = from_x(ahead), from_z(ahead)
-            total = total_sum(gram)
-            own, x, z = solve(BF16, total, ahead, ahead_x, ahead_z)
-    (vectors,) = solve(F32, total_sum(gram), image)
-    return vectors.T
+        if step == 0:
+            image, own, gram = join(held, given, root)
+        else:
+            image, own, gram = advance(total, held, given, root)
+        total = total_sum(gram)
+    return solve(total, image).T
 
 
 def solution(mesh):

time: 167 us -> 159 us (0.952)
  waiting for transfers between devices: 77.2 us -> 67.1 us
  starting transfers between devices: 46.9 us -> 49.2 us
    ppermute x4, waiting for transfers between devices: 15.5 us -> 10.2 us  [to_z(): lax.ppermute(value, 'col', [(i, side_of(i)) for i in range(col_count)])]
    ppermute x21, waiting for transfers between devices: 18.6 us -> 13.7 us  [fetched(): return lax.ppermute(value, ('row', 'col'), pairs)]
    ppermute x5, starting transfers between devices: 1.11 us -> 4.38 us  [from_x(): return lax.ppermute(value, 'col', [(i, i ^ 1) for i in range(col_count)])]
    ppermute x21, starting transfers between devices: 25.7 us -> 24 us  [fetched(): return lax.ppermute(value, ('row', 'col'), pairs)]
    pallas_call x6 -> x4, Pallas kernels: 9.8 us -> 9.14 us  [the longest x2 5.67 us: on_device(): image, own, gram = advance(total, held, given, root)]
  transfers between devices with their start and end apart: 36 -> 36, of which waited for: 19 -> 16; matrix products, arithmetic and copies ran while one was open for 1% -> 1% of each run, Pallas kernels for 10% -> 12%
where the time goes in v5:
time: 159 us
  waiting for transfers between devices  67.1 us (42%)
  starting transfers between devices  49.2 us (31%)
  Pallas kernels  39.6 us (25%)
  local copies, waits for them, and re-layouts  2.12 us (1%)
    ppermute x6, waiting for transfers between devices, from_z(): lax.ppermute(value, 'col', [(side_of(i), i) for i in range(col_count)])  38.2 us
    ppermute x21, starting transfers between devices, fetched(): return lax.ppermute(value, ('row', 'col'), pairs)  24 us
    ppermute x6, starting transfers between devices, from_z(): lax.ppermute(value, 'col', [(side_of(i), i) for i in range(col_count)])  17.6 us
    ppermute x21, waiting for transfers between devices, fetched(): return lax.ppermute(value, ('row', 'col'), pairs)  13.7 us
    ppermute x4, waiting for transfers between devices, to_z(): lax.ppermute(value, 'col', [(i, side_of(i)) for i in range(col_count)])  10.2 us
    pallas_call x1, Pallas kernels, on_device(): call(first_tiles_body, (shaped((most * size, points), BF16), shaped((most...  7.16 us
    pallas_call x1, Pallas kernels, on_device(): call(last_tiles_body, (shaped((size, points), BF16), shaped((size, size),...  6.54 us
    pallas_call x3, Pallas kernels, on_device(): held = near_rows(own_mask, own, x, z, near0, near1, far0, far1)  6.45 us
  transfers between devices with their start and end apart: 36, of which 16 were waited for; matrix products, arithmetic and copies ran while one was open for 1% of the time, Pallas kernels for 12%

profile of v5, /device:TPU:0, one launch (start us, length us, event | category | flops | bytes accessed | tf_op | source)
XLA Modules:
  0.0 158.7 jit_solution(3720538487973098229)
XLA Ops:
  0.0 3.0 %unit_rows.2.b0 = bf16[512,1024]{1,0:T(8,128)(2,1)} custom-call(f32[1024,1024]{1,0:T(8,128)} %points_ref.3), custom_call_target="tpu_custom_call" | custom-call | flops 1572864 | bytes 3145728 | tf_op jit(solution)/shard_map/unit_rows/pallas_call | solution.py:69
  3.0 5.1 %collective-permute-start.3 = (bf16[512,1024]{1,0:T(8,128)(2,1)}, bf16[512,1024]{1,0:T(8,128)(2,1)S(1)}, u32[]{:S(2)}, u32[]{:S(2)}) collective-permute-start(bf16[512,1024]{1,0:T(8,128)(2,1)} %unit_rows.2.b0), channel_id=1, source_target_pairs={{2,0},{7,1},{4,2},{1,3},{6,4},{3,5},{0,6},{5,7},{10,8},{15,9},{12,... | collective-permute-start | bytes 3145736 | tf_op jit(solution)/shard_map/ppermute | solution.py:324
  8.1 2.9 %unit_rows.3.b1 = bf16[512,1024]{1,0:T(8,128)(2,1)} custom-call(f32[1024,1024]{1,0:T(8,128)} %points_ref.3), custom_call_target="tpu_custom_call" | custom-call | flops 1572864 | bytes 3145728 | tf_op jit(solution)/shard_map/unit_rows/pallas_call | solution.py:69
  11.0 1.8 %collective-permute-start.4 = (bf16[512,1024]{1,0:T(8,128)(2,1)}, bf16[512,1024]{1,0:T(8,128)(2,1)}, u32[]{:S(2)}, u32[]{:S(2)}) collective-permute-start(bf16[512,1024]{1,0:T(8,128)(2,1)} %unit_rows.3.b1), channel_id=1, source_target_pairs={{2,0},{7,1},{4,2},{1,3},{6,4},{3,5},{0,6},{5,7},{10,8},{15,9},{12,... | collective-permute-start | bytes 3145736 | tf_op jit(solution)/shard_map/ppermute | solution.py:324
  13.2 3.7 %collective-permute-start = (s32[2,12]{1,0:T(2,128)S(1)}, s32[2,12]{1,0:T(2,128)S(1)}, u32[]{:S(2)}, u32[]{:S(2)}) collective-permute-start(s32[2,12]{1,0:T(2,128)S(1)} %copy-done.4), channel_id=1, source_target_pairs={{2,0},{7,1},{4,2},{1,3},{6,4},{3,5},{0,6},{5,7},{10,8},{15,9},{12,... | collective-permute-start | bytes 296 | tf_op jit(solution)/shard_map/ppermute | solution.py:324
  17.7 35.6 %collective-permute-done = s32[2,12]{1,0:T(2,128)S(1)} collective-permute-done((s32[2,12]{1,0:T(2,128)S(1)}, s32[2,12]{1,0:T(2,128)S(1)}, u32[]{:S(2)}, u32[]{:S(2)}) %collective-permute-start) | collective-permute-done | bytes 128 | tf_op jit(solution)/shard_map/ppermute | solution.py:324
  53.8 1.2 copy-done.1
  55.0 7.2 %shard_map.37 = (bf16[1536,1024]{1,0:T(8,128)(2,1)S(1)}, bf16[1536,512]{1,0:T(8,128)(2,1)S(1)}, f32[1,1024]{1,0:T(1,128)S(1)}, f32[3,512]{1,0:T(4,128)S(1)}) custom-call(f32[2,6]{1,0:T(2,128)S(1)} %or_convert_fusion.1.own_mask.mask, bf16[512,1024]{1,0:T(8,128)(2,1)S(1)} %copy-done, bf16[512,1024]{1,0:T(8,128)(2,1)S(1)} %copy-done.1, ...), custom_call_target="tpu_custom_call" | custom-call | flops 4831838208 | bytes 18874368 | tf_op jit(solution)/shard_map/pallas_call | solution.py:350
  62.2 6.5 %shard_map.38 = (bf16[512,1024]{1,0:T(8,128)(2,1)S(1)}, bf16[512,512]{1,0:T(8,128)(2,1)S(1)}, bf16[2048,512]{1,0:T(8,128)(2,1)S(1)}, f32[1,1024]{1,0:T(1,128)S(1)}, f32[1,1024]{1,0:T(1,128)S(1)}) custom-call(f32[2,6]{1,0:T(2,128)S(1)} %or_convert_fusion.1.own_mask.mask, f32[2,4]{1,0:T(2,128)S(1)} %or_convert_fusion.far_mask.mask, ...), custom_call_target="tpu_custom_call" | custom-call | flops 3758096384 | bytes 14680064 | tf_op jit(solution)/shard_map/pallas_call | solution.py:358
  69.3 5.4 %collective-permute-done.5 = f32[1,1024]{1,0:T(1,128)S(1)} collective-permute-done((f32[1,1024]{1,0:T(1,128)S(1)}, f32[1,1024]{1,0:T(1,128)S(1)}, u32[]{:S(2)}, u32[]{:S(2)}) %collective-permute-start.5) | collective-permute-done | bytes 4128 | tf_op jit(solution)/shard_map/ppermute | solution.py:327
  74.8 5.0 %collective-permute-done.6.x_ref = bf16[64,1024]{1,0:T(8,128)(2,1)S(1)} collective-permute-done((bf16[64,1024]{1,0:T(8,128)(2,1)S(1)}, bf16[64,1024]{1,0:T(8,128)(2,1)S(1)}, u32[]{:S(2)}, u32[]{:S(2)}) %collective-permute-start.6) | collective-permute-done | bytes 131104 | tf_op jit(solution)/shard_map/ppermute | solution.py:321
  79.8 1.4 shard_map.40
  81.2 3.8 %collective-permute-start.7 = (bf16[64,1024]{1,0:T(8,128)(2,1)S(1)}, bf16[64,1024]{1,0:T(8,128)(2,1)S(1)}, u32[]{:S(2)}, u32[]{:S(2)}) collective-permute-start(bf16[64,1024]{1,0:T(8,128)(2,1)S(1)} %fusion.own_ref), channel_id=1, source_target_pairs={{2,0},{7,1},{4,2},{1,3},{6,4},{3,5},{0,6},{5,7},{10,8},{15,9},{12,... | collective-permute-start | bytes 393224 | tf_op jit(solution)/shard_map/ppermute | solution.py:324
  85.1 2.5 %collective-permute-done.7.z_ref = bf16[64,1024]{1,0:T(8,128)(2,1)S(1)} collective-permute-done((bf16[64,1024]{1,0:T(8,128)(2,1)S(1)}, bf16[64,1024]{1,0:T(8,128)(2,1)S(1)}, u32[]{:S(2)}, u32[]{:S(2)}) %collective-permute-start.7) | collective-permute-done | bytes 131104 | tf_op jit(solution)/shard_map/ppermute | solution.py:324
  87.6 2.0 %shard_map.39.near = f32[64,1024]{1,0:T(8,128)S(1)} custom-call(f32[2,6]{1,0:T(2,128)S(1)} %or_convert_fusion.1.own_mask.mask, bf16[64,1024]{1,0:T(8,128)(2,1)S(1)} %fusion.own_ref, bf16[64,1024]{1,0:T(8,128)(2,1)S(1)} %collective-permute-done.6.x_ref, bf16[64,1024]{1,0:T(8,128)(2,1)S(1)} %collective-permute-done.7.z_ref, ...), custom_call_target="tpu_custom_call" | custom-call | flops 402653184 | bytes 6291456 | tf_op jit(solution)/shard_map/pallas_call | solution.py:386
  89.6 0.8 shard_map.41
  90.4 3.9 %collective-permute-start.16 = (f32[64,1024]{1,0:T(8,128)S(1)}, f32[64,1024]{1,0:T(8,128)S(1)}, u32[]{:S(2)}, u32[]{:S(2)}) collective-permute-start(f32[64,1024]{1,0:T(8,128)S(1)} %get-tuple-element.30.own_ref), channel_id=1, source_target_pairs={{0,1},{1,0},{2,3},{3,2},{4,5},{5,4},{6,7},{7,6},{8,9},{9,8},{10,11... | collective-permute-start | bytes 786440 | tf_op jit(solution)/shard_map/ppermute | solution.py:321
  94.7 2.1 %collective-permute-start.10 = (f32[64,64]{1,0:T(8,128)S(1)}, f32[64,64]{1,0:T(8,128)S(1)}, u32[]{:S(2)}, u32[]{:S(2)}) collective-permute-start(f32[64,64]{1,0:T(8,128)S(1)} %get-tuple-element.29), channel_id=1, source_target_pairs={{0,4},{1,5},{2,6},{3,7},{4,0},{5,1},{6,2},{7,3},{8,12},{9,13},{10,... | collective-permute-start | bytes 49160 | tf_op jit(solution)/shard_map/ppermute | solution.py:289
  96.8 1.9 %collective-permute-start.9 = (f32[64,64]{1,0:T(8,128)S(1)}, f32[64,64]{1,0:T(8,128)S(1)}, u32[]{:S(2)}, u32[]{:S(2)}) collective-permute-start(f32[64,64]{1,0:T(8,128)S(1)} %get-tuple-element.29), channel_id=1, source_target_pairs={{0,2},{1,3},{2,0},{3,1},{4,6},{5,7},{6,4},{7,5},{8,10},{9,11},{10,... | collective-permute-start | bytes 49160 | tf_op jit(solution)/shard_map/ppermute | solution.py:289
  99.1 1.0 collective-permute-done.11
  100.1 0.7 collective-permute-done.9
  100.8 1.6 %collective-permute-start.13 = (f32[64,64]{1,0:T(8,128)S(1)}, f32[64,64]{1,0:T(8,128)S(1)}, u32[]{:S(2)}, u32[]{:S(2)}) collective-permute-start(f32[64,64]{1,0:T(8,128)S(1)} %add_add_fusion.5), channel_id=1, source_target_pairs={{0,16},{1,17},{2,18},{3,19},{4,20},{5,21},{6,22},{7,23},{8,24},{9,... | collective-permute-start | bytes 49160 | tf_op jit(solution)/shard_map/ppermute | solution.py:289
  102.7 1.5 shard_map.43
  104.2 2.0 %collective-permute-start.18 = (f32[64,1024]{1,0:T(8,128)S(1)}, f32[64,1024]{1,0:T(8,128)S(1)}, u32[]{:S(2)}, u32[]{:S(2)}) collective-permute-start(f32[64,1024]{1,0:T(8,128)S(1)} %shard_map.43), channel_id=1, source_target_pairs={{0,2},{1,7},{2,4},{3,1},{4,6},{5,3},{6,0},{7,5},{8,10},{9,15},{10,... | collective-permute-start | bytes 786440 | tf_op jit(solution)/shard_map/ppermute | solution.py:327
  106.2 0.9 collective-permute-start.15
  107.1 3.1 %collective-permute-done.15 = f32[64,64]{1,0:T(8,128)S(1)} collective-permute-done((f32[64,64]{1,0:T(8,128)S(1)}, f32[64,64]{1,0:T(8,128)S(1)}, u32[]{:S(2)}, u32[]{:S(2)}) %collective-permute-start.15) | collective-permute-done | bytes 16416 | tf_op jit(solution)/shard_map/ppermute | solution.py:289
  110.2 2.2 %shard_map.42.near = f32[64,1024]{1,0:T(8,128)S(1)} custom-call(f32[2,6]{1,0:T(2,128)S(1)} %or_convert_fusion.1.own_mask.mask, f32[64,1024]{1,0:T(8,128)S(1)} %get-tuple-element.30.own_ref, f32[64,1024]{1,0:T(8,128)S(1)} %collective-permute-done.16.x_ref, f32[64,1024]{1,0:T(8,128)S(1)} %collective-permute-done.17.z_ref, ...), custom_call_target="tpu_custom_call" | custom-call | flops 402653184 | bytes 6291456 | tf_op jit(solution)/shard_map/pallas_call | solution.py:386
  112.5 2.1 %collective-permute-done.18.given = f32[64,1024]{1,0:T(8,128)S(1)} collective-permute-done((f32[64,1024]{1,0:T(8,128)S(1)}, f32[64,1024]{1,0:T(8,128)S(1)}, u32[]{:S(2)}, u32[]{:S(2)}) %collective-permute-start.18) | collective-permute-done | bytes 262176 | tf_op jit(solution)/shard_map/ppermute | solution.py:327
  114.5 2.8 %shard_map.44 = (f32[64,1024]{1,0:T(8,128)}, f32[64,1024]{1,0:T(8,128)S(1)}, f32[64,64]{1,0:T(8,128)S(1)}) custom-call(f32[64,64]{1,0:T(8,128)S(1)} %add.122.total, f32[64,1024]{1,0:T(8,128)S(1)} %shard_map.42.near, f32[64,1024]{1,0:T(8,128)S(1)} %collective-permute-done.18.given, f32[1,1024]{1,0:T(1,128)S(1)} %add_rsqrt_fusion.root), custom_call_target="tpu_custom_call" | custom-call | flops 8388608 | bytes 262144 | tf_op jit(solution)/shard_map/pallas_call | solution.py:390
  117.4 2.8 %collective-permute-start.21 = (f32[64,64]{1,0:T(8,128)S(1)}, f32[64,64]{1,0:T(8,128)S(1)}, u32[]{:S(2)}, u32[]{:S(2)}) collective-permute-start(f32[64,64]{1,0:T(8,128)S(1)} %get-tuple-element.31), channel_id=1, source_target_pairs={{0,6},{1,7},{2,4},{3,5},{4,2},{5,3},{6,0},{7,1},{8,14},{9,15},{10,... | collective-permute-start | bytes 49160 | tf_op jit(solution)/shard_map/ppermute | solution.py:289
  120.1 1.6 %collective-permute-start.19 = (f32[64,64]{1,0:T(8,128)S(1)}, f32[64,64]{1,0:T(8,128)S(1)}, u32[]{:S(2)}, u32[]{:S(2)}) collective-permute-start(f32[64,64]{1,0:T(8,128)S(1)} %get-tuple-element.31), channel_id=1, source_target_pairs={{0,2},{1,3},{2,0},{3,1},{4,6},{5,7},{6,4},{7,5},{8,10},{9,11},{10,... | collective-permute-start | bytes 49160 | tf_op jit(solution)/shard_map/ppermute | solution.py:289
  121.8 2.8 %collective-permute-start.27 = (f32[64,1024]{1,0:T(8,128)S(1)}, f32[64,1024]{1,0:T(8,128)S(1)}, u32[]{:S(2)}, u32[]{:S(2)}) collective-permute-start(f32[64,1024]{1,0:T(8,128)S(1)} %get-tuple-element.32.own_ref), channel_id=1, source_target_pairs={{2,0},{7,1},{4,2},{1,3},{6,4},{3,5},{0,6},{5,7},{10,8},{15,9},{12,... | collective-permute-start | bytes 786440 | tf_op jit(solution)/shard_map/ppermute | solution.py:324
  124.5 0.8 collective-permute-done.20
  125.4 1.3 collective-permute-start.23
  127.2 1.5 shard_map.46
  128.8 0.7 collective-permute-start.28
  129.6 2.5 %collective-permute-start.25 = (f32[64,64]{1,0:T(8,128)S(1)}, f32[64,64]{1,0:T(8,128)S(1)}, u32[]{:S(2)}, u32[]{:S(2)}) collective-permute-start(f32[64,64]{1,0:T(8,128)S(1)} %add_add_fusion.2), channel_id=1, source_target_pairs={{0,1},{1,0},{2,3},{3,2},{4,5},{5,4},{6,7},{7,6},{8,9},{9,8},{10,11... | collective-permute-start | bytes 49160 | tf_op jit(solution)/shard_map/ppermute | solution.py:289
  132.0 1.9 %collective-permute-done.25 = f32[64,64]{1,0:T(8,128)S(1)} collective-permute-done((f32[64,64]{1,0:T(8,128)S(1)}, f32[64,64]{1,0:T(8,128)S(1)}, u32[]{:S(2)}, u32[]{:S(2)}) %collective-permute-start.25) | collective-permute-done | bytes 16416 | tf_op jit(solution)/shard_map/ppermute | solution.py:289
  133.9 2.2 %shard_map.45.near = f32[64,1024]{1,0:T(8,128)S(1)} custom-call(f32[2,6]{1,0:T(2,128)S(1)} %or_convert_fusion.1.own_mask.mask, f32[64,1024]{1,0:T(8,128)S(1)} %get-tuple-element.32.own_ref, f32[64,1024]{1,0:T(8,128)S(1)} %collective-permute-done.26.x_ref, f32[64,1024]{1,0:T(8,128)S(1)} %collective-permute-done.27.z_ref, ...), custom_call_target="tpu_custom_call" | custom-call | flops 402653184 | bytes 6291456 | tf_op jit(solution)/shard_map/pallas_call | solution.py:386
  136.2 2.7 %collective-permute-done.28.given = f32[64,1024]{1,0:T(8,128)S(1)} collective-permute-done((f32[64,1024]{1,0:T(8,128)S(1)}, f32[64,1024]{1,0:T(8,128)S(1)}, u32[]{:S(2)}, u32[]{:S(2)}) %collective-permute-start.28) | collective-permute-done | bytes 262176 | tf_op jit(solution)/shard_map/ppermute | solution.py:327
  138.9 2.8 %shard_map.47 = (f32[64,1024]{1,0:T(8,128)S(1)}, f32[64,1024]{1,0:T(8,128)}, f32[64,64]{1,0:T(8,128)S(1)}) custom-call(f32[64,64]{1,0:T(8,128)S(1)} %add.129.total, f32[64,1024]{1,0:T(8,128)S(1)} %shard_map.45.near, f32[64,1024]{1,0:T(8,128)S(1)} %collective-permute-done.28.given, f32[1,1024]{1,0:T(1,128)S(1)} %add_rsqrt_fusion.root), custom_call_target="tpu_custom_call" | custom-call | flops 8388608 | bytes 262144 | tf_op jit(solution)/shard_map/pallas_call | solution.py:390
  142.1 4.0 %collective-permute-start.29 = (f32[64,64]{1,0:T(8,128)S(1)}, f32[64,64]{1,0:T(8,128)S(1)}, u32[]{:S(2)}, u32[]{:S(2)}) collective-permute-start(f32[64,64]{1,0:T(8,128)S(1)} %get-tuple-element.33), channel_id=1, source_target_pairs={{0,2},{1,3},{2,0},{3,1},{4,6},{5,7},{6,4},{7,5},{8,10},{9,11},{10,... | collective-permute-start | bytes 49160 | tf_op jit(solution)/shard_map/ppermute | solution.py:289
  146.1 1.3 collective-permute-done.31
  148.1 1.3 collective-permute-start.33
  149.9 1.7 %collective-permute-done.34 = f32[64,64]{1,0:T(8,128)S(1)} collective-permute-done((f32[64,64]{1,0:T(8,128)S(1)}, f32[64,64]{1,0:T(8,128)S(1)}, u32[]{:S(2)}, u32[]{:S(2)}) %collective-permute-start.34) | collective-permute-done | bytes 16416 | tf_op jit(solution)/shard_map/ppermute | solution.py:289
  152.1 1.7 %collective-permute-start.35 = (f32[64,64]{1,0:T(8,128)S(1)}, f32[64,64]{1,0:T(8,128)S(1)}, u32[]{:S(2)}, u32[]{:S(2)}) collective-permute-start(f32[64,64]{1,0:T(8,128)S(1)} %add_add_fusion), channel_id=1, source_target_pairs={{0,1},{1,0},{2,3},{3,2},{4,5},{5,4},{6,7},{7,6},{8,9},{9,8},{10,11... | collective-permute-start | bytes 49160 | tf_op jit(solution)/shard_map/ppermute | solution.py:289
  153.8 2.3 %collective-permute-done.35 = f32[64,64]{1,0:T(8,128)S(1)} collective-permute-done((f32[64,64]{1,0:T(8,128)S(1)}, f32[64,64]{1,0:T(8,128)S(1)}, u32[]{:S(2)}, u32[]{:S(2)}) %collective-permute-start.35) | collective-permute-done | bytes 16416 | tf_op jit(solution)/shard_map/ppermute | solution.py:289
  156.1 2.7 %shard_map.48 = f32[64,1024]{1,0:T(8,128)} custom-call(f32[64,64]{1,0:T(8,128)S(1)} %add.136.total, f32[64,1024]{1,0:T(8,128)S(1)} %get-tuple-element.34.image), custom_call_target="tpu_custom_call" | custom-call | flops 8388608 | bytes 262144 | tf_op jit(solution)/shard_map/pallas_call | solution.py:392
  (68 shorter events, 6.1 us)
Async XLA Ops:
  3.0 10.2 %copy-start.4 = (s32[2,12]{1,0:T(2,128)S(1)}, s32[2,12]{1,0:T(2,128)}, u32[]{:S(2)}) copy-start(s32[2,12]{1,0:T(2,128)} %param.4) | copy-start | bytes 292
  3.0 50.8 %copy-start = (bf16[512,1024]{1,0:T(8,128)(2,1)S(1)}, bf16[512,1024]{1,0:T(8,128)(2,1)}, u32[]{:S(2)}) copy-start(bf16[512,1024]{1,0:T(8,128)(2,1)} %unit_rows.2.b0) | copy-start | bytes 3145732
  3.0 50.8 %collective-permute-start.3 = (bf16[512,1024]{1,0:T(8,128)(2,1)}, bf16[512,1024]{1,0:T(8,128)(2,1)S(1)}, u32[]{:S(2)}, u32[]{:S(2)}) collective-permute-start(bf16[512,1024]{1,0:T(8,128)(2,1)} %unit_rows.2.b0), channel_id=1, source_target_pairs={{2,0},{7,1},{4,2},{1,3},{6,4},{3,5},{0,6},{5,7},{10,8},{15,9},{12,... | collective-permute-start | bytes 3145736 | tf_op jit(solution)/shard_map/ppermute | solution.py:324
  8.1 45.7 %collective-permute-start.1 = (bf16[512,1024]{1,0:T(8,128)(2,1)}, bf16[512,1024]{1,0:T(8,128)(2,1)}, u32[]{:S(2)}, u32[]{:S(2)}) collective-permute-start(bf16[512,1024]{1,0:T(8,128)(2,1)} %unit_rows.2.b0), channel_id=1, source_target_pairs={{0,1},{1,0},{2,3},{3,2},{4,5},{5,4},{6,7},{7,6},{8,9},{9,8},{10,11... | collective-permute-start | bytes 3145736 | tf_op jit(solution)/shard_map/ppermute | solution.py:321
  11.0 51.2 %collective-permute-start.4 = (bf16[512,1024]{1,0:T(8,128)(2,1)}, bf16[512,1024]{1,0:T(8,128)(2,1)}, u32[]{:S(2)}, u32[]{:S(2)}) collective-permute-start(bf16[512,1024]{1,0:T(8,128)(2,1)} %unit_rows.3.b1), channel_id=1, source_target_pairs={{2,0},{7,1},{4,2},{1,3},{6,4},{3,5},{0,6},{5,7},{10,8},{15,9},{12,... | collective-permute-start | bytes 3145736 | tf_op jit(solution)/shard_map/ppermute | solution.py:324
  12.8 49.4 %collective-permute-start.2 = (bf16[512,1024]{1,0:T(8,128)(2,1)}, bf16[512,1024]{1,0:T(8,128)(2,1)}, u32[]{:S(2)}, u32[]{:S(2)}) collective-permute-start(bf16[512,1024]{1,0:T(8,128)(2,1)} %unit_rows.3.b1), channel_id=1, source_target_pairs={{0,1},{1,0},{2,3},{3,2},{4,5},{5,4},{6,7},{7,6},{8,9},{9,8},{10,11... | collective-permute-start | bytes 3145736 | tf_op jit(solution)/shard_map/ppermute | solution.py:321
  13.2 40.2 %collective-permute-start = (s32[2,12]{1,0:T(2,128)S(1)}, s32[2,12]{1,0:T(2,128)S(1)}, u32[]{:S(2)}, u32[]{:S(2)}) collective-permute-start(s32[2,12]{1,0:T(2,128)S(1)} %copy-done.4), channel_id=1, source_target_pairs={{2,0},{7,1},{4,2},{1,3},{6,4},{3,5},{0,6},{5,7},{10,8},{15,9},{12,... | collective-permute-start | bytes 296 | tf_op jit(solution)/shard_map/ppermute | solution.py:324
  53.8 1.2 copy-start.1
  55.0 7.2 %copy-start.2 = (bf16[512,1024]{1,0:T(8,128)(2,1)S(1)}, bf16[512,1024]{1,0:T(8,128)(2,1)}, u32[]{:S(2)}) copy-start(bf16[512,1024]{1,0:T(8,128)(2,1)} %unit_rows.3.b1) | copy-start | bytes 3145732
  62.2 12.5 %copy-start.3 = (f32[1024,64]{0,1:T(8,128)S(1)}, f32[1024,64]{0,1:T(8,128)}, u32[]{:S(2)}) copy-start(f32[1024,64]{0,1:T(8,128)} %param.5) | copy-start | bytes 786436
  68.8 5.9 %collective-permute-start.5 = (f32[1,1024]{1,0:T(1,128)S(1)}, f32[1,1024]{1,0:T(1,128)S(1)}, u32[]{:S(2)}, u32[]{:S(2)}) collective-permute-start(f32[1,1024]{1,0:T(1,128)S(1)} %get-tuple-element.23), channel_id=1, source_target_pairs={{0,2},{1,7},{2,4},{3,1},{4,6},{5,3},{6,0},{7,5},{8,10},{9,15},{10,... | collective-permute-start | bytes 12296 | tf_op jit(solution)/shard_map/ppermute | solution.py:327
  74.8 5.0 %collective-permute-start.6 = (bf16[64,1024]{1,0:T(8,128)(2,1)S(1)}, bf16[64,1024]{1,0:T(8,128)(2,1)S(1)}, u32[]{:S(2)}, u32[]{:S(2)}) collective-permute-start(bf16[64,1024]{1,0:T(8,128)(2,1)S(1)} %fusion.own_ref), channel_id=1, source_target_pairs={{0,1},{1,0},{2,3},{3,2},{4,5},{5,4},{6,7},{7,6},{8,9},{9,8},{10,11... | collective-permute-start | bytes 393224 | tf_op jit(solution)/shard_map/ppermute | solution.py:321
  81.2 8.5 %collective-permute-start.8 = (f32[64,1024]{1,0:T(8,128)S(1)}, f32[64,1024]{1,0:T(8,128)S(1)}, u32[]{:S(2)}, u32[]{:S(2)}) collective-permute-start(f32[64,1024]{1,0:T(8,128)S(1)} %shard_map.40), channel_id=1, source_target_pairs={{0,2},{1,7},{2,4},{3,1},{4,6},{5,3},{6,0},{7,5},{8,10},{9,15},{10,... | collective-permute-start | bytes 786440 | tf_op jit(solution)/shard_map/ppermute | solution.py:327
  81.2 6.3 %collective-permute-start.7 = (bf16[64,1024]{1,0:T(8,128)(2,1)S(1)}, bf16[64,1024]{1,0:T(8,128)(2,1)S(1)}, u32[]{:S(2)}, u32[]{:S(2)}) collective-permute-start(bf16[64,1024]{1,0:T(8,128)(2,1)S(1)} %fusion.own_ref), channel_id=1, source_target_pairs={{2,0},{7,1},{4,2},{1,3},{6,4},{3,5},{0,6},{5,7},{10,8},{15,9},{12,... | collective-permute-start | bytes 393224 | tf_op jit(solution)/shard_map/ppermute | solution.py:324
  90.4 12.2 %collective-permute-start.16 = (f32[64,1024]{1,0:T(8,128)S(1)}, f32[64,1024]{1,0:T(8,128)S(1)}, u32[]{:S(2)}, u32[]{:S(2)}) collective-permute-start(f32[64,1024]{1,0:T(8,128)S(1)} %get-tuple-element.30.own_ref), channel_id=1, source_target_pairs={{0,1},{1,0},{2,3},{3,2},{4,5},{5,4},{6,7},{7,6},{8,9},{9,8},{10,11... | collective-permute-start | bytes 786440 | tf_op jit(solution)/shard_map/ppermute | solution.py:321
  94.3 5.7 %collective-permute-start.11 = (f32[64,64]{1,0:T(8,128)S(1)}, f32[64,64]{1,0:T(8,128)S(1)}, u32[]{:S(2)}, u32[]{:S(2)}) collective-permute-start(f32[64,64]{1,0:T(8,128)S(1)} %get-tuple-element.29), channel_id=1, source_target_pairs={{0,6},{1,7},{2,4},{3,5},{4,2},{5,3},{6,0},{7,1},{8,14},{9,15},{10,... | collective-permute-start | bytes 49160 | tf_op jit(solution)/shard_map/ppermute | solution.py:289
  94.7 5.3 %collective-permute-start.10 = (f32[64,64]{1,0:T(8,128)S(1)}, f32[64,64]{1,0:T(8,128)S(1)}, u32[]{:S(2)}, u32[]{:S(2)}) collective-permute-start(f32[64,64]{1,0:T(8,128)S(1)} %get-tuple-element.29), channel_id=1, source_target_pairs={{0,4},{1,5},{2,6},{3,7},{4,0},{5,1},{6,2},{7,3},{8,12},{9,13},{10,... | collective-permute-start | bytes 49160 | tf_op jit(solution)/shard_map/ppermute | solution.py:289
  96.8 3.9 %collective-permute-start.9 = (f32[64,64]{1,0:T(8,128)S(1)}, f32[64,64]{1,0:T(8,128)S(1)}, u32[]{:S(2)}, u32[]{:S(2)}) collective-permute-start(f32[64,64]{1,0:T(8,128)S(1)} %get-tuple-element.29), channel_id=1, source_target_pairs={{0,2},{1,3},{2,0},{3,1},{4,6},{5,7},{6,4},{7,5},{8,10},{9,11},{10,... | collective-permute-start | bytes 49160 | tf_op jit(solution)/shard_map/ppermute | solution.py:289
  98.7 11.5 %collective-permute-start.17 = (f32[64,1024]{1,0:T(8,128)S(1)}, f32[64,1024]{1,0:T(8,128)S(1)}, u32[]{:S(2)}, u32[]{:S(2)}) collective-permute-start(f32[64,1024]{1,0:T(8,128)S(1)} %get-tuple-element.30.own_ref), channel_id=1, source_target_pairs={{2,0},{7,1},{4,2},{1,3},{6,4},{3,5},{0,6},{5,7},{10,8},{15,9},{12,... | collective-permute-start | bytes 786440 | tf_op jit(solution)/shard_map/ppermute | solution.py:324
  100.7 5.5 %collective-permute-start.14 = (f32[64,64]{1,0:T(8,128)S(1)}, f32[64,64]{1,0:T(8,128)S(1)}, u32[]{:S(2)}, u32[]{:S(2)}) collective-permute-start(f32[64,64]{1,0:T(8,128)S(1)} %add_add_fusion.5), channel_id=1, source_target_pairs={{0,24},{1,25},{2,26},{3,27},{4,28},{5,29},{6,30},{7,31},{8,16},{9,... | collective-permute-start | bytes 49160 | tf_op jit(solution)/shard_map/ppermute | solution.py:289
  100.8 5.4 %collective-permute-start.13 = (f32[64,64]{1,0:T(8,128)S(1)}, f32[64,64]{1,0:T(8,128)S(1)}, u32[]{:S(2)}, u32[]{:S(2)}) collective-permute-start(f32[64,64]{1,0:T(8,128)S(1)} %add_add_fusion.5), channel_id=1, source_target_pairs={{0,16},{1,17},{2,18},{3,19},{4,20},{5,21},{6,22},{7,23},{8,24},{9,... | collective-permute-start | bytes 49160 | tf_op jit(solution)/shard_map/ppermute | solution.py:289
  102.4 3.8 %collective-permute-start.12 = (f32[64,64]{1,0:T(8,128)S(1)}, f32[64,64]{1,0:T(8,128)S(1)}, u32[]{:S(2)}, u32[]{:S(2)}) collective-permute-start(f32[64,64]{1,0:T(8,128)S(1)} %add_add_fusion.5), channel_id=1, source_target_pairs={{0,8},{1,9},{2,10},{3,11},{4,12},{5,13},{6,14},{7,15},{8,0},{9,1},... | collective-permute-start | bytes 49160 | tf_op jit(solution)/shard_map/ppermute | solution.py:289
  104.2 10.3 %collective-permute-start.18 = (f32[64,1024]{1,0:T(8,128)S(1)}, f32[64,1024]{1,0:T(8,128)S(1)}, u32[]{:S(2)}, u32[]{:S(2)}) collective-permute-start(f32[64,1024]{1,0:T(8,128)S(1)} %shard_map.43), channel_id=1, source_target_pairs={{0,2},{1,7},{2,4},{3,1},{4,6},{5,3},{6,0},{7,5},{8,10},{9,15},{10,... | collective-permute-start | bytes 786440 | tf_op jit(solution)/shard_map/ppermute | solution.py:327
  106.2 4.0 %collective-permute-start.15 = (f32[64,64]{1,0:T(8,128)S(1)}, f32[64,64]{1,0:T(8,128)S(1)}, u32[]{:S(2)}, u32[]{:S(2)}) collective-permute-start(f32[64,64]{1,0:T(8,128)S(1)} %add_add_fusion.4), channel_id=1, source_target_pairs={{0,1},{1,0},{2,3},{3,2},{4,5},{5,4},{6,7},{7,6},{8,9},{9,8},{10,11... | collective-permute-start | bytes 49160 | tf_op jit(solution)/shard_map/ppermute | solution.py:289
  117.4 9.9 %collective-permute-start.26 = (f32[64,1024]{1,0:T(8,128)S(1)}, f32[64,1024]{1,0:T(8,128)S(1)}, u32[]{:S(2)}, u32[]{:S(2)}) collective-permute-start(f32[64,1024]{1,0:T(8,128)S(1)} %get-tuple-element.32.own_ref), channel_id=1, source_target_pairs={{0,1},{1,0},{2,3},{3,2},{4,5},{5,4},{6,7},{7,6},{8,9},{9,8},{10,11... | collective-permute-start | bytes 786440 | tf_op jit(solution)/shard_map/ppermute | solution.py:321
  117.4 7.1 %collective-permute-start.21 = (f32[64,64]{1,0:T(8,128)S(1)}, f32[64,64]{1,0:T(8,128)S(1)}, u32[]{:S(2)}, u32[]{:S(2)}) collective-permute-start(f32[64,64]{1,0:T(8,128)S(1)} %get-tuple-element.31), channel_id=1, source_target_pairs={{0,6},{1,7},{2,4},{3,5},{4,2},{5,3},{6,0},{7,1},{8,14},{9,15},{10,... | collective-permute-start | bytes 49160 | tf_op jit(solution)/shard_map/ppermute | solution.py:289
  120.1 5.2 %collective-permute-start.20 = (f32[64,64]{1,0:T(8,128)S(1)}, f32[64,64]{1,0:T(8,128)S(1)}, u32[]{:S(2)}, u32[]{:S(2)}) collective-permute-start(f32[64,64]{1,0:T(8,128)S(1)} %get-tuple-element.31), channel_id=1, source_target_pairs={{0,4},{1,5},{2,6},{3,7},{4,0},{5,1},{6,2},{7,3},{8,12},{9,13},{10,... | collective-permute-start | bytes 49160 | tf_op jit(solution)/shard_map/ppermute | solution.py:289
  120.1 5.2 %collective-permute-start.19 = (f32[64,64]{1,0:T(8,128)S(1)}, f32[64,64]{1,0:T(8,128)S(1)}, u32[]{:S(2)}, u32[]{:S(2)}) collective-permute-start(f32[64,64]{1,0:T(8,128)S(1)} %get-tuple-element.31), channel_id=1, source_target_pairs={{0,2},{1,3},{2,0},{3,1},{4,6},{5,7},{6,4},{7,5},{8,10},{9,11},{10,... | collective-permute-start | bytes 49160 | tf_op jit(solution)/shard_map/ppermute | solution.py:289
  121.8 12.2 %collective-permute-start.27 = (f32[64,1024]{1,0:T(8,128)S(1)}, f32[64,1024]{1,0:T(8,128)S(1)}, u32[]{:S(2)}, u32[]{:S(2)}) collective-permute-start(f32[64,1024]{1,0:T(8,128)S(1)} %get-tuple-element.32.own_ref), channel_id=1, source_target_pairs={{2,0},{7,1},{4,2},{1,3},{6,4},{3,5},{0,6},{5,7},{10,8},{15,9},{12,... | collective-permute-start | bytes 786440 | tf_op jit(solution)/shard_map/ppermute | solution.py:324
  125.3 4.2 %collective-permute-start.24 = (f32[64,64]{1,0:T(8,128)S(1)}, f32[64,64]{1,0:T(8,128)S(1)}, u32[]{:S(2)}, u32[]{:S(2)}) collective-permute-start(f32[64,64]{1,0:T(8,128)S(1)} %add_add_fusion.3), channel_id=1, source_target_pairs={{0,24},{1,25},{2,26},{3,27},{4,28},{5,29},{6,30},{7,31},{8,16},{9,... | collective-permute-start | bytes 49160 | tf_op jit(solution)/shard_map/ppermute | solution.py:289
  125.4 4.1 %collective-permute-start.23 = (f32[64,64]{1,0:T(8,128)S(1)}, f32[64,64]{1,0:T(8,128)S(1)}, u32[]{:S(2)}, u32[]{:S(2)}) collective-permute-start(f32[64,64]{1,0:T(8,128)S(1)} %add_add_fusion.3), channel_id=1, source_target_pairs={{0,16},{1,17},{2,18},{3,19},{4,20},{5,21},{6,22},{7,23},{8,24},{9,... | collective-permute-start | bytes 49160 | tf_op jit(solution)/shard_map/ppermute | solution.py:289
  126.7 2.8 %collective-permute-start.22 = (f32[64,64]{1,0:T(8,128)S(1)}, f32[64,64]{1,0:T(8,128)S(1)}, u32[]{:S(2)}, u32[]{:S(2)}) collective-permute-start(f32[64,64]{1,0:T(8,128)S(1)} %add_add_fusion.3), channel_id=1, source_target_pairs={{0,8},{1,9},{2,10},{3,11},{4,12},{5,13},{6,14},{7,15},{8,0},{9,1},... | collective-permute-start | bytes 49160 | tf_op jit(solution)/shard_map/ppermute | solution.py:289
  128.8 10.1 %collective-permute-start.28 = (f32[64,1024]{1,0:T(8,128)S(1)}, f32[64,1024]{1,0:T(8,128)S(1)}, u32[]{:S(2)}, u32[]{:S(2)}) collective-permute-start(f32[64,1024]{1,0:T(8,128)S(1)} %shard_map.46), channel_id=1, source_target_pairs={{0,2},{1,7},{2,4},{3,1},{4,6},{5,3},{6,0},{7,5},{8,10},{9,15},{10,... | collective-permute-start | bytes 786440 | tf_op jit(solution)/shard_map/ppermute | solution.py:327
  129.6 4.4 %collective-permute-start.25 = (f32[64,64]{1,0:T(8,128)S(1)}, f32[64,64]{1,0:T(8,128)S(1)}, u32[]{:S(2)}, u32[]{:S(2)}) collective-permute-start(f32[64,64]{1,0:T(8,128)S(1)} %add_add_fusion.2), channel_id=1, source_target_pairs={{0,1},{1,0},{2,3},{3,2},{4,5},{5,4},{6,7},{7,6},{8,9},{9,8},{10,11... | collective-permute-start | bytes 49160 | tf_op jit(solution)/shard_map/ppermute | solution.py:289
  141.7 5.7 %collective-permute-start.31 = (f32[64,64]{1,0:T(8,128)S(1)}, f32[64,64]{1,0:T(8,128)S(1)}, u32[]{:S(2)}, u32[]{:S(2)}) collective-permute-start(f32[64,64]{1,0:T(8,128)S(1)} %get-tuple-element.33), channel_id=1, source_target_pairs={{0,6},{1,7},{2,4},{3,5},{4,2},{5,3},{6,0},{7,1},{8,14},{9,15},{10,... | collective-permute-start | bytes 49160 | tf_op jit(solution)/shard_map/ppermute | solution.py:289
  141.8 5.7 %collective-permute-start.30 = (f32[64,64]{1,0:T(8,128)S(1)}, f32[64,64]{1,0:T(8,128)S(1)}, u32[]{:S(2)}, u32[]{:S(2)}) collective-permute-start(f32[64,64]{1,0:T(8,128)S(1)} %get-tuple-element.33), channel_id=1, source_target_pairs={{0,4},{1,5},{2,6},{3,7},{4,0},{5,1},{6,2},{7,3},{8,12},{9,13},{10,... | collective-permute-start | bytes 49160 | tf_op jit(solution)/shard_map/ppermute | solution.py:289
  142.1 5.9 %collective-permute-start.29 = (f32[64,64]{1,0:T(8,128)S(1)}, f32[64,64]{1,0:T(8,128)S(1)}, u32[]{:S(2)}, u32[]{:S(2)}) collective-permute-start(f32[64,64]{1,0:T(8,128)S(1)} %get-tuple-element.33), channel_id=1, source_target_pairs={{0,2},{1,3},{2,0},{3,1},{4,6},{5,7},{6,4},{7,5},{8,10},{9,11},{10,... | collective-permute-start | bytes 49160 | tf_op jit(solution)/shard_map/ppermute | solution.py:289
  148.0 3.6 %collective-permute-start.34 = (f32[64,64]{1,0:T(8,128)S(1)}, f32[64,64]{1,0:T(8,128)S(1)}, u32[]{:S(2)}, u32[]{:S(2)}) collective-permute-start(f32[64,64]{1,0:T(8,128)S(1)} %add_add_fusion.1), channel_id=1, source_target_pairs={{0,24},{1,25},{2,26},{3,27},{4,28},{5,29},{6,30},{7,31},{8,16},{9,... | collective-permute-start | bytes 49160 | tf_op jit(solution)/shard_map/ppermute | solution.py:289
  148.1 4.0 %collective-permute-start.33 = (f32[64,64]{1,0:T(8,128)S(1)}, f32[64,64]{1,0:T(8,128)S(1)}, u32[]{:S(2)}, u32[]{:S(2)}) collective-permute-start(f32[64,64]{1,0:T(8,128)S(1)} %add_add_fusion.1), channel_id=1, source_target_pairs={{0,16},{1,17},{2,18},{3,19},{4,20},{5,21},{6,22},{7,23},{8,24},{9,... | collective-permute-start | bytes 49160 | tf_op jit(solution)/shard_map/ppermute | solution.py:289
  149.4 2.7 %collective-permute-start.32 = (f32[64,64]{1,0:T(8,128)S(1)}, f32[64,64]{1,0:T(8,128)S(1)}, u32[]{:S(2)}, u32[]{:S(2)}) collective-permute-start(f32[64,64]{1,0:T(8,128)S(1)} %add_add_fusion.1), channel_id=1, source_target_pairs={{0,8},{1,9},{2,10},{3,11},{4,12},{5,13},{6,14},{7,15},{8,0},{9,1},... | collective-permute-start | bytes 49160 | tf_op jit(solution)/shard_map/ppermute | solution.py:289
  152.1 4.0 %collective-permute-start.35 = (f32[64,64]{1,0:T(8,128)S(1)}, f32[64,64]{1,0:T(8,128)S(1)}, u32[]{:S(2)}, u32[]{:S(2)}) collective-permute-start(f32[64,64]{1,0:T(8,128)S(1)} %add_add_fusion), channel_id=1, source_target_pairs={{0,1},{1,0},{2,3},{3,2},{4,5},{5,4},{6,7},{7,6},{8,9},{9,8},{10,11... | collective-permute-start | bytes 49160 | tf_op jit(solution)/shard_map/ppermute | solution.py:289

commit v6 on v5

--- a/solution.py
+++ b/solution.py
@@ -75,9 +75,9 @@
         cost_estimate=pl.CostEstimate(
             flops=3 * size * width, bytes_accessed=6 * size * width, transcendentals=0
         ),
-        compiler_params=pltpu.CompilerParams(vmem_limit_bytes=61 << 20),
+        compiler_params=pltpu.CompilerParams(vmem_limit_bytes=4 << 20),
         name="unit_rows",
-    )(points)
+    )(pltpu.with_memory_space_constraint(points, pltpu.HBM))
 
 
 def affinity(rows, cols):
@@ -269,15 +269,18 @@
     out[...] = jnp.dot(factor, image[...], preferred_element_type=F32, precision=EXACT)
 
 
-def exchange_masks(row_count, col_count):
+def exchange_masks(row_count, col_count, alone):
     low = [1 << bit for bit in range(col_count.bit_length() - 1)]
     high = [col_count << bit for bit in range(row_count.bit_length() - 1)]
-    stages = [(low[1], low[2]), (high[0], high[1]), (low[0],)]
+    if alone:
+        stages = [(high[0],), (high[1], low[0]), (low[1], low[2])]
+    else:
+        stages = [(low[1], low[2]), (high[0], high[1]), (low[0],)]
     rest = high[2:] + low[3:]
     return stages + [tuple(rest[at : at + 2]) for at in range(0, len(rest), 2)]
 
 
-def total_sum(value):
+def total_sum(value, alone):
     row_count = lax.axis_size("row")
     col_count = lax.axis_size("col")
     devices = row_count * col_count
@@ -288,7 +291,7 @@
         pairs = [(source, source ^ mask) for source in range(devices)]
         return lax.ppermute(value, ("row", "col"), pairs)
 
-    for masks in exchange_masks(row_count, col_count):
+    for masks in exchange_masks(row_count, col_count, alone):
         if len(masks) == 1:
             value = value + fetched(masks[0])
         else:
@@ -326,6 +329,9 @@
     def to_z(value):
         return lax.ppermute(value, "col", [(i, side_of(i)) for i in range(col_count)])
 
+    def to_z_side(value):
+        return lax.ppermute(value, "col", [(i, side_of(i) ^ 1) for i in range(col_count)])
+
     b0 = unit_rows(embeddings, 0, size)
     z0 = from_z(b0)
     x0 = from_x(b0)
@@ -333,6 +339,9 @@
     z1 = from_z(b1)
     x1 = from_x(b1)
     far_ids = from_z(neighbour_ids)
+    start = start_vectors.T
+    start_x = from_x(start)
+    start_z = from_z(start)
 
     here = base + col
     x_side = base + (col ^ 1)
@@ -364,6 +373,8 @@
         [SMEM] * 2 + [VMEM] * 8, 7 * one, 7 * moved,
     )(own_mask, far_mask, b0, b1, x0, x1, z0, z1, degree, far_sums)
     root = lax.rsqrt(degree + to_z(far_degree))
+    root_x = lax.rsqrt(from_x(degree) + to_z_side(far_degree))
+    root_z = lax.rsqrt(from_z(degree) + far_degree)
 
     across_shape = (columns, points)
     work = 2 * columns * size * size
@@ -377,10 +388,14 @@
     advance = call(functools.partial(advance_body, scale), results, [VMEM] * 4, *effort)
     solve = call(functools.partial(solve_body, scale), wide, [VMEM] * 2, *effort)
 
-    own = (start_vectors.T * root).astype(BF16)
+    own, x, z = (
+        (value * line).astype(BF16)
+        for value, line in ((start, root), (start_x, root_x), (start_z, root_z))
+    )
     for step in range(ITERS):
-        x = from_x(own)
-        z = from_z(own)
+        if step > 0:
+            x = from_x(own)
+            z = from_z(own)
         sent = far_rows(far_mask, own, x, far0, corner, far1)
         given = to_z(sent)
         held = near_rows(own_mask, own, x, z, near0, near1, far0, far1)
@@ -388,7 +403,7 @@
             image, own, gram = join(held, given, root)
         else:
             image, own, gram = advance(total, held, given, root)
-        total = total_sum(gram)
+        total = total_sum(gram, step == ITERS - 1)
     return solve(total, image).T
 
 

time: 159 us -> 160 us (level)
  waiting for transfers between devices: 67.1 us -> 73.2 us
  Pallas kernels: 39.6 us -> 37.6 us
  starting transfers between devices: 49.2 us -> 47.5 us
    ppermute x21, waiting for transfers between devices: 13.7 us -> 20.4 us  [fetched(): return lax.ppermute(value, ('row', 'col'), pairs)]
    ppermute x6 -> x7, starting transfers between devices: 17.6 us -> 13.8 us  [from_z(): lax.ppermute(value, 'col', [(side_of(i), i) for i in range(col_count)])]
    ppermute x5 -> x6, waiting for transfers between devices: 4.96 us -> 2.19 us  [from_x(): return lax.ppermute(value, 'col', [(i, i ^ 1) for i in range(col_count)])]
    ppermute x0 -> x1, starting transfers between devices: none -> 2.44 us  [to_z_side(): lax.ppermute(value, 'col', [(i, side_of(i) ^ 1) for i in range(col_count)])]
    ppermute x5 -> x6, starting transfers between devices: 4.38 us -> 6.72 us  [from_x(): return lax.ppermute(value, 'col', [(i, i ^ 1) for i in range(col_count)])]
    ppermute x4, starting transfers between devices: 3.28 us -> 1.01 us  [to_z(): lax.ppermute(value, 'col', [(i, side_of(i)) for i in range(col_count)])]
    pallas_call x2, Pallas kernels: 5.85 us -> 3.84 us  [unit_rows(): pl.pallas_call(functools.partial(unit_rows_body, block), in_specs=[pl.Blo...]
    ppermute x6 -> x7, waiting for transfers between devices: 38.2 us -> 39.3 us  [from_z(): lax.ppermute(value, 'col', [(side_of(i), i) for i in range(col_count)])]
  transfers between devices with their start and end apart: 36 -> 39, of which waited for: 16 -> 19; matrix products, arithmetic and copies ran while one was open for 1% -> 1% of each run, Pallas kernels for 12% -> 12%
where the time goes in v6:
time: 160 us
  waiting for transfers between devices  73.2 us (46%)
  starting transfers between devices  47.5 us (30%)
  Pallas kernels  37.6 us (24%)
    ppermute x7, waiting for transfers between devices, from_z(): lax.ppermute(value, 'col', [(side_of(i), i) for i in range(col_count)])  39.3 us
    ppermute x21, starting transfers between devices, fetched(): return lax.ppermute(value, ('row', 'col'), pairs)  23.6 us
    ppermute x21, waiting for transfers between devices, fetched(): return lax.ppermute(value, ('row', 'col'), pairs)  20.4 us
    ppermute x7, starting transfers between devices, from_z(): lax.ppermute(value, 'col', [(side_of(i), i) for i in range(col_count)])  13.8 us
    ppermute x4, waiting for transfers between devices, to_z(): lax.ppermute(value, 'col', [(i, side_of(i)) for i in range(col_count)])  11.2 us
    pallas_call x1, Pallas kernels, on_device(): call(first_tiles_body, (shaped((most * size, points), BF16), shaped((most...  7.11 us
    ppermute x6, starting transfers between devices, from_x(): return lax.ppermute(value, 'col', [(i, i ^ 1) for i in range(col_count)])  6.72 us
    pallas_call x1, Pallas kernels, on_device(): call(last_tiles_body, (shaped((size, points), BF16), shaped((size, size),...  6.54 us
  transfers between devices with their start and end apart: 39, of which 19 were waited for; matrix products, arithmetic and copies ran while one was open for 1% of the time, Pallas kernels for 12%

profile of v6, /device:TPU:0, one launch (start us, length us, event | category | flops | bytes accessed | tf_op | source)
XLA Modules:
  0.0 159.9 jit_solution(9642871739523248640)
XLA Ops:
  0.0 1.9 %unit_rows.2.b0 = bf16[512,1024]{1,0:T(8,128)(2,1)S(1)} custom-call(f32[1024,1024]{1,0:T(8,128)} %points_ref.3), custom_call_target="tpu_custom_call" | custom-call | flops 1572864 | bytes 3145728 | tf_op jit(solution)/shard_map/unit_rows/pallas_call | solution.py:69
  1.9 3.0 %collective-permute-start.1 = (bf16[512,1024]{1,0:T(8,128)(2,1)S(1)}, bf16[512,1024]{1,0:T(8,128)(2,1)S(1)}, u32[]{:S(2)}, u32[]{:S(2)}) collective-permute-start(bf16[512,1024]{1,0:T(8,128)(2,1)S(1)} %unit_rows.2.b0), channel_id=1, source_target_pairs={{0,1},{1,0},{2,3},{3,2},{4,5},{5,4},{6,7},{7,6},{8,9},{9,8},{10,11... | collective-permute-start | bytes 3145736 | tf_op jit(solution)/shard_map/ppermute | solution.py:324
  5.0 3.6 %collective-permute-start.3 = (bf16[512,1024]{1,0:T(8,128)(2,1)S(1)}, bf16[512,1024]{1,0:T(8,128)(2,1)}, u32[]{:S(2)}, u32[]{:S(2)}) collective-permute-start(bf16[512,1024]{1,0:T(8,128)(2,1)S(1)} %unit_rows.2.b0), channel_id=1, source_target_pairs={{2,0},{7,1},{4,2},{1,3},{6,4},{3,5},{0,6},{5,7},{10,8},{15,9},{12,... | collective-permute-start | bytes 3145736 | tf_op jit(solution)/shard_map/ppermute | solution.py:327
  8.6 1.9 %unit_rows.3.b1 = bf16[512,1024]{1,0:T(8,128)(2,1)S(1)} custom-call(f32[1024,1024]{1,0:T(8,128)} %points_ref.3), custom_call_target="tpu_custom_call" | custom-call | flops 1572864 | bytes 3145728 | tf_op jit(solution)/shard_map/unit_rows/pallas_call | solution.py:69
  11.1 2.0 %collective-permute-start = (s32[2,12]{1,0:T(2,128)S(1)}, s32[2,12]{1,0:T(2,128)S(1)}, u32[]{:S(2)}, u32[]{:S(2)}) collective-permute-start(s32[2,12]{1,0:T(2,128)S(1)} %copy-done.1), channel_id=1, source_target_pairs={{2,0},{7,1},{4,2},{1,3},{6,4},{3,5},{0,6},{5,7},{10,8},{15,9},{12,... | collective-permute-start | bytes 296 | tf_op jit(solution)/shard_map/ppermute | solution.py:327
  13.9 39.3 %collective-permute-done = s32[2,12]{1,0:T(2,128)S(1)} collective-permute-done((s32[2,12]{1,0:T(2,128)S(1)}, s32[2,12]{1,0:T(2,128)S(1)}, u32[]{:S(2)}, u32[]{:S(2)}) %collective-permute-start) | collective-permute-done | bytes 128 | tf_op jit(solution)/shard_map/ppermute | solution.py:327
  53.7 7.1 %shard_map.37 = (bf16[1536,1024]{1,0:T(8,128)(2,1)S(1)}, bf16[1536,512]{1,0:T(8,128)(2,1)S(1)}, f32[1,1024]{1,0:T(1,128)S(1)}, f32[3,512]{1,0:T(4,128)S(1)}) custom-call(f32[2,6]{1,0:T(2,128)S(1)} %or_convert_fusion.1.own_mask.mask, bf16[512,1024]{1,0:T(8,128)(2,1)S(1)} %unit_rows.2.b0, bf16[512,1024]{1,0:T(8,128)(2,1)S(1)} %unit_rows.3.b1, ...), custom_call_target="tpu_custom_call" | custom-call | flops 4831838208 | bytes 18874368 | tf_op jit(solution)/shard_map/pallas_call | solution.py:359
  60.8 6.5 %shard_map.38 = (bf16[512,1024]{1,0:T(8,128)(2,1)S(1)}, bf16[512,512]{1,0:T(8,128)(2,1)S(1)}, bf16[2048,512]{1,0:T(8,128)(2,1)S(1)}, f32[1,1024]{1,0:T(1,128)S(1)}, f32[1,1024]{1,0:T(1,128)S(1)}) custom-call(f32[2,6]{1,0:T(2,128)S(1)} %or_convert_fusion.1.own_mask.mask, f32[2,4]{1,0:T(2,128)S(1)} %or_convert_fusion.far_mask.mask, ...), custom_call_target="tpu_custom_call" | custom-call | flops 3758096384 | bytes 14680064 | tf_op jit(solution)/shard_map/pallas_call | solution.py:367
  68.0 2.6 %collective-permute-start.6 = (f32[64,1024]{1,0:T(8,128)S(1)}, f32[64,1024]{1,0:T(8,128)S(1)}, u32[]{:S(2)}, u32[]{:S(2)}) collective-permute-start(f32[64,1024]{1,0:T(8,128)S(1)} %bitcast.10), channel_id=1, source_target_pairs={{0,1},{1,0},{2,3},{3,2},{4,5},{5,4},{6,7},{7,6},{8,9},{9,8},{10,11... | collective-permute-start | bytes 786440 | tf_op jit(solution)/shard_map/ppermute | solution.py:324
  70.5 1.4 collective-permute-start.9
  72.0 2.4 %collective-permute-start.8 = (f32[1,1024]{1,0:T(1,128)S(1)}, f32[1,1024]{1,0:T(1,128)S(1)}, u32[]{:S(2)}, u32[]{:S(2)}) collective-permute-start(f32[1,1024]{1,0:T(1,128)S(1)} %get-tuple-element.23), channel_id=1, source_target_pairs={{0,3},{1,6},{2,5},{3,0},{4,7},{5,2},{6,1},{7,4},{8,11},{9,14},{10,... | collective-permute-start | bytes 12296 | tf_op jit(solution)/shard_map/ppermute | solution.py:333
  74.4 0.9 collective-permute-start.7
  75.8 2.2 %collective-permute-done.7 = f32[1,1024]{1,0:T(1,128)S(1)} collective-permute-done((f32[1,1024]{1,0:T(1,128)S(1)}, f32[1,1024]{1,0:T(1,128)S(1)}, u32[]{:S(2)}, u32[]{:S(2)}) %collective-permute-start.7) | collective-permute-done | bytes 4128 | tf_op jit(solution)/shard_map/ppermute | solution.py:324
  78.1 1.4 shard_map.40
  79.8 2.0 %shard_map.39.near = f32[64,1024]{1,0:T(8,128)S(1)} custom-call(f32[2,6]{1,0:T(2,128)S(1)} %or_convert_fusion.1.own_mask.mask, bf16[64,1024]{1,0:T(8,128)(2,1)S(1)} %multiply_convert_fusion.2.own_ref, bf16[64,1024]{1,0:T(8,128)(2,1)S(1)} %multiply_convert_fusion.1.x_ref, bf16[64,1024]{1,0:T(8,128)(2,1)S(1)} %multiply_convert_fusion.z_ref, ...), custom_call_target="tpu_custom_call" | custom-call | flops 402653184 | bytes 6291456 | tf_op jit(solution)/shard_map/pallas_call | solution.py:401
  81.9 6.1 %collective-permute-done.11.given = f32[64,1024]{1,0:T(8,128)S(1)} collective-permute-done((f32[64,1024]{1,0:T(8,128)S(1)}, f32[64,1024]{1,0:T(8,128)S(1)}, u32[]{:S(2)}, u32[]{:S(2)}) %collective-permute-start.11) | collective-permute-done | bytes 262176 | tf_op jit(solution)/shard_map/ppermute | solution.py:330
  88.0 0.8 shard_map.41
  89.3 2.2 %collective-permute-start.13 = (f32[64,64]{1,0:T(8,128)S(1)}, f32[64,64]{1,0:T(8,128)S(1)}, u32[]{:S(2)}, u32[]{:S(2)}) collective-permute-start(f32[64,64]{1,0:T(8,128)S(1)} %get-tuple-element.29), channel_id=1, source_target_pairs={{0,4},{1,5},{2,6},{3,7},{4,0},{5,1},{6,2},{7,3},{8,12},{9,13},{10,... | collective-permute-start | bytes 49160 | tf_op jit(solution)/shard_map/ppermute | solution.py:292
  91.6 1.8 %collective-permute-start.14 = (f32[64,64]{1,0:T(8,128)S(1)}, f32[64,64]{1,0:T(8,128)S(1)}, u32[]{:S(2)}, u32[]{:S(2)}) collective-permute-start(f32[64,64]{1,0:T(8,128)S(1)} %get-tuple-element.29), channel_id=1, source_target_pairs={{0,6},{1,7},{2,4},{3,5},{4,2},{5,3},{6,0},{7,1},{8,14},{9,15},{10,... | collective-permute-start | bytes 49160 | tf_op jit(solution)/shard_map/ppermute | solution.py:292
  93.3 2.0 %collective-permute-start.20 = (f32[64,1024]{1,0:T(8,128)S(1)}, f32[64,1024]{1,0:T(8,128)S(1)}, u32[]{:S(2)}, u32[]{:S(2)}) collective-permute-start(f32[64,1024]{1,0:T(8,128)S(1)} %get-tuple-element.30.own_ref), channel_id=1, source_target_pairs={{2,0},{7,1},{4,2},{1,3},{6,4},{3,5},{0,6},{5,7},{10,8},{15,9},{12,... | collective-permute-start | bytes 786440 | tf_op jit(solution)/shard_map/ppermute | solution.py:327
  95.4 2.0 %collective-permute-done.14 = f32[64,64]{1,0:T(8,128)S(1)} collective-permute-done((f32[64,64]{1,0:T(8,128)S(1)}, f32[64,64]{1,0:T(8,128)S(1)}, u32[]{:S(2)}, u32[]{:S(2)}) %collective-permute-start.14) | collective-permute-done | bytes 16416 | tf_op jit(solution)/shard_map/ppermute | solution.py:292
  97.5 1.6 %collective-permute-start.16 = (f32[64,64]{1,0:T(8,128)S(1)}, f32[64,64]{1,0:T(8,128)S(1)}, u32[]{:S(2)}, u32[]{:S(2)}) collective-permute-start(f32[64,64]{1,0:T(8,128)S(1)} %add_add_fusion.5), channel_id=1, source_target_pairs={{0,16},{1,17},{2,18},{3,19},{4,20},{5,21},{6,22},{7,23},{8,24},{9,... | collective-permute-start | bytes 49160 | tf_op jit(solution)/shard_map/ppermute | solution.py:292
  99.3 1.5 shard_map.43
  101.5 1.0 collective-permute-done.17
  102.4 2.2 %collective-permute-start.18 = (f32[64,64]{1,0:T(8,128)S(1)}, f32[64,64]{1,0:T(8,128)S(1)}, u32[]{:S(2)}, u32[]{:S(2)}) collective-permute-start(f32[64,64]{1,0:T(8,128)S(1)} %add_add_fusion.4), channel_id=1, source_target_pairs={{0,1},{1,0},{2,3},{3,2},{4,5},{5,4},{6,7},{7,6},{8,9},{9,8},{10,11... | collective-permute-start | bytes 49160 | tf_op jit(solution)/shard_map/ppermute | solution.py:292
  104.7 1.9 %collective-permute-done.18 = f32[64,64]{1,0:T(8,128)S(1)} collective-permute-done((f32[64,64]{1,0:T(8,128)S(1)}, f32[64,64]{1,0:T(8,128)S(1)}, u32[]{:S(2)}, u32[]{:S(2)}) %collective-permute-start.18) | collective-permute-done | bytes 16416 | tf_op jit(solution)/shard_map/ppermute | solution.py:292
  106.6 2.2 %shard_map.42.near = f32[64,1024]{1,0:T(8,128)S(1)} custom-call(f32[2,6]{1,0:T(2,128)S(1)} %or_convert_fusion.1.own_mask.mask, f32[64,1024]{1,0:T(8,128)S(1)} %get-tuple-element.30.own_ref, f32[64,1024]{1,0:T(8,128)S(1)} %collective-permute-done.19.x_ref, f32[64,1024]{1,0:T(8,128)S(1)} %collective-permute-done.20.z_ref, ...), custom_call_target="tpu_custom_call" | custom-call | flops 402653184 | bytes 6291456 | tf_op jit(solution)/shard_map/pallas_call | solution.py:401
  108.8 2.5 %collective-permute-done.21.given = f32[64,1024]{1,0:T(8,128)S(1)} collective-permute-done((f32[64,1024]{1,0:T(8,128)S(1)}, f32[64,1024]{1,0:T(8,128)S(1)}, u32[]{:S(2)}, u32[]{:S(2)}) %collective-permute-start.21) | collective-permute-done | bytes 262176 | tf_op jit(solution)/shard_map/ppermute | solution.py:330
  111.3 2.8 %shard_map.44 = (f32[64,1024]{1,0:T(8,128)}, f32[64,1024]{1,0:T(8,128)S(1)}, f32[64,64]{1,0:T(8,128)S(1)}) custom-call(f32[64,64]{1,0:T(8,128)S(1)} %add.130.total, f32[64,1024]{1,0:T(8,128)S(1)} %shard_map.42.near, f32[64,1024]{1,0:T(8,128)S(1)} %collective-permute-done.21.given, f32[1,1024]{1,0:T(1,128)S(1)} %add_rsqrt_fusion.2.root), custom_call_target="tpu_custom_call" | custom-call | flops 8388608 | bytes 262144 | tf_op jit(solution)/shard_map/pallas_call | solution.py:405
  114.1 4.2 %collective-permute-start.23 = (f32[64,64]{1,0:T(8,128)S(1)}, f32[64,64]{1,0:T(8,128)S(1)}, u32[]{:S(2)}, u32[]{:S(2)}) collective-permute-start(f32[64,64]{1,0:T(8,128)S(1)} %get-tuple-element.31), channel_id=1, source_target_pairs={{0,4},{1,5},{2,6},{3,7},{4,0},{5,1},{6,2},{7,3},{8,12},{9,13},{10,... | collective-permute-start | bytes 49160 | tf_op jit(solution)/shard_map/ppermute | solution.py:292
  118.5 3.7 %collective-permute-start.30 = (f32[64,1024]{1,0:T(8,128)S(1)}, f32[64,1024]{1,0:T(8,128)S(1)}, u32[]{:S(2)}, u32[]{:S(2)}) collective-permute-start(f32[64,1024]{1,0:T(8,128)S(1)} %get-tuple-element.32.own_ref), channel_id=1, source_target_pairs={{2,0},{7,1},{4,2},{1,3},{6,4},{3,5},{0,6},{5,7},{10,8},{15,9},{12,... | collective-permute-start | bytes 786440 | tf_op jit(solution)/shard_map/ppermute | solution.py:327
  122.2 2.2 %collective-permute-done.24 = f32[64,64]{1,0:T(8,128)S(1)} collective-permute-done((f32[64,64]{1,0:T(8,128)S(1)}, f32[64,64]{1,0:T(8,128)S(1)}, u32[]{:S(2)}, u32[]{:S(2)}) %collective-permute-start.24) | collective-permute-done | bytes 16416 | tf_op jit(solution)/shard_map/ppermute | solution.py:292
  124.5 1.6 %collective-permute-start.26 = (f32[64,64]{1,0:T(8,128)S(1)}, f32[64,64]{1,0:T(8,128)S(1)}, u32[]{:S(2)}, u32[]{:S(2)}) collective-permute-start(f32[64,64]{1,0:T(8,128)S(1)} %add_add_fusion.3), channel_id=1, source_target_pairs={{0,16},{1,17},{2,18},{3,19},{4,20},{5,21},{6,22},{7,23},{8,24},{9,... | collective-permute-start | bytes 49160 | tf_op jit(solution)/shard_map/ppermute | solution.py:292
  126.4 1.5 shard_map.46
  128.5 1.0 collective-permute-done.27
  130.2 3.2 %collective-permute-done.28 = f32[64,64]{1,0:T(8,128)S(1)} collective-permute-done((f32[64,64]{1,0:T(8,128)S(1)}, f32[64,64]{1,0:T(8,128)S(1)}, u32[]{:S(2)}, u32[]{:S(2)}) %collective-permute-start.28) | collective-permute-done | bytes 16416 | tf_op jit(solution)/shard_map/ppermute | solution.py:292
  133.5 2.2 %shard_map.45.near = f32[64,1024]{1,0:T(8,128)S(1)} custom-call(f32[2,6]{1,0:T(2,128)S(1)} %or_convert_fusion.1.own_mask.mask, f32[64,1024]{1,0:T(8,128)S(1)} %get-tuple-element.32.own_ref, f32[64,1024]{1,0:T(8,128)S(1)} %collective-permute-done.29.x_ref, f32[64,1024]{1,0:T(8,128)S(1)} %collective-permute-done.30.z_ref, ...), custom_call_target="tpu_custom_call" | custom-call | flops 402653184 | bytes 6291456 | tf_op jit(solution)/shard_map/pallas_call | solution.py:401
  135.7 2.6 %collective-permute-done.31.given = f32[64,1024]{1,0:T(8,128)S(1)} collective-permute-done((f32[64,1024]{1,0:T(8,128)S(1)}, f32[64,1024]{1,0:T(8,128)S(1)}, u32[]{:S(2)}, u32[]{:S(2)}) %collective-permute-start.31) | collective-permute-done | bytes 262176 | tf_op jit(solution)/shard_map/ppermute | solution.py:330
  138.3 2.8 %shard_map.47 = (f32[64,1024]{1,0:T(8,128)S(1)}, f32[64,1024]{1,0:T(8,128)}, f32[64,64]{1,0:T(8,128)S(1)}) custom-call(f32[64,64]{1,0:T(8,128)S(1)} %add.137.total, f32[64,1024]{1,0:T(8,128)S(1)} %shard_map.45.near, f32[64,1024]{1,0:T(8,128)S(1)} %collective-permute-done.31.given, f32[1,1024]{1,0:T(1,128)S(1)} %add_rsqrt_fusion.2.root), custom_call_target="tpu_custom_call" | custom-call | flops 8388608 | bytes 262144 | tf_op jit(solution)/shard_map/pallas_call | solution.py:405
  141.2 1.2 collective-permute-done.32
  142.4 1.5 collective-permute-start.33
  143.9 1.9 %collective-permute-start.35 = (f32[64,64]{1,0:T(8,128)S(1)}, f32[64,64]{1,0:T(8,128)S(1)}, u32[]{:S(2)}, u32[]{:S(2)}) collective-permute-start(f32[64,64]{1,0:T(8,128)S(1)} %add.138), channel_id=1, source_target_pairs={{0,17},{1,16},{2,19},{3,18},{4,21},{5,20},{6,23},{7,22},{8,25},{9,... | collective-permute-start | bytes 49160 | tf_op jit(solution)/shard_map/ppermute | solution.py:292
  146.3 1.5 collective-permute-done.34
  147.8 0.9 collective-permute-done.35
  148.8 2.7 %collective-permute-start.37 = (f32[64,64]{1,0:T(8,128)S(1)}, f32[64,64]{1,0:T(8,128)S(1)}, u32[]{:S(2)}, u32[]{:S(2)}) collective-permute-start(f32[64,64]{1,0:T(8,128)S(1)} %add_add_fusion.1), channel_id=1, source_target_pairs={{0,4},{1,5},{2,6},{3,7},{4,0},{5,1},{6,2},{7,3},{8,12},{9,13},{10,... | collective-permute-start | bytes 49160 | tf_op jit(solution)/shard_map/ppermute | solution.py:292
  151.6 1.6 %collective-permute-start.38 = (f32[64,64]{1,0:T(8,128)S(1)}, f32[64,64]{1,0:T(8,128)S(1)}, u32[]{:S(2)}, u32[]{:S(2)}) collective-permute-start(f32[64,64]{1,0:T(8,128)S(1)} %add_add_fusion.1), channel_id=1, source_target_pairs={{0,6},{1,7},{2,4},{3,5},{4,2},{5,3},{6,0},{7,1},{8,14},{9,15},{10,... | collective-permute-start | bytes 49160 | tf_op jit(solution)/shard_map/ppermute | solution.py:292
  153.7 3.6 %collective-permute-done.38 = f32[64,64]{1,0:T(8,128)S(1)} collective-permute-done((f32[64,64]{1,0:T(8,128)S(1)}, f32[64,64]{1,0:T(8,128)S(1)}, u32[]{:S(2)}, u32[]{:S(2)}) %collective-permute-start.38) | collective-permute-done | bytes 16416 | tf_op jit(solution)/shard_map/ppermute | solution.py:292
  157.3 2.7 %shard_map.48 = f32[64,1024]{1,0:T(8,128)} custom-call(f32[64,64]{1,0:T(8,128)S(1)} %add_add_fusion.total, f32[64,1024]{1,0:T(8,128)S(1)} %get-tuple-element.34.image), custom_call_target="tpu_custom_call" | custom-call | flops 8388608 | bytes 262144 | tf_op jit(solution)/shard_map/pallas_call | solution.py:407
  (72 shorter events, 7.7 us)
Async XLA Ops:
  1.9 9.2 %copy-start.1 = (s32[2,12]{1,0:T(2,128)S(1)}, s32[2,12]{1,0:T(2,128)}, u32[]{:S(2)}) copy-start(s32[2,12]{1,0:T(2,128)} %param.4) | copy-start | bytes 292
  1.9 51.7 %collective-permute-start.1 = (bf16[512,1024]{1,0:T(8,128)(2,1)S(1)}, bf16[512,1024]{1,0:T(8,128)(2,1)S(1)}, u32[]{:S(2)}, u32[]{:S(2)}) collective-permute-start(bf16[512,1024]{1,0:T(8,128)(2,1)S(1)} %unit_rows.2.b0), channel_id=1, source_target_pairs={{0,1},{1,0},{2,3},{3,2},{4,5},{5,4},{6,7},{7,6},{8,9},{9,8},{10,11... | collective-permute-start | bytes 3145736 | tf_op jit(solution)/shard_map/ppermute | solution.py:324
  5.0 48.7 %collective-permute-start.3 = (bf16[512,1024]{1,0:T(8,128)(2,1)S(1)}, bf16[512,1024]{1,0:T(8,128)(2,1)}, u32[]{:S(2)}, u32[]{:S(2)}) collective-permute-start(bf16[512,1024]{1,0:T(8,128)(2,1)S(1)} %unit_rows.2.b0), channel_id=1, source_target_pairs={{2,0},{7,1},{4,2},{1,3},{6,4},{3,5},{0,6},{5,7},{10,8},{15,9},{12,... | collective-permute-start | bytes 3145736 | tf_op jit(solution)/shard_map/ppermute | solution.py:327
  10.5 50.3 %collective-permute-start.2 = (bf16[512,1024]{1,0:T(8,128)(2,1)S(1)}, bf16[512,1024]{1,0:T(8,128)(2,1)}, u32[]{:S(2)}, u32[]{:S(2)}) collective-permute-start(bf16[512,1024]{1,0:T(8,128)(2,1)S(1)} %unit_rows.3.b1), channel_id=1, source_target_pairs={{0,1},{1,0},{2,3},{3,2},{4,5},{5,4},{6,7},{7,6},{8,9},{9,8},{10,11... | collective-permute-start | bytes 3145736 | tf_op jit(solution)/shard_map/ppermute | solution.py:324
  10.6 50.2 %collective-permute-start.4 = (bf16[512,1024]{1,0:T(8,128)(2,1)S(1)}, bf16[512,1024]{1,0:T(8,128)(2,1)}, u32[]{:S(2)}, u32[]{:S(2)}) collective-permute-start(bf16[512,1024]{1,0:T(8,128)(2,1)S(1)} %unit_rows.3.b1), channel_id=1, source_target_pairs={{2,0},{7,1},{4,2},{1,3},{6,4},{3,5},{0,6},{5,7},{10,8},{15,9},{12,... | collective-permute-start | bytes 3145736 | tf_op jit(solution)/shard_map/ppermute | solution.py:327
  11.1 42.1 %collective-permute-start = (s32[2,12]{1,0:T(2,128)S(1)}, s32[2,12]{1,0:T(2,128)S(1)}, u32[]{:S(2)}, u32[]{:S(2)}) collective-permute-start(s32[2,12]{1,0:T(2,128)S(1)} %copy-done.1), channel_id=1, source_target_pairs={{2,0},{7,1},{4,2},{1,3},{6,4},{3,5},{0,6},{5,7},{10,8},{15,9},{12,... | collective-permute-start | bytes 296 | tf_op jit(solution)/shard_map/ppermute | solution.py:327
  60.8 7.1 %copy-start = (f32[1024,64]{0,1:T(8,128)S(1)}, f32[1024,64]{0,1:T(8,128)}, u32[]{:S(2)}) copy-start(f32[1024,64]{0,1:T(8,128)} %param.5) | copy-start | bytes 786436
  67.4 7.9 %collective-permute-start.5 = (f32[1,1024]{1,0:T(1,128)S(1)}, f32[1,1024]{1,0:T(1,128)S(1)}, u32[]{:S(2)}, u32[]{:S(2)}) collective-permute-start(f32[1,1024]{1,0:T(1,128)S(1)} %get-tuple-element.23), channel_id=1, source_target_pairs={{0,2},{1,7},{2,4},{3,1},{4,6},{5,3},{6,0},{7,5},{8,10},{9,15},{10,... | collective-permute-start | bytes 12296 | tf_op jit(solution)/shard_map/ppermute | solution.py:330
  68.0 10.1 %collective-permute-start.6 = (f32[64,1024]{1,0:T(8,128)S(1)}, f32[64,1024]{1,0:T(8,128)S(1)}, u32[]{:S(2)}, u32[]{:S(2)}) collective-permute-start(f32[64,1024]{1,0:T(8,128)S(1)} %bitcast.10), channel_id=1, source_target_pairs={{0,1},{1,0},{2,3},{3,2},{4,5},{5,4},{6,7},{7,6},{8,9},{9,8},{10,11... | collective-permute-start | bytes 786440 | tf_op jit(solution)/shard_map/ppermute | solution.py:324
  70.5 9.3 %collective-permute-start.9 = (f32[64,1024]{1,0:T(8,128)S(1)}, f32[64,1024]{1,0:T(8,128)S(1)}, u32[]{:S(2)}, u32[]{:S(2)}) collective-permute-start(f32[64,1024]{1,0:T(8,128)S(1)} %bitcast.11), channel_id=1, source_target_pairs={{2,0},{7,1},{4,2},{1,3},{6,4},{3,5},{0,6},{5,7},{10,8},{15,9},{12,... | collective-permute-start | bytes 786440 | tf_op jit(solution)/shard_map/ppermute | solution.py:327
  72.0 6.0 %collective-permute-start.8 = (f32[1,1024]{1,0:T(1,128)S(1)}, f32[1,1024]{1,0:T(1,128)S(1)}, u32[]{:S(2)}, u32[]{:S(2)}) collective-permute-start(f32[1,1024]{1,0:T(1,128)S(1)} %get-tuple-element.23), channel_id=1, source_target_pairs={{0,3},{1,6},{2,5},{3,0},{4,7},{5,2},{6,1},{7,4},{8,11},{9,14},{10,... | collective-permute-start | bytes 12296 | tf_op jit(solution)/shard_map/ppermute | solution.py:333
  74.4 3.6 %collective-permute-start.7 = (f32[1,1024]{1,0:T(1,128)S(1)}, f32[1,1024]{1,0:T(1,128)S(1)}, u32[]{:S(2)}, u32[]{:S(2)}) collective-permute-start(f32[1,1024]{1,0:T(1,128)S(1)} %get-tuple-element.22), channel_id=1, source_target_pairs={{0,1},{1,0},{2,3},{3,2},{4,5},{5,4},{6,7},{7,6},{8,9},{9,8},{10,11... | collective-permute-start | bytes 12296 | tf_op jit(solution)/shard_map/ppermute | solution.py:324
  75.3 4.5 %collective-permute-start.10 = (f32[1,1024]{1,0:T(1,128)S(1)}, f32[1,1024]{1,0:T(1,128)S(1)}, u32[]{:S(2)}, u32[]{:S(2)}) collective-permute-start(f32[1,1024]{1,0:T(1,128)S(1)} %get-tuple-element.22), channel_id=1, source_target_pairs={{2,0},{7,1},{4,2},{1,3},{6,4},{3,5},{0,6},{5,7},{10,8},{15,9},{12,... | collective-permute-start | bytes 12296 | tf_op jit(solution)/shard_map/ppermute | solution.py:327
  79.5 8.5 %collective-permute-start.11 = (f32[64,1024]{1,0:T(8,128)S(1)}, f32[64,1024]{1,0:T(8,128)S(1)}, u32[]{:S(2)}, u32[]{:S(2)}) collective-permute-start(f32[64,1024]{1,0:T(8,128)S(1)} %shard_map.40), channel_id=1, source_target_pairs={{0,2},{1,7},{2,4},{3,1},{4,6},{5,3},{6,0},{7,5},{8,10},{9,15},{10,... | collective-permute-start | bytes 786440 | tf_op jit(solution)/shard_map/ppermute | solution.py:330
  88.8 10.5 %collective-permute-start.19 = (f32[64,1024]{1,0:T(8,128)S(1)}, f32[64,1024]{1,0:T(8,128)S(1)}, u32[]{:S(2)}, u32[]{:S(2)}) collective-permute-start(f32[64,1024]{1,0:T(8,128)S(1)} %get-tuple-element.30.own_ref), channel_id=1, source_target_pairs={{0,1},{1,0},{2,3},{3,2},{4,5},{5,4},{6,7},{7,6},{8,9},{9,8},{10,11... | collective-permute-start | bytes 786440 | tf_op jit(solution)/shard_map/ppermute | solution.py:324
  89.0 6.4 %collective-permute-start.12 = (f32[64,64]{1,0:T(8,128)S(1)}, f32[64,64]{1,0:T(8,128)S(1)}, u32[]{:S(2)}, u32[]{:S(2)}) collective-permute-start(f32[64,64]{1,0:T(8,128)S(1)} %get-tuple-element.29), channel_id=1, source_target_pairs={{0,2},{1,3},{2,0},{3,1},{4,6},{5,7},{6,4},{7,5},{8,10},{9,11},{10,... | collective-permute-start | bytes 49160 | tf_op jit(solution)/shard_map/ppermute | solution.py:292
  89.3 6.1 %collective-permute-start.13 = (f32[64,64]{1,0:T(8,128)S(1)}, f32[64,64]{1,0:T(8,128)S(1)}, u32[]{:S(2)}, u32[]{:S(2)}) collective-permute-start(f32[64,64]{1,0:T(8,128)S(1)} %get-tuple-element.29), channel_id=1, source_target_pairs={{0,4},{1,5},{2,6},{3,7},{4,0},{5,1},{6,2},{7,3},{8,12},{9,13},{10,... | collective-permute-start | bytes 49160 | tf_op jit(solution)/shard_map/ppermute | solution.py:292
  91.6 5.8 %collective-permute-start.14 = (f32[64,64]{1,0:T(8,128)S(1)}, f32[64,64]{1,0:T(8,128)S(1)}, u32[]{:S(2)}, u32[]{:S(2)}) collective-permute-start(f32[64,64]{1,0:T(8,128)S(1)} %get-tuple-element.29), channel_id=1, source_target_pairs={{0,6},{1,7},{2,4},{3,5},{4,2},{5,3},{6,0},{7,1},{8,14},{9,15},{10,... | collective-permute-start | bytes 49160 | tf_op jit(solution)/shard_map/ppermute | solution.py:292
  93.3 13.2 %collective-permute-start.20 = (f32[64,1024]{1,0:T(8,128)S(1)}, f32[64,1024]{1,0:T(8,128)S(1)}, u32[]{:S(2)}, u32[]{:S(2)}) collective-permute-start(f32[64,1024]{1,0:T(8,128)S(1)} %get-tuple-element.30.own_ref), channel_id=1, source_target_pairs={{2,0},{7,1},{4,2},{1,3},{6,4},{3,5},{0,6},{5,7},{10,8},{15,9},{12,... | collective-permute-start | bytes 786440 | tf_op jit(solution)/shard_map/ppermute | solution.py:327
  97.4 3.5 %collective-permute-start.15 = (f32[64,64]{1,0:T(8,128)S(1)}, f32[64,64]{1,0:T(8,128)S(1)}, u32[]{:S(2)}, u32[]{:S(2)}) collective-permute-start(f32[64,64]{1,0:T(8,128)S(1)} %add_add_fusion.5), channel_id=1, source_target_pairs={{0,8},{1,9},{2,10},{3,11},{4,12},{5,13},{6,14},{7,15},{8,0},{9,1},... | collective-permute-start | bytes 49160 | tf_op jit(solution)/shard_map/ppermute | solution.py:292
  97.5 4.0 %collective-permute-start.16 = (f32[64,64]{1,0:T(8,128)S(1)}, f32[64,64]{1,0:T(8,128)S(1)}, u32[]{:S(2)}, u32[]{:S(2)}) collective-permute-start(f32[64,64]{1,0:T(8,128)S(1)} %add_add_fusion.5), channel_id=1, source_target_pairs={{0,16},{1,17},{2,18},{3,19},{4,20},{5,21},{6,22},{7,23},{8,24},{9,... | collective-permute-start | bytes 49160 | tf_op jit(solution)/shard_map/ppermute | solution.py:292
  99.1 3.4 %collective-permute-start.17 = (f32[64,64]{1,0:T(8,128)S(1)}, f32[64,64]{1,0:T(8,128)S(1)}, u32[]{:S(2)}, u32[]{:S(2)}) collective-permute-start(f32[64,64]{1,0:T(8,128)S(1)} %add_add_fusion.5), channel_id=1, source_target_pairs={{0,24},{1,25},{2,26},{3,27},{4,28},{5,29},{6,30},{7,31},{8,16},{9,... | collective-permute-start | bytes 49160 | tf_op jit(solution)/shard_map/ppermute | solution.py:292
  100.9 10.4 %collective-permute-start.21 = (f32[64,1024]{1,0:T(8,128)S(1)}, f32[64,1024]{1,0:T(8,128)S(1)}, u32[]{:S(2)}, u32[]{:S(2)}) collective-permute-start(f32[64,1024]{1,0:T(8,128)S(1)} %shard_map.43), channel_id=1, source_target_pairs={{0,2},{1,7},{2,4},{3,1},{4,6},{5,3},{6,0},{7,5},{8,10},{9,15},{10,... | collective-permute-start | bytes 786440 | tf_op jit(solution)/shard_map/ppermute | solution.py:330
  102.4 4.1 %collective-permute-start.18 = (f32[64,64]{1,0:T(8,128)S(1)}, f32[64,64]{1,0:T(8,128)S(1)}, u32[]{:S(2)}, u32[]{:S(2)}) collective-permute-start(f32[64,64]{1,0:T(8,128)S(1)} %add_add_fusion.4), channel_id=1, source_target_pairs={{0,1},{1,0},{2,3},{3,2},{4,5},{5,4},{6,7},{7,6},{8,9},{9,8},{10,11... | collective-permute-start | bytes 49160 | tf_op jit(solution)/shard_map/ppermute | solution.py:292
  114.1 12.2 %collective-permute-start.29 = (f32[64,1024]{1,0:T(8,128)S(1)}, f32[64,1024]{1,0:T(8,128)S(1)}, u32[]{:S(2)}, u32[]{:S(2)}) collective-permute-start(f32[64,1024]{1,0:T(8,128)S(1)} %get-tuple-element.32.own_ref), channel_id=1, source_target_pairs={{0,1},{1,0},{2,3},{3,2},{4,5},{5,4},{6,7},{7,6},{8,9},{9,8},{10,11... | collective-permute-start | bytes 786440 | tf_op jit(solution)/shard_map/ppermute | solution.py:324
  114.1 8.1 %collective-permute-start.22 = (f32[64,64]{1,0:T(8,128)S(1)}, f32[64,64]{1,0:T(8,128)S(1)}, u32[]{:S(2)}, u32[]{:S(2)}) collective-permute-start(f32[64,64]{1,0:T(8,128)S(1)} %get-tuple-element.31), channel_id=1, source_target_pairs={{0,2},{1,3},{2,0},{3,1},{4,6},{5,7},{6,4},{7,5},{8,10},{9,11},{10,... | collective-permute-start | bytes 49160 | tf_op jit(solution)/shard_map/ppermute | solution.py:292
  114.1 8.1 %collective-permute-start.23 = (f32[64,64]{1,0:T(8,128)S(1)}, f32[64,64]{1,0:T(8,128)S(1)}, u32[]{:S(2)}, u32[]{:S(2)}) collective-permute-start(f32[64,64]{1,0:T(8,128)S(1)} %get-tuple-element.31), channel_id=1, source_target_pairs={{0,4},{1,5},{2,6},{3,7},{4,0},{5,1},{6,2},{7,3},{8,12},{9,13},{10,... | collective-permute-start | bytes 49160 | tf_op jit(solution)/shard_map/ppermute | solution.py:292
  118.4 6.1 %collective-permute-start.24 = (f32[64,64]{1,0:T(8,128)S(1)}, f32[64,64]{1,0:T(8,128)S(1)}, u32[]{:S(2)}, u32[]{:S(2)}) collective-permute-start(f32[64,64]{1,0:T(8,128)S(1)} %get-tuple-element.31), channel_id=1, source_target_pairs={{0,6},{1,7},{2,4},{3,5},{4,2},{5,3},{6,0},{7,1},{8,14},{9,15},{10,... | collective-permute-start | bytes 49160 | tf_op jit(solution)/shard_map/ppermute | solution.py:292
  118.5 15.0 %collective-permute-start.30 = (f32[64,1024]{1,0:T(8,128)S(1)}, f32[64,1024]{1,0:T(8,128)S(1)}, u32[]{:S(2)}, u32[]{:S(2)}) collective-permute-start(f32[64,1024]{1,0:T(8,128)S(1)} %get-tuple-element.32.own_ref), channel_id=1, source_target_pairs={{2,0},{7,1},{4,2},{1,3},{6,4},{3,5},{0,6},{5,7},{10,8},{15,9},{12,... | collective-permute-start | bytes 786440 | tf_op jit(solution)/shard_map/ppermute | solution.py:327
  124.4 3.6 %collective-permute-start.25 = (f32[64,64]{1,0:T(8,128)S(1)}, f32[64,64]{1,0:T(8,128)S(1)}, u32[]{:S(2)}, u32[]{:S(2)}) collective-permute-start(f32[64,64]{1,0:T(8,128)S(1)} %add_add_fusion.3), channel_id=1, source_target_pairs={{0,8},{1,9},{2,10},{3,11},{4,12},{5,13},{6,14},{7,15},{8,0},{9,1},... | collective-permute-start | bytes 49160 | tf_op jit(solution)/shard_map/ppermute | solution.py:292
  124.5 4.0 %collective-permute-start.26 = (f32[64,64]{1,0:T(8,128)S(1)}, f32[64,64]{1,0:T(8,128)S(1)}, u32[]{:S(2)}, u32[]{:S(2)}) collective-permute-start(f32[64,64]{1,0:T(8,128)S(1)} %add_add_fusion.3), channel_id=1, source_target_pairs={{0,16},{1,17},{2,18},{3,19},{4,20},{5,21},{6,22},{7,23},{8,24},{9,... | collective-permute-start | bytes 49160 | tf_op jit(solution)/shard_map/ppermute | solution.py:292
  126.1 3.4 %collective-permute-start.27 = (f32[64,64]{1,0:T(8,128)S(1)}, f32[64,64]{1,0:T(8,128)S(1)}, u32[]{:S(2)}, u32[]{:S(2)}) collective-permute-start(f32[64,64]{1,0:T(8,128)S(1)} %add_add_fusion.3), channel_id=1, source_target_pairs={{0,24},{1,25},{2,26},{3,27},{4,28},{5,29},{6,30},{7,31},{8,16},{9,... | collective-permute-start | bytes 49160 | tf_op jit(solution)/shard_map/ppermute | solution.py:292
  127.9 10.4 %collective-permute-start.31 = (f32[64,1024]{1,0:T(8,128)S(1)}, f32[64,1024]{1,0:T(8,128)S(1)}, u32[]{:S(2)}, u32[]{:S(2)}) collective-permute-start(f32[64,1024]{1,0:T(8,128)S(1)} %shard_map.46), channel_id=1, source_target_pairs={{0,2},{1,7},{2,4},{3,1},{4,6},{5,3},{6,0},{7,5},{8,10},{9,15},{10,... | collective-permute-start | bytes 786440 | tf_op jit(solution)/shard_map/ppermute | solution.py:330
  129.5 4.0 %collective-permute-start.28 = (f32[64,64]{1,0:T(8,128)S(1)}, f32[64,64]{1,0:T(8,128)S(1)}, u32[]{:S(2)}, u32[]{:S(2)}) collective-permute-start(f32[64,64]{1,0:T(8,128)S(1)} %add_add_fusion.2), channel_id=1, source_target_pairs={{0,1},{1,0},{2,3},{3,2},{4,5},{5,4},{6,7},{7,6},{8,9},{9,8},{10,11... | collective-permute-start | bytes 49160 | tf_op jit(solution)/shard_map/ppermute | solution.py:292
  141.2 1.2 collective-permute-start.32
  142.4 3.9 %collective-permute-start.33 = (f32[64,64]{1,0:T(8,128)S(1)}, f32[64,64]{1,0:T(8,128)S(1)}, u32[]{:S(2)}, u32[]{:S(2)}) collective-permute-start(f32[64,64]{1,0:T(8,128)S(1)} %add.138), channel_id=1, source_target_pairs={{0,16},{1,17},{2,18},{3,19},{4,20},{5,21},{6,22},{7,23},{8,24},{9,... | collective-permute-start | bytes 49160 | tf_op jit(solution)/shard_map/ppermute | solution.py:292
  143.9 3.9 %collective-permute-start.34 = (f32[64,64]{1,0:T(8,128)S(1)}, f32[64,64]{1,0:T(8,128)S(1)}, u32[]{:S(2)}, u32[]{:S(2)}) collective-permute-start(f32[64,64]{1,0:T(8,128)S(1)} %add.138), channel_id=1, source_target_pairs={{0,1},{1,0},{2,3},{3,2},{4,5},{5,4},{6,7},{7,6},{8,9},{9,8},{10,11... | collective-permute-start | bytes 49160 | tf_op jit(solution)/shard_map/ppermute | solution.py:292
  143.9 4.8 %collective-permute-start.35 = (f32[64,64]{1,0:T(8,128)S(1)}, f32[64,64]{1,0:T(8,128)S(1)}, u32[]{:S(2)}, u32[]{:S(2)}) collective-permute-start(f32[64,64]{1,0:T(8,128)S(1)} %add.138), channel_id=1, source_target_pairs={{0,17},{1,16},{2,19},{3,18},{4,21},{5,20},{6,23},{7,22},{8,25},{9,... | collective-permute-start | bytes 49160 | tf_op jit(solution)/shard_map/ppermute | solution.py:292
  148.7 4.5 %collective-permute-start.36 = (f32[64,64]{1,0:T(8,128)S(1)}, f32[64,64]{1,0:T(8,128)S(1)}, u32[]{:S(2)}, u32[]{:S(2)}) collective-permute-start(f32[64,64]{1,0:T(8,128)S(1)} %add_add_fusion.1), channel_id=1, source_target_pairs={{0,2},{1,3},{2,0},{3,1},{4,6},{5,7},{6,4},{7,5},{8,10},{9,11},{10,... | collective-permute-start | bytes 49160 | tf_op jit(solution)/shard_map/ppermute | solution.py:292
  148.8 4.9 %collective-permute-start.37 = (f32[64,64]{1,0:T(8,128)S(1)}, f32[64,64]{1,0:T(8,128)S(1)}, u32[]{:S(2)}, u32[]{:S(2)}) collective-permute-start(f32[64,64]{1,0:T(8,128)S(1)} %add_add_fusion.1), channel_id=1, source_target_pairs={{0,4},{1,5},{2,6},{3,7},{4,0},{5,1},{6,2},{7,3},{8,12},{9,13},{10,... | collective-permute-start | bytes 49160 | tf_op jit(solution)/shard_map/ppermute | solution.py:292
  151.6 5.7 %collective-permute-start.38 = (f32[64,64]{1,0:T(8,128)S(1)}, f32[64,64]{1,0:T(8,128)S(1)}, u32[]{:S(2)}, u32[]{:S(2)}) collective-permute-start(f32[64,64]{1,0:T(8,128)S(1)} %add_add_fusion.1), channel_id=1, source_target_pairs={{0,6},{1,7},{2,4},{3,5},{4,2},{5,3},{6,0},{7,1},{8,14},{9,15},{10,... | collective-permute-start | bytes 49160 | tf_op jit(solution)/shard_map/ppermute | solution.py:292

commit v7 on v6

--- a/solution.py
+++ b/solution.py
@@ -22,13 +22,12 @@
 SMEM = pl.BlockSpec(memory_space=pltpu.SMEM)
 
 
-def call(body, out_shape, in_specs, flops, moved, room=6, aliases=None):
+def call(body, out_shape, in_specs, flops, moved, room=6):
     return pl.pallas_call(
         body,
         out_shape=out_shape,
         in_specs=in_specs,
         out_specs=jax.tree.map(lambda _: VMEM, out_shape),
-        input_output_aliases=aliases or {},
         cost_estimate=pl.CostEstimate(flops=flops, bytes_accessed=moved, transcendentals=0),
         compiler_params=pltpu.CompilerParams(vmem_limit_bytes=room << 20),
     )
@@ -47,13 +46,13 @@
 STEPS = 8
 
 
-def unit_rows_body(block, points_ref, out_ref, held, arrived):
+def unit_rows_body(first, points_ref, out_ref, held, arrived):
     size = out_ref.shape[0]
     step = size // STEPS
     copies = []
     for at in range(STEPS):
         rows = pl.ds(at * step, step)
-        source = points_ref.at[pl.ds(block * size + at * step, step)]
+        source = points_ref.at[pl.ds(first + at * step, step)]
         copies.append(pltpu.make_async_copy(source, held.at[rows], arrived.at[at]))
         copies[-1].start()
     for at in range(STEPS):
@@ -64,10 +63,10 @@
         out_ref[rows, :] = (points * lax.rsqrt(mean + EPSILON)).astype(BF16)
 
 
-def unit_rows(points, block, size):
+def unit_rows(points, first, size):
     width = points.shape[1]
     return pl.pallas_call(
-        functools.partial(unit_rows_body, block),
+        functools.partial(unit_rows_body, first),
         in_specs=[pl.BlockSpec(memory_space=pltpu.HBM)],
         out_specs=VMEM,
         out_shape=shaped((size, width), BF16),
@@ -105,58 +104,76 @@
     return slice(index * size, (index + 1) * size)
 
 
-def x_own(own_mask, l, x, owns, near, first, degree):
-    size = x.shape[0]
-    for m, cols in enumerate(owns):
-        tile = affinity(x[...], cols[...])
-        near[span(l - first, size), span(m, size)] = tile.astype(BF16)
-        degree[:, span(m, size)] += gated(own_mask[m, l], down(tile))
-
-
-def own_z(own_mask, owns, m, z, far, degree):
-    size = z.shape[0]
-    sums = []
-    for l, rows in enumerate(owns):
-        tile = affinity(rows[...], z[...])
-        far[span(l, size), :] = tile.astype(BF16)
-        degree[:, span(l, size)] += gated(own_mask[l, 2 * BLK_DEV + m], across(tile))
-        sums.append(down(tile))
-    return sums
-
-
-def x_z(x, z, far, at):
-    tile = affinity(x[...], z[...])
-    far[span(at, z.shape[0]), :] = tile.astype(BF16)
-    return down(tile)
-
-
-def first_tiles_body(own_mask, b0, b1, x0, z0, near, far, degree, far_sums):
+def pieces(part, block, start, size):
+    found = []
+    at = 0
+    while at < part.shape[0]:
+        inside = (start + at) % size
+        count = min(size - inside, part.shape[0] - at)
+        index = block + (start + at) // size
+        found.append((part[at : at + count, :], index, slice(start + at, start + at + count)))
+        at += count
+    return found
+
+
+def shifted(where, by):
+    return slice(where.start + by, where.stop + by)
+
+
+def near_tiles(own_mask, rows, cols, near, base, degree):
+    for left, l, down_at in rows:
+        for right, m, at in cols:
+            tile = affinity(left, right)
+            near[shifted(down_at, base), at] = tile.astype(BF16)
+            degree[:, at] += gated(own_mask[m, l], down(tile))
+
+
+def far_tiles(own_mask, rows, cols, far, by, degree, sums):
+    for left, l, down_at in rows:
+        for right, m, at in cols:
+            tile = affinity(left, right)
+            far[shifted(down_at, by[0]), shifted(at, by[1])] = tile.astype(BF16)
+            sums[l : l + 1, shifted(at, by[1])] += down(tile)
+            if l < BLK_DEV:
+                degree[:, down_at] += gated(own_mask[l, 2 * BLK_DEV + m], across(tile))
+
+
+def first_tiles_body(own_mask, pa, pb, xa, za, near, far, degree, sums):
+    most, points = pa.shape[0], near.shape[1]
+    size = points // BLK_DEV
     degree[...] = jnp.zeros_like(degree)
-    for l, rows in enumerate((b0, b1, x0)):
-        x_own(own_mask, l, rows, (b0, b1), near, 0, degree)
-    sums = own_z(own_mask, (b0, b1), 0, z0, far, degree)
-    sums.append(x_z(x0, z0, far, BLK_DEV))
-    for l, line in enumerate(sums):
-        far_sums[l : l + 1, :] = line
+    sums[...] = jnp.zeros_like(sums)
+    own = pieces(pa, 0, 0, size) + pieces(pb, 0, most, size)
+    side = pieces(xa, BLK_DEV, 0, size)
+    away = pieces(za, 0, 0, size)
+    near_tiles(own_mask, own, own, near, 0, degree)
+    near_tiles(own_mask, side, own, near, points, degree)
+    far_tiles(own_mask, own, away, far, (0, 0), degree, sums)
+    far_tiles(own_mask, side, away, far, (points, 0), degree, sums)
 
 
 def last_tiles_body(
-    own_mask, far_mask, b0, b1, x0, x1, z0, z1, degree_in, far_sums,
-    near, corner, far, degree, far_degree,
+    own_mask, far_mask, pa, pb, xa, xb, za, zb, degree_in, sums_in,
+    near, corner, far, degree, far_degree, sums, late,
 ):
-    size = z0.shape[0]
+    most, points = pa.shape[0], near.shape[1]
+    size = points // BLK_DEV
     degree[...] = degree_in[...]
-    x_own(own_mask, BLK_DEV + 1, x1, (b0, b1), near, BLK_DEV + 1, degree)
-    early = [far_sums[l : l + 1, :] for l in range(far_sums.shape[0])]
-    early.append(x_z(x1, z0, corner, 0))
-    late = own_z(own_mask, (b0, b1), 1, z1, far, degree)
-    late.append(x_z(x0, z1, far, BLK_DEV))
-    late.append(x_z(x1, z1, far, BLK_DEV + 1))
-    for m, sums in enumerate((early, late)):
-        total = jnp.zeros((1, size), F32)
-        for l, line in enumerate(sums):
-            total += gated(far_mask[m, l], line)
-        far_degree[:, span(m, size)] = total
+    sums[...] = sums_in[...]
+    late[...] = jnp.zeros_like(late)
+    own = pieces(pa, 0, 0, size) + pieces(pb, 0, most, size)
+    side, rest = pieces(xa, BLK_DEV, 0, size), pieces(xb, BLK_DEV, most, size)
+    away, final = pieces(za, 0, 0, size), pieces(zb, 0, most, size)
+    near_tiles(own_mask, rest, own, near, -most, degree)
+    far_tiles(own_mask, rest, away, corner, (-most, 0), degree, sums)
+    far_tiles(own_mask, own, final, far, (0, -most), degree, late)
+    far_tiles(own_mask, side + rest, final, far, (points, -most), degree, late)
+    for cols, source, by in ((away, sums, 0), (final, late, -most)):
+        for _, m, at in cols:
+            total = jnp.zeros((1, at.stop - at.start), F32)
+            for l in range(2 * BLK_DEV):
+                total += gated(far_mask[m, l], source[l : l + 1, shifted(at, by)])
+            far_degree[:, at] = total
 
 
 def bfloat_rows(value):
@@ -193,25 +210,27 @@
 
 def far_rows_body(mask, own_ref, x_ref, far0, corner, far1, out):
     own, x = bfloat_rows(own_ref[...]), bfloat_rows(x_ref[...])
-    size = own.shape[1] // BLK_DEV
-    count = out.shape[0]
-    cut = far0.shape[0]
-    left = kept(mask, 0, 0, own, x)
-    first = apart(left[:, :cut], far0[...]) + apart(left[:, cut:], corner[...])
-    out[:, span(0, size)] = whole_rows(first, count)
-    out[:, span(1, size)] = whole_rows(apart(kept(mask, 1, 0, own, x), far1[...]), count)
+    count, points = out.shape
+    size = points // BLK_DEV
+    cut, most = far0.shape
+    for m in range(BLK_DEV):
+        left = kept(mask, m, 0, own, x)
+        there = slice(m * size, min((m + 1) * size, most))
+        total = apart(left[:, :cut], far0[:, there]) + apart(left[:, cut:], corner[:, there])
+        out[:, there] = whole_rows(total, count)
+    out[:, most:] = whole_rows(apart(left, far1[...]), count)
 
 
 def near_rows_body(mask, own_ref, x_ref, z_ref, near0, near1, far0, far1, out):
     own, x, z = bfloat_rows(own_ref[...]), bfloat_rows(x_ref[...]), bfloat_rows(z_ref[...])
     size = own.shape[1] // BLK_DEV
-    cut = near0.shape[0]
+    cut, most = far0.shape
     for m in range(BLK_DEV):
         there = span(m, size)
         left = kept(mask, m, 0, own, x)
         side = kept(mask, m, 2 * BLK_DEV, z)
         total = apart(left[:, :cut], near0[:, there]) + apart(left[:, cut:], near1[:, there])
-        total += cross(side[:, :size], far0[there, :]) + cross(side[:, size:], far1[there, :])
+        total += cross(side[:, :most], far0[there, :]) + cross(side[:, most:], far1[there, :])
         out[:, there] = whole_rows(total, out.shape[0])
 
 
@@ -332,10 +351,11 @@
     def to_z_side(value):
         return lax.ppermute(value, "col", [(i, side_of(i) ^ 1) for i in range(col_count)])
 
-    b0 = unit_rows(embeddings, 0, size)
+    most = points - size // 2
+    b0 = unit_rows(embeddings, 0, most)
     z0 = from_z(b0)
     x0 = from_x(b0)
-    b1 = unit_rows(embeddings, 1, size)
+    b1 = unit_rows(embeddings, most, points - most)
     z1 = from_z(b1)
     x1 = from_x(b1)
     far_ids = from_z(neighbour_ids)
@@ -355,23 +375,24 @@
     line = shaped((1, points), F32)
     one = 2 * size * size * width
     moved = 4 * size * width
-    most = 2 * BLK_DEV - 1
-    near0, far0, degree, far_sums = call(
+    tall, less = points + most, points - most
+    near0, far0, degree, sums = call(
         first_tiles_body,
         (
-            shaped((most * size, points), BF16), shaped((most * size, size), BF16), line,
-            shaped((most, size), F32),
+            shaped((tall, points), BF16), shaped((tall, most), BF16), line,
+            shaped((2 * BLK_DEV, most), F32),
         ),
-        [SMEM] + [VMEM] * 4, 9 * one, 9 * moved,
+        [SMEM] + [VMEM] * 4, 12 * one, 12 * moved, room=14,
     )(own_mask, b0, b1, x0, z0)
-    near1, corner, far1, degree, far_degree = call(
+    near1, corner, far1, degree, far_degree, _, _ = call(
         last_tiles_body,
         (
-            shaped((size, points), BF16), shaped((size, size), BF16),
-            shaped((2 * points, size), BF16), line, line,
+            shaped((less, points), BF16), shaped((less, most), BF16),
+            shaped((2 * points, less), BF16), line, line,
+            shaped((2 * BLK_DEV, most), F32), shaped((2 * BLK_DEV, less), F32),
         ),
-        [SMEM] * 2 + [VMEM] * 8, 7 * one, 7 * moved,
-    )(own_mask, far_mask, b0, b1, x0, x1, z0, z1, degree, far_sums)
+        [SMEM] * 2 + [VMEM] * 8, 4 * one, 4 * moved, room=14,
+    )(own_mask, far_mask, b0, b1, x0, x1, z0, z1, degree, sums)
     root = lax.rsqrt(degree + to_z(far_degree))
     root_x = lax.rsqrt(from_x(degree) + to_z_side(far_degree))
     root_z = lax.rsqrt(from_z(degree) + far_degree)

time: 160 us -> 160 us (level)
  transfers between devices with their start and end apart: 39 -> 39, of which waited for: 19 -> 19; matrix products, arithmetic and copies ran while one was open for 1% -> 1% of each run, Pallas kernels for 12% -> 13%
where the time goes in v7:
time: 160 us
  waiting for transfers between devices  73.2 us (46%)
  starting transfers between devices  47.5 us (30%)
  Pallas kernels  37.7 us (24%)
    ppermute x7, waiting for transfers between devices, from_z(): lax.ppermute(value, 'col', [(side_of(i), i) for i in range(col_count)])  39.5 us
    ppermute x21, starting transfers between devices, fetched(): return lax.ppermute(value, ('row', 'col'), pairs)  23.6 us
    ppermute x21, waiting for transfers between devices, fetched(): return lax.ppermute(value, ('row', 'col'), pairs)  20.3 us
    ppermute x7, starting transfers between devices, from_z(): lax.ppermute(value, 'col', [(side_of(i), i) for i in range(col_count)])  13.9 us
    ppermute x4, waiting for transfers between devices, to_z(): lax.ppermute(value, 'col', [(i, side_of(i)) for i in range(col_count)])  11.3 us
    pallas_call x1, Pallas kernels, on_device(): call(first_tiles_body, (shaped((tall, points), BF16), shaped((tall, most)...  8.84 us
    ppermute x6, starting transfers between devices, from_x(): return lax.ppermute(value, 'col', [(i, i ^ 1) for i in range(col_count)])  6.58 us
    pallas_call x3, Pallas kernels, on_device(): held = near_rows(own_mask, own, x, z, near0, near1, far0, far1)  6.49 us
  transfers between devices with their start and end apart: 39, of which 19 were waited for; matrix products, arithmetic and copies ran while one was open for 1% of the time, Pallas kernels for 13%

profile of v7, /device:TPU:0, one launch (start us, length us, event | category | flops | bytes accessed | tf_op | source)
XLA Modules:
  0.0 160.2 jit_solution(6041177052041576849)
XLA Ops:
  0.0 2.0 %unit_rows.2.pa = bf16[768,1024]{1,0:T(8,128)(2,1)S(1)} custom-call(f32[1024,1024]{1,0:T(8,128)} %points_ref.3), custom_call_target="tpu_custom_call" | custom-call | flops 2359296 | bytes 4718592 | tf_op jit(solution)/shard_map/unit_rows/pallas_call | solution.py:68
  2.0 3.0 %collective-permute-start.1 = (bf16[768,1024]{1,0:T(8,128)(2,1)S(1)}, bf16[768,1024]{1,0:T(8,128)(2,1)}, u32[]{:S(2)}, u32[]{:S(2)}) collective-permute-start(bf16[768,1024]{1,0:T(8,128)(2,1)S(1)} %unit_rows.2.pa), channel_id=1, source_target_pairs={{0,1},{1,0},{2,3},{3,2},{4,5},{5,4},{6,7},{7,6},{8,9},{9,8},{10,11... | collective-permute-start | bytes 4718600 | tf_op jit(solution)/shard_map/ppermute | solution.py:343
  5.1 3.6 %collective-permute-start.3 = (bf16[768,1024]{1,0:T(8,128)(2,1)S(1)}, bf16[768,1024]{1,0:T(8,128)(2,1)}, u32[]{:S(2)}, u32[]{:S(2)}) collective-permute-start(bf16[768,1024]{1,0:T(8,128)(2,1)S(1)} %unit_rows.2.pa), channel_id=1, source_target_pairs={{2,0},{7,1},{4,2},{1,3},{6,4},{3,5},{0,6},{5,7},{10,8},{15,9},{12,... | collective-permute-start | bytes 4718600 | tf_op jit(solution)/shard_map/ppermute | solution.py:346
  8.7 1.8 %unit_rows.3.pb = bf16[256,1024]{1,0:T(8,128)(2,1)S(1)} custom-call(f32[1024,1024]{1,0:T(8,128)} %points_ref.3), custom_call_target="tpu_custom_call" | custom-call | flops 786432 | bytes 1572864 | tf_op jit(solution)/shard_map/unit_rows/pallas_call | solution.py:68
  11.1 2.0 %collective-permute-start = (s32[2,12]{1,0:T(2,128)S(1)}, s32[2,12]{1,0:T(2,128)S(1)}, u32[]{:S(2)}, u32[]{:S(2)}) collective-permute-start(s32[2,12]{1,0:T(2,128)S(1)} %copy-done.1), channel_id=1, source_target_pairs={{2,0},{7,1},{4,2},{1,3},{6,4},{3,5},{0,6},{5,7},{10,8},{15,9},{12,... | collective-permute-start | bytes 296 | tf_op jit(solution)/shard_map/ppermute | solution.py:346
  13.9 39.5 %collective-permute-done = s32[2,12]{1,0:T(2,128)S(1)} collective-permute-done((s32[2,12]{1,0:T(2,128)S(1)}, s32[2,12]{1,0:T(2,128)S(1)}, u32[]{:S(2)}, u32[]{:S(2)}) %collective-permute-start) | collective-permute-done | bytes 128 | tf_op jit(solution)/shard_map/ppermute | solution.py:346
  53.8 8.8 %shard_map.37 = (bf16[1792,1024]{1,0:T(8,128)(2,1)S(1)}, bf16[1792,768]{1,0:T(8,128)(2,1)S(1)}, f32[1,1024]{1,0:T(1,128)S(1)}, f32[4,768]{1,0:T(4,128)S(1)}) custom-call(f32[2,6]{1,0:T(2,128)S(1)} %or_convert_fusion.1.own_mask.mask, bf16[768,1024]{1,0:T(8,128)(2,1)S(1)} %unit_rows.2.pa, bf16[256,1024]{1,0:T(8,128)(2,1)S(1)} %unit_rows.3.pb, ...), custom_call_target="tpu_custom_call" | custom-call | flops 6442450944 | bytes 25165824 | tf_op jit(solution)/shard_map/pallas_call | solution.py:379
  62.7 5.0 %shard_map.38 = (bf16[256,1024]{1,0:T(8,128)(2,1)S(1)}, bf16[256,768]{1,0:T(8,128)(2,1)S(1)}, bf16[2048,256]{1,0:T(8,128)(2,1)S(1)}, f32[1,1024]{1,0:T(1,128)S(1...) custom-call(f32[2,6]{1,0:T(2,128)S(1)} %or_convert_fusion.1.own_mask.mask, ...), custom_call_target="tpu_custom_call" | custom-call | flops 2147483648 | bytes 8388608 | tf_op jit(solution)/shard_map/pallas_call | solution.py:387
  68.2 2.6 %collective-permute-start.6 = (f32[64,1024]{1,0:T(8,128)S(1)}, f32[64,1024]{1,0:T(8,128)S(1)}, u32[]{:S(2)}, u32[]{:S(2)}) collective-permute-start(f32[64,1024]{1,0:T(8,128)S(1)} %bitcast.10), channel_id=1, source_target_pairs={{0,1},{1,0},{2,3},{3,2},{4,5},{5,4},{6,7},{7,6},{8,9},{9,8},{10,11... | collective-permute-start | bytes 786440 | tf_op jit(solution)/shard_map/ppermute | solution.py:343
  70.7 1.4 collective-permute-start.9
  72.1 2.5 %collective-permute-start.8 = (f32[1,1024]{1,0:T(1,128)S(1)}, f32[1,1024]{1,0:T(1,128)S(1)}, u32[]{:S(2)}, u32[]{:S(2)}) collective-permute-start(f32[1,1024]{1,0:T(1,128)S(1)} %get-tuple-element.23), channel_id=1, source_target_pairs={{0,3},{1,6},{2,5},{3,0},{4,7},{5,2},{6,1},{7,4},{8,11},{9,14},{10,... | collective-permute-start | bytes 12296 | tf_op jit(solution)/shard_map/ppermute | solution.py:352
  74.6 0.9 collective-permute-start.7
  76.0 2.2 %collective-permute-done.7 = f32[1,1024]{1,0:T(1,128)S(1)} collective-permute-done((f32[1,1024]{1,0:T(1,128)S(1)}, f32[1,1024]{1,0:T(1,128)S(1)}, u32[]{:S(2)}, u32[]{:S(2)}) %collective-permute-start.7) | collective-permute-done | bytes 4128 | tf_op jit(solution)/shard_map/ppermute | solution.py:343
  78.3 1.4 shard_map.40
  80.0 2.0 %shard_map.39.near = f32[64,1024]{1,0:T(8,128)S(1)} custom-call(f32[2,6]{1,0:T(2,128)S(1)} %or_convert_fusion.1.own_mask.mask, bf16[64,1024]{1,0:T(8,128)(2,1)S(1)} %multiply_convert_fusion.2.own_ref, bf16[64,1024]{1,0:T(8,128)(2,1)S(1)} %multiply_convert_fusion.1.x_ref, bf16[64,1024]{1,0:T(8,128)(2,1)S(1)} %multiply_convert_fusion.z_ref, ...), custom_call_target="tpu_custom_call" | custom-call | flops 402653184 | bytes 6291456 | tf_op jit(solution)/shard_map/pallas_call | solution.py:422
  82.1 6.3 %collective-permute-done.11.given = f32[64,1024]{1,0:T(8,128)S(1)} collective-permute-done((f32[64,1024]{1,0:T(8,128)S(1)}, f32[64,1024]{1,0:T(8,128)S(1)}, u32[]{:S(2)}, u32[]{:S(2)}) %collective-permute-start.11) | collective-permute-done | bytes 262176 | tf_op jit(solution)/shard_map/ppermute | solution.py:349
  88.3 0.8 shard_map.41
  89.5 2.3 %collective-permute-start.13 = (f32[64,64]{1,0:T(8,128)S(1)}, f32[64,64]{1,0:T(8,128)S(1)}, u32[]{:S(2)}, u32[]{:S(2)}) collective-permute-start(f32[64,64]{1,0:T(8,128)S(1)} %get-tuple-element.29), channel_id=1, source_target_pairs={{0,4},{1,5},{2,6},{3,7},{4,0},{5,1},{6,2},{7,3},{8,12},{9,13},{10,... | collective-permute-start | bytes 49160 | tf_op jit(solution)/shard_map/ppermute | solution.py:311
  91.8 1.7 %collective-permute-start.14 = (f32[64,64]{1,0:T(8,128)S(1)}, f32[64,64]{1,0:T(8,128)S(1)}, u32[]{:S(2)}, u32[]{:S(2)}) collective-permute-start(f32[64,64]{1,0:T(8,128)S(1)} %get-tuple-element.29), channel_id=1, source_target_pairs={{0,6},{1,7},{2,4},{3,5},{4,2},{5,3},{6,0},{7,1},{8,14},{9,15},{10,... | collective-permute-start | bytes 49160 | tf_op jit(solution)/shard_map/ppermute | solution.py:311
  93.5 2.1 %collective-permute-start.20 = (f32[64,1024]{1,0:T(8,128)S(1)}, f32[64,1024]{1,0:T(8,128)S(1)}, u32[]{:S(2)}, u32[]{:S(2)}) collective-permute-start(f32[64,1024]{1,0:T(8,128)S(1)} %get-tuple-element.30.own_ref), channel_id=1, source_target_pairs={{2,0},{7,1},{4,2},{1,3},{6,4},{3,5},{0,6},{5,7},{10,8},{15,9},{12,... | collective-permute-start | bytes 786440 | tf_op jit(solution)/shard_map/ppermute | solution.py:346
  95.6 2.0 %collective-permute-done.14 = f32[64,64]{1,0:T(8,128)S(1)} collective-permute-done((f32[64,64]{1,0:T(8,128)S(1)}, f32[64,64]{1,0:T(8,128)S(1)}, u32[]{:S(2)}, u32[]{:S(2)}) %collective-permute-start.14) | collective-permute-done | bytes 16416 | tf_op jit(solution)/shard_map/ppermute | solution.py:311
  97.7 1.6 collective-permute-start.16
  99.6 1.5 shard_map.43
  101.7 0.9 collective-permute-done.17
  102.6 2.4 %collective-permute-start.18 = (f32[64,64]{1,0:T(8,128)S(1)}, f32[64,64]{1,0:T(8,128)S(1)}, u32[]{:S(2)}, u32[]{:S(2)}) collective-permute-start(f32[64,64]{1,0:T(8,128)S(1)} %add_add_fusion.4), channel_id=1, source_target_pairs={{0,1},{1,0},{2,3},{3,2},{4,5},{5,4},{6,7},{7,6},{8,9},{9,8},{10,11... | collective-permute-start | bytes 49160 | tf_op jit(solution)/shard_map/ppermute | solution.py:311
  105.0 1.9 %collective-permute-done.18 = f32[64,64]{1,0:T(8,128)S(1)} collective-permute-done((f32[64,64]{1,0:T(8,128)S(1)}, f32[64,64]{1,0:T(8,128)S(1)}, u32[]{:S(2)}, u32[]{:S(2)}) %collective-permute-start.18) | collective-permute-done | bytes 16416 | tf_op jit(solution)/shard_map/ppermute | solution.py:311
  106.9 2.2 %shard_map.42.near = f32[64,1024]{1,0:T(8,128)S(1)} custom-call(f32[2,6]{1,0:T(2,128)S(1)} %or_convert_fusion.1.own_mask.mask, f32[64,1024]{1,0:T(8,128)S(1)} %get-tuple-element.30.own_ref, f32[64,1024]{1,0:T(8,128)S(1)} %collective-permute-done.19.x_ref, f32[64,1024]{1,0:T(8,128)S(1)} %collective-permute-done.20.z_ref, ...), custom_call_target="tpu_custom_call" | custom-call | flops 402653184 | bytes 6291456 | tf_op jit(solution)/shard_map/pallas_call | solution.py:422
  109.2 2.4 %collective-permute-done.21.given = f32[64,1024]{1,0:T(8,128)S(1)} collective-permute-done((f32[64,1024]{1,0:T(8,128)S(1)}, f32[64,1024]{1,0:T(8,128)S(1)}, u32[]{:S(2)}, u32[]{:S(2)}) %collective-permute-start.21) | collective-permute-done | bytes 262176 | tf_op jit(solution)/shard_map/ppermute | solution.py:349
  111.5 2.8 %shard_map.44 = (f32[64,1024]{1,0:T(8,128)}, f32[64,1024]{1,0:T(8,128)S(1)}, f32[64,64]{1,0:T(8,128)S(1)}) custom-call(f32[64,64]{1,0:T(8,128)S(1)} %add.130.total, f32[64,1024]{1,0:T(8,128)S(1)} %shard_map.42.near, f32[64,1024]{1,0:T(8,128)S(1)} %collective-permute-done.21.given, f32[1,1024]{1,0:T(1,128)S(1)} %add_rsqrt_fusion.2.root), custom_call_target="tpu_custom_call" | custom-call | flops 8388608 | bytes 262144 | tf_op jit(solution)/shard_map/pallas_call | solution.py:426
  114.4 4.3 %collective-permute-start.23 = (f32[64,64]{1,0:T(8,128)S(1)}, f32[64,64]{1,0:T(8,128)S(1)}, u32[]{:S(2)}, u32[]{:S(2)}) collective-permute-start(f32[64,64]{1,0:T(8,128)S(1)} %get-tuple-element.31), channel_id=1, source_target_pairs={{0,4},{1,5},{2,6},{3,7},{4,0},{5,1},{6,2},{7,3},{8,12},{9,13},{10,... | collective-permute-start | bytes 49160 | tf_op jit(solution)/shard_map/ppermute | solution.py:311
  118.8 3.8 %collective-permute-start.30 = (f32[64,1024]{1,0:T(8,128)S(1)}, f32[64,1024]{1,0:T(8,128)S(1)}, u32[]{:S(2)}, u32[]{:S(2)}) collective-permute-start(f32[64,1024]{1,0:T(8,128)S(1)} %get-tuple-element.32.own_ref), channel_id=1, source_target_pairs={{2,0},{7,1},{4,2},{1,3},{6,4},{3,5},{0,6},{5,7},{10,8},{15,9},{12,... | collective-permute-start | bytes 786440 | tf_op jit(solution)/shard_map/ppermute | solution.py:346
  122.5 2.2 %collective-permute-done.24 = f32[64,64]{1,0:T(8,128)S(1)} collective-permute-done((f32[64,64]{1,0:T(8,128)S(1)}, f32[64,64]{1,0:T(8,128)S(1)}, u32[]{:S(2)}, u32[]{:S(2)}) %collective-permute-start.24) | collective-permute-done | bytes 16416 | tf_op jit(solution)/shard_map/ppermute | solution.py:311
  124.8 1.6 collective-permute-start.26
  126.7 1.5 shard_map.46
  128.8 0.9 collective-permute-done.27
  130.5 3.3 %collective-permute-done.28 = f32[64,64]{1,0:T(8,128)S(1)} collective-permute-done((f32[64,64]{1,0:T(8,128)S(1)}, f32[64,64]{1,0:T(8,128)S(1)}, u32[]{:S(2)}, u32[]{:S(2)}) %collective-permute-start.28) | collective-permute-done | bytes 16416 | tf_op jit(solution)/shard_map/ppermute | solution.py:311
  133.8 2.2 %shard_map.45.near = f32[64,1024]{1,0:T(8,128)S(1)} custom-call(f32[2,6]{1,0:T(2,128)S(1)} %or_convert_fusion.1.own_mask.mask, f32[64,1024]{1,0:T(8,128)S(1)} %get-tuple-element.32.own_ref, f32[64,1024]{1,0:T(8,128)S(1)} %collective-permute-done.29.x_ref, f32[64,1024]{1,0:T(8,128)S(1)} %collective-permute-done.30.z_ref, ...), custom_call_target="tpu_custom_call" | custom-call | flops 402653184 | bytes 6291456 | tf_op jit(solution)/shard_map/pallas_call | solution.py:422
  136.0 2.7 %collective-permute-done.31.given = f32[64,1024]{1,0:T(8,128)S(1)} collective-permute-done((f32[64,1024]{1,0:T(8,128)S(1)}, f32[64,1024]{1,0:T(8,128)S(1)}, u32[]{:S(2)}, u32[]{:S(2)}) %collective-permute-start.31) | collective-permute-done | bytes 262176 | tf_op jit(solution)/shard_map/ppermute | solution.py:349
  138.7 2.8 %shard_map.47 = (f32[64,1024]{1,0:T(8,128)S(1)}, f32[64,1024]{1,0:T(8,128)}, f32[64,64]{1,0:T(8,128)S(1)}) custom-call(f32[64,64]{1,0:T(8,128)S(1)} %add.137.total, f32[64,1024]{1,0:T(8,128)S(1)} %shard_map.45.near, f32[64,1024]{1,0:T(8,128)S(1)} %collective-permute-done.31.given, f32[1,1024]{1,0:T(1,128)S(1)} %add_rsqrt_fusion.2.root), custom_call_target="tpu_custom_call" | custom-call | flops 8388608 | bytes 262144 | tf_op jit(solution)/shard_map/pallas_call | solution.py:426
  141.5 1.2 collective-permute-done.32
  142.7 1.5 collective-permute-start.33
  144.2 2.0 %collective-permute-start.35 = (f32[64,64]{1,0:T(8,128)S(1)}, f32[64,64]{1,0:T(8,128)S(1)}, u32[]{:S(2)}, u32[]{:S(2)}) collective-permute-start(f32[64,64]{1,0:T(8,128)S(1)} %add.138), channel_id=1, source_target_pairs={{0,17},{1,16},{2,19},{3,18},{4,21},{5,20},{6,23},{7,22},{8,25},{9,... | collective-permute-start | bytes 49160 | tf_op jit(solution)/shard_map/ppermute | solution.py:311
  146.6 1.5 collective-permute-done.34
  148.1 0.9 collective-permute-done.35
  149.1 2.7 %collective-permute-start.37 = (f32[64,64]{1,0:T(8,128)S(1)}, f32[64,64]{1,0:T(8,128)S(1)}, u32[]{:S(2)}, u32[]{:S(2)}) collective-permute-start(f32[64,64]{1,0:T(8,128)S(1)} %add_add_fusion.1), channel_id=1, source_target_pairs={{0,4},{1,5},{2,6},{3,7},{4,0},{5,1},{6,2},{7,3},{8,12},{9,13},{10,... | collective-permute-start | bytes 49160 | tf_op jit(solution)/shard_map/ppermute | solution.py:311
  151.8 1.7 %collective-permute-start.38 = (f32[64,64]{1,0:T(8,128)S(1)}, f32[64,64]{1,0:T(8,128)S(1)}, u32[]{:S(2)}, u32[]{:S(2)}) collective-permute-start(f32[64,64]{1,0:T(8,128)S(1)} %add_add_fusion.1), channel_id=1, source_target_pairs={{0,6},{1,7},{2,4},{3,5},{4,2},{5,3},{6,0},{7,1},{8,14},{9,15},{10,... | collective-permute-start | bytes 49160 | tf_op jit(solution)/shard_map/ppermute | solution.py:311
  154.0 3.5 %collective-permute-done.38 = f32[64,64]{1,0:T(8,128)S(1)} collective-permute-done((f32[64,64]{1,0:T(8,128)S(1)}, f32[64,64]{1,0:T(8,128)S(1)}, u32[]{:S(2)}, u32[]{:S(2)}) %collective-permute-start.38) | collective-permute-done | bytes 16416 | tf_op jit(solution)/shard_map/ppermute | solution.py:311
  157.5 2.7 %shard_map.48 = f32[64,1024]{1,0:T(8,128)} custom-call(f32[64,64]{1,0:T(8,128)S(1)} %add_add_fusion.total, f32[64,1024]{1,0:T(8,128)S(1)} %get-tuple-element.34.image), custom_call_target="tpu_custom_call" | custom-call | flops 8388608 | bytes 262144 | tf_op jit(solution)/shard_map/pallas_call | solution.py:428
  (72 shorter events, 7.3 us)
Async XLA Ops:
  2.0 9.0 %copy-start.1 = (s32[2,12]{1,0:T(2,128)S(1)}, s32[2,12]{1,0:T(2,128)}, u32[]{:S(2)}) copy-start(s32[2,12]{1,0:T(2,128)} %param.4) | copy-start | bytes 292
  2.0 51.7 %collective-permute-start.1 = (bf16[768,1024]{1,0:T(8,128)(2,1)S(1)}, bf16[768,1024]{1,0:T(8,128)(2,1)}, u32[]{:S(2)}, u32[]{:S(2)}) collective-permute-start(bf16[768,1024]{1,0:T(8,128)(2,1)S(1)} %unit_rows.2.pa), channel_id=1, source_target_pairs={{0,1},{1,0},{2,3},{3,2},{4,5},{5,4},{6,7},{7,6},{8,9},{9,8},{10,11... | collective-permute-start | bytes 4718600 | tf_op jit(solution)/shard_map/ppermute | solution.py:343
  5.1 48.7 %collective-permute-start.3 = (bf16[768,1024]{1,0:T(8,128)(2,1)S(1)}, bf16[768,1024]{1,0:T(8,128)(2,1)}, u32[]{:S(2)}, u32[]{:S(2)}) collective-permute-start(bf16[768,1024]{1,0:T(8,128)(2,1)S(1)} %unit_rows.2.pa), channel_id=1, source_target_pairs={{2,0},{7,1},{4,2},{1,3},{6,4},{3,5},{0,6},{5,7},{10,8},{15,9},{12,... | collective-permute-start | bytes 4718600 | tf_op jit(solution)/shard_map/ppermute | solution.py:346
  10.5 52.2 %collective-permute-start.2 = (bf16[256,1024]{1,0:T(8,128)(2,1)S(1)}, bf16[256,1024]{1,0:T(8,128)(2,1)S(1)}, u32[]{:S(2)}, u32[]{:S(2)}) collective-permute-start(bf16[256,1024]{1,0:T(8,128)(2,1)S(1)} %unit_rows.3.pb), channel_id=1, source_target_pairs={{0,1},{1,0},{2,3},{3,2},{4,5},{5,4},{6,7},{7,6},{8,9},{9,8},{10,11... | collective-permute-start | bytes 1572872 | tf_op jit(solution)/shard_map/ppermute | solution.py:343
  10.5 52.1 %collective-permute-start.4 = (bf16[256,1024]{1,0:T(8,128)(2,1)S(1)}, bf16[256,1024]{1,0:T(8,128)(2,1)S(1)}, u32[]{:S(2)}, u32[]{:S(2)}) collective-permute-start(bf16[256,1024]{1,0:T(8,128)(2,1)S(1)} %unit_rows.3.pb), channel_id=1, source_target_pairs={{2,0},{7,1},{4,2},{1,3},{6,4},{3,5},{0,6},{5,7},{10,8},{15,9},{12,... | collective-permute-start | bytes 1572872 | tf_op jit(solution)/shard_map/ppermute | solution.py:346
  11.1 42.3 %collective-permute-start = (s32[2,12]{1,0:T(2,128)S(1)}, s32[2,12]{1,0:T(2,128)S(1)}, u32[]{:S(2)}, u32[]{:S(2)}) collective-permute-start(s32[2,12]{1,0:T(2,128)S(1)} %copy-done.1), channel_id=1, source_target_pairs={{2,0},{7,1},{4,2},{1,3},{6,4},{3,5},{0,6},{5,7},{10,8},{15,9},{12,... | collective-permute-start | bytes 296 | tf_op jit(solution)/shard_map/ppermute | solution.py:346
  62.7 5.5 %copy-start = (f32[1024,64]{0,1:T(8,128)S(1)}, f32[1024,64]{0,1:T(8,128)}, u32[]{:S(2)}) copy-start(f32[1024,64]{0,1:T(8,128)} %param.5) | copy-start | bytes 786436
  67.7 7.8 %collective-permute-start.5 = (f32[1,1024]{1,0:T(1,128)S(1)}, f32[1,1024]{1,0:T(1,128)S(1)}, u32[]{:S(2)}, u32[]{:S(2)}) collective-permute-start(f32[1,1024]{1,0:T(1,128)S(1)} %get-tuple-element.23), channel_id=1, source_target_pairs={{0,2},{1,7},{2,4},{3,1},{4,6},{5,3},{6,0},{7,5},{8,10},{9,15},{10,... | collective-permute-start | bytes 12296 | tf_op jit(solution)/shard_map/ppermute | solution.py:349
  68.2 10.1 %collective-permute-start.6 = (f32[64,1024]{1,0:T(8,128)S(1)}, f32[64,1024]{1,0:T(8,128)S(1)}, u32[]{:S(2)}, u32[]{:S(2)}) collective-permute-start(f32[64,1024]{1,0:T(8,128)S(1)} %bitcast.10), channel_id=1, source_target_pairs={{0,1},{1,0},{2,3},{3,2},{4,5},{5,4},{6,7},{7,6},{8,9},{9,8},{10,11... | collective-permute-start | bytes 786440 | tf_op jit(solution)/shard_map/ppermute | solution.py:343
  70.7 9.3 %collective-permute-start.9 = (f32[64,1024]{1,0:T(8,128)S(1)}, f32[64,1024]{1,0:T(8,128)S(1)}, u32[]{:S(2)}, u32[]{:S(2)}) collective-permute-start(f32[64,1024]{1,0:T(8,128)S(1)} %bitcast.11), channel_id=1, source_target_pairs={{2,0},{7,1},{4,2},{1,3},{6,4},{3,5},{0,6},{5,7},{10,8},{15,9},{12,... | collective-permute-start | bytes 786440 | tf_op jit(solution)/shard_map/ppermute | solution.py:346
  72.1 6.1 %collective-permute-start.8 = (f32[1,1024]{1,0:T(1,128)S(1)}, f32[1,1024]{1,0:T(1,128)S(1)}, u32[]{:S(2)}, u32[]{:S(2)}) collective-permute-start(f32[1,1024]{1,0:T(1,128)S(1)} %get-tuple-element.23), channel_id=1, source_target_pairs={{0,3},{1,6},{2,5},{3,0},{4,7},{5,2},{6,1},{7,4},{8,11},{9,14},{10,... | collective-permute-start | bytes 12296 | tf_op jit(solution)/shard_map/ppermute | solution.py:352
  74.6 3.6 %collective-permute-start.7 = (f32[1,1024]{1,0:T(1,128)S(1)}, f32[1,1024]{1,0:T(1,128)S(1)}, u32[]{:S(2)}, u32[]{:S(2)}) collective-permute-start(f32[1,1024]{1,0:T(1,128)S(1)} %get-tuple-element.22), channel_id=1, source_target_pairs={{0,1},{1,0},{2,3},{3,2},{4,5},{5,4},{6,7},{7,6},{8,9},{9,8},{10,11... | collective-permute-start | bytes 12296 | tf_op jit(solution)/shard_map/ppermute | solution.py:343
  75.5 4.5 %collective-permute-start.10 = (f32[1,1024]{1,0:T(1,128)S(1)}, f32[1,1024]{1,0:T(1,128)S(1)}, u32[]{:S(2)}, u32[]{:S(2)}) collective-permute-start(f32[1,1024]{1,0:T(1,128)S(1)} %get-tuple-element.22), channel_id=1, source_target_pairs={{2,0},{7,1},{4,2},{1,3},{6,4},{3,5},{0,6},{5,7},{10,8},{15,9},{12,... | collective-permute-start | bytes 12296 | tf_op jit(solution)/shard_map/ppermute | solution.py:346
  79.7 8.7 %collective-permute-start.11 = (f32[64,1024]{1,0:T(8,128)S(1)}, f32[64,1024]{1,0:T(8,128)S(1)}, u32[]{:S(2)}, u32[]{:S(2)}) collective-permute-start(f32[64,1024]{1,0:T(8,128)S(1)} %shard_map.40), channel_id=1, source_target_pairs={{0,2},{1,7},{2,4},{3,1},{4,6},{5,3},{6,0},{7,5},{8,10},{9,15},{10,... | collective-permute-start | bytes 786440 | tf_op jit(solution)/shard_map/ppermute | solution.py:349
  89.1 10.4 %collective-permute-start.19 = (f32[64,1024]{1,0:T(8,128)S(1)}, f32[64,1024]{1,0:T(8,128)S(1)}, u32[]{:S(2)}, u32[]{:S(2)}) collective-permute-start(f32[64,1024]{1,0:T(8,128)S(1)} %get-tuple-element.30.own_ref), channel_id=1, source_target_pairs={{0,1},{1,0},{2,3},{3,2},{4,5},{5,4},{6,7},{7,6},{8,9},{9,8},{10,11... | collective-permute-start | bytes 786440 | tf_op jit(solution)/shard_map/ppermute | solution.py:343
  89.1 6.5 %collective-permute-start.12 = (f32[64,64]{1,0:T(8,128)S(1)}, f32[64,64]{1,0:T(8,128)S(1)}, u32[]{:S(2)}, u32[]{:S(2)}) collective-permute-start(f32[64,64]{1,0:T(8,128)S(1)} %get-tuple-element.29), channel_id=1, source_target_pairs={{0,2},{1,3},{2,0},{3,1},{4,6},{5,7},{6,4},{7,5},{8,10},{9,11},{10,... | collective-permute-start | bytes 49160 | tf_op jit(solution)/shard_map/ppermute | solution.py:311
  89.5 6.1 %collective-permute-start.13 = (f32[64,64]{1,0:T(8,128)S(1)}, f32[64,64]{1,0:T(8,128)S(1)}, u32[]{:S(2)}, u32[]{:S(2)}) collective-permute-start(f32[64,64]{1,0:T(8,128)S(1)} %get-tuple-element.29), channel_id=1, source_target_pairs={{0,4},{1,5},{2,6},{3,7},{4,0},{5,1},{6,2},{7,3},{8,12},{9,13},{10,... | collective-permute-start | bytes 49160 | tf_op jit(solution)/shard_map/ppermute | solution.py:311
  91.8 5.8 %collective-permute-start.14 = (f32[64,64]{1,0:T(8,128)S(1)}, f32[64,64]{1,0:T(8,128)S(1)}, u32[]{:S(2)}, u32[]{:S(2)}) collective-permute-start(f32[64,64]{1,0:T(8,128)S(1)} %get-tuple-element.29), channel_id=1, source_target_pairs={{0,6},{1,7},{2,4},{3,5},{4,2},{5,3},{6,0},{7,1},{8,14},{9,15},{10,... | collective-permute-start | bytes 49160 | tf_op jit(solution)/shard_map/ppermute | solution.py:311
  93.5 13.4 %collective-permute-start.20 = (f32[64,1024]{1,0:T(8,128)S(1)}, f32[64,1024]{1,0:T(8,128)S(1)}, u32[]{:S(2)}, u32[]{:S(2)}) collective-permute-start(f32[64,1024]{1,0:T(8,128)S(1)} %get-tuple-element.30.own_ref), channel_id=1, source_target_pairs={{2,0},{7,1},{4,2},{1,3},{6,4},{3,5},{0,6},{5,7},{10,8},{15,9},{12,... | collective-permute-start | bytes 786440 | tf_op jit(solution)/shard_map/ppermute | solution.py:346
  97.6 3.5 %collective-permute-start.15 = (f32[64,64]{1,0:T(8,128)S(1)}, f32[64,64]{1,0:T(8,128)S(1)}, u32[]{:S(2)}, u32[]{:S(2)}) collective-permute-start(f32[64,64]{1,0:T(8,128)S(1)} %add_add_fusion.5), channel_id=1, source_target_pairs={{0,8},{1,9},{2,10},{3,11},{4,12},{5,13},{6,14},{7,15},{8,0},{9,1},... | collective-permute-start | bytes 49160 | tf_op jit(solution)/shard_map/ppermute | solution.py:311
  97.7 4.0 %collective-permute-start.16 = (f32[64,64]{1,0:T(8,128)S(1)}, f32[64,64]{1,0:T(8,128)S(1)}, u32[]{:S(2)}, u32[]{:S(2)}) collective-permute-start(f32[64,64]{1,0:T(8,128)S(1)} %add_add_fusion.5), channel_id=1, source_target_pairs={{0,16},{1,17},{2,18},{3,19},{4,20},{5,21},{6,22},{7,23},{8,24},{9,... | collective-permute-start | bytes 49160 | tf_op jit(solution)/shard_map/ppermute | solution.py:311
  99.3 3.4 %collective-permute-start.17 = (f32[64,64]{1,0:T(8,128)S(1)}, f32[64,64]{1,0:T(8,128)S(1)}, u32[]{:S(2)}, u32[]{:S(2)}) collective-permute-start(f32[64,64]{1,0:T(8,128)S(1)} %add_add_fusion.5), channel_id=1, source_target_pairs={{0,24},{1,25},{2,26},{3,27},{4,28},{5,29},{6,30},{7,31},{8,16},{9,... | collective-permute-start | bytes 49160 | tf_op jit(solution)/shard_map/ppermute | solution.py:311
  101.1 10.4 %collective-permute-start.21 = (f32[64,1024]{1,0:T(8,128)S(1)}, f32[64,1024]{1,0:T(8,128)S(1)}, u32[]{:S(2)}, u32[]{:S(2)}) collective-permute-start(f32[64,1024]{1,0:T(8,128)S(1)} %shard_map.43), channel_id=1, source_target_pairs={{0,2},{1,7},{2,4},{3,1},{4,6},{5,3},{6,0},{7,5},{8,10},{9,15},{10,... | collective-permute-start | bytes 786440 | tf_op jit(solution)/shard_map/ppermute | solution.py:349
  102.6 4.3 %collective-permute-start.18 = (f32[64,64]{1,0:T(8,128)S(1)}, f32[64,64]{1,0:T(8,128)S(1)}, u32[]{:S(2)}, u32[]{:S(2)}) collective-permute-start(f32[64,64]{1,0:T(8,128)S(1)} %add_add_fusion.4), channel_id=1, source_target_pairs={{0,1},{1,0},{2,3},{3,2},{4,5},{5,4},{6,7},{7,6},{8,9},{9,8},{10,11... | collective-permute-start | bytes 49160 | tf_op jit(solution)/shard_map/ppermute | solution.py:311
  114.4 12.3 %collective-permute-start.29 = (f32[64,1024]{1,0:T(8,128)S(1)}, f32[64,1024]{1,0:T(8,128)S(1)}, u32[]{:S(2)}, u32[]{:S(2)}) collective-permute-start(f32[64,1024]{1,0:T(8,128)S(1)} %get-tuple-element.32.own_ref), channel_id=1, source_target_pairs={{0,1},{1,0},{2,3},{3,2},{4,5},{5,4},{6,7},{7,6},{8,9},{9,8},{10,11... | collective-permute-start | bytes 786440 | tf_op jit(solution)/shard_map/ppermute | solution.py:343
  114.4 8.2 %collective-permute-start.22 = (f32[64,64]{1,0:T(8,128)S(1)}, f32[64,64]{1,0:T(8,128)S(1)}, u32[]{:S(2)}, u32[]{:S(2)}) collective-permute-start(f32[64,64]{1,0:T(8,128)S(1)} %get-tuple-element.31), channel_id=1, source_target_pairs={{0,2},{1,3},{2,0},{3,1},{4,6},{5,7},{6,4},{7,5},{8,10},{9,11},{10,... | collective-permute-start | bytes 49160 | tf_op jit(solution)/shard_map/ppermute | solution.py:311
  114.4 8.2 %collective-permute-start.23 = (f32[64,64]{1,0:T(8,128)S(1)}, f32[64,64]{1,0:T(8,128)S(1)}, u32[]{:S(2)}, u32[]{:S(2)}) collective-permute-start(f32[64,64]{1,0:T(8,128)S(1)} %get-tuple-element.31), channel_id=1, source_target_pairs={{0,4},{1,5},{2,6},{3,7},{4,0},{5,1},{6,2},{7,3},{8,12},{9,13},{10,... | collective-permute-start | bytes 49160 | tf_op jit(solution)/shard_map/ppermute | solution.py:311
  118.7 6.1 %collective-permute-start.24 = (f32[64,64]{1,0:T(8,128)S(1)}, f32[64,64]{1,0:T(8,128)S(1)}, u32[]{:S(2)}, u32[]{:S(2)}) collective-permute-start(f32[64,64]{1,0:T(8,128)S(1)} %get-tuple-element.31), channel_id=1, source_target_pairs={{0,6},{1,7},{2,4},{3,5},{4,2},{5,3},{6,0},{7,1},{8,14},{9,15},{10,... | collective-permute-start | bytes 49160 | tf_op jit(solution)/shard_map/ppermute | solution.py:311
  118.8 15.0 %collective-permute-start.30 = (f32[64,1024]{1,0:T(8,128)S(1)}, f32[64,1024]{1,0:T(8,128)S(1)}, u32[]{:S(2)}, u32[]{:S(2)}) collective-permute-start(f32[64,1024]{1,0:T(8,128)S(1)} %get-tuple-element.32.own_ref), channel_id=1, source_target_pairs={{2,0},{7,1},{4,2},{1,3},{6,4},{3,5},{0,6},{5,7},{10,8},{15,9},{12,... | collective-permute-start | bytes 786440 | tf_op jit(solution)/shard_map/ppermute | solution.py:346
  124.8 3.5 %collective-permute-start.25 = (f32[64,64]{1,0:T(8,128)S(1)}, f32[64,64]{1,0:T(8,128)S(1)}, u32[]{:S(2)}, u32[]{:S(2)}) collective-permute-start(f32[64,64]{1,0:T(8,128)S(1)} %add_add_fusion.3), channel_id=1, source_target_pairs={{0,8},{1,9},{2,10},{3,11},{4,12},{5,13},{6,14},{7,15},{8,0},{9,1},... | collective-permute-start | bytes 49160 | tf_op jit(solution)/shard_map/ppermute | solution.py:311
  124.8 4.0 %collective-permute-start.26 = (f32[64,64]{1,0:T(8,128)S(1)}, f32[64,64]{1,0:T(8,128)S(1)}, u32[]{:S(2)}, u32[]{:S(2)}) collective-permute-start(f32[64,64]{1,0:T(8,128)S(1)} %add_add_fusion.3), channel_id=1, source_target_pairs={{0,16},{1,17},{2,18},{3,19},{4,20},{5,21},{6,22},{7,23},{8,24},{9,... | collective-permute-start | bytes 49160 | tf_op jit(solution)/shard_map/ppermute | solution.py:311
  126.4 3.4 %collective-permute-start.27 = (f32[64,64]{1,0:T(8,128)S(1)}, f32[64,64]{1,0:T(8,128)S(1)}, u32[]{:S(2)}, u32[]{:S(2)}) collective-permute-start(f32[64,64]{1,0:T(8,128)S(1)} %add_add_fusion.3), channel_id=1, source_target_pairs={{0,24},{1,25},{2,26},{3,27},{4,28},{5,29},{6,30},{7,31},{8,16},{9,... | collective-permute-start | bytes 49160 | tf_op jit(solution)/shard_map/ppermute | solution.py:311
  128.2 10.4 %collective-permute-start.31 = (f32[64,1024]{1,0:T(8,128)S(1)}, f32[64,1024]{1,0:T(8,128)S(1)}, u32[]{:S(2)}, u32[]{:S(2)}) collective-permute-start(f32[64,1024]{1,0:T(8,128)S(1)} %shard_map.46), channel_id=1, source_target_pairs={{0,2},{1,7},{2,4},{3,1},{4,6},{5,3},{6,0},{7,5},{8,10},{9,15},{10,... | collective-permute-start | bytes 786440 | tf_op jit(solution)/shard_map/ppermute | solution.py:349
  129.8 4.0 %collective-permute-start.28 = (f32[64,64]{1,0:T(8,128)S(1)}, f32[64,64]{1,0:T(8,128)S(1)}, u32[]{:S(2)}, u32[]{:S(2)}) collective-permute-start(f32[64,64]{1,0:T(8,128)S(1)} %add_add_fusion.2), channel_id=1, source_target_pairs={{0,1},{1,0},{2,3},{3,2},{4,5},{5,4},{6,7},{7,6},{8,9},{9,8},{10,11... | collective-permute-start | bytes 49160 | tf_op jit(solution)/shard_map/ppermute | solution.py:311
  141.5 1.2 collective-permute-start.32
  142.7 3.9 %collective-permute-start.33 = (f32[64,64]{1,0:T(8,128)S(1)}, f32[64,64]{1,0:T(8,128)S(1)}, u32[]{:S(2)}, u32[]{:S(2)}) collective-permute-start(f32[64,64]{1,0:T(8,128)S(1)} %add.138), channel_id=1, source_target_pairs={{0,16},{1,17},{2,18},{3,19},{4,20},{5,21},{6,22},{7,23},{8,24},{9,... | collective-permute-start | bytes 49160 | tf_op jit(solution)/shard_map/ppermute | solution.py:311
  144.2 3.9 %collective-permute-start.34 = (f32[64,64]{1,0:T(8,128)S(1)}, f32[64,64]{1,0:T(8,128)S(1)}, u32[]{:S(2)}, u32[]{:S(2)}) collective-permute-start(f32[64,64]{1,0:T(8,128)S(1)} %add.138), channel_id=1, source_target_pairs={{0,1},{1,0},{2,3},{3,2},{4,5},{5,4},{6,7},{7,6},{8,9},{9,8},{10,11... | collective-permute-start | bytes 49160 | tf_op jit(solution)/shard_map/ppermute | solution.py:311
  144.2 4.8 %collective-permute-start.35 = (f32[64,64]{1,0:T(8,128)S(1)}, f32[64,64]{1,0:T(8,128)S(1)}, u32[]{:S(2)}, u32[]{:S(2)}) collective-permute-start(f32[64,64]{1,0:T(8,128)S(1)} %add.138), channel_id=1, source_target_pairs={{0,17},{1,16},{2,19},{3,18},{4,21},{5,20},{6,23},{7,22},{8,25},{9,... | collective-permute-start | bytes 49160 | tf_op jit(solution)/shard_map/ppermute | solution.py:311
  149.0 4.5 %collective-permute-start.36 = (f32[64,64]{1,0:T(8,128)S(1)}, f32[64,64]{1,0:T(8,128)S(1)}, u32[]{:S(2)}, u32[]{:S(2)}) collective-permute-start(f32[64,64]{1,0:T(8,128)S(1)} %add_add_fusion.1), channel_id=1, source_target_pairs={{0,2},{1,3},{2,0},{3,1},{4,6},{5,7},{6,4},{7,5},{8,10},{9,11},{10,... | collective-permute-start | bytes 49160 | tf_op jit(solution)/shard_map/ppermute | solution.py:311
  149.1 4.9 %collective-permute-start.37 = (f32[64,64]{1,0:T(8,128)S(1)}, f32[64,64]{1,0:T(8,128)S(1)}, u32[]{:S(2)}, u32[]{:S(2)}) collective-permute-start(f32[64,64]{1,0:T(8,128)S(1)} %add_add_fusion.1), channel_id=1, source_target_pairs={{0,4},{1,5},{2,6},{3,7},{4,0},{5,1},{6,2},{7,3},{8,12},{9,13},{10,... | collective-permute-start | bytes 49160 | tf_op jit(solution)/shard_map/ppermute | solution.py:311
  151.8 5.7 %collective-permute-start.38 = (f32[64,64]{1,0:T(8,128)S(1)}, f32[64,64]{1,0:T(8,128)S(1)}, u32[]{:S(2)}, u32[]{:S(2)}) collective-permute-start(f32[64,64]{1,0:T(8,128)S(1)} %add_add_fusion.1), channel_id=1, source_target_pairs={{0,6},{1,7},{2,4},{3,5},{4,2},{5,3},{6,0},{7,1},{8,14},{9,15},{10,... | collective-permute-start | bytes 49160 | tf_op jit(solution)/shard_map/ppermute | solution.py:311
